TPU v7x, 32 devices: a whole 2x2x4 slice. The times are simulated.
32 devices in a mesh: dp: 8 (over y, x, core), mp: 4 (over z).
Axes of the slice: x: 2, y: 2, z: 4, core: 2. Of those that a mesh axis runs over, the one named last changes fastest.
Arguments:
- inputs: bfloat16 [16, 512, 1024], P('dp'), may hold values from -6 to 6
- memory: bfloat16 [16, 512, 1024], P('dp'), may hold values from -6 to 6
- compressed_memory: bfloat16 [16, 512, 1024], P('dp'), may hold values from -6 to 6
- memory_fill: int32 [16], P('dp'), may hold values from 0 to 512, as said below
- compressed_fill: int32 [16], P('dp'), may hold values from 0 to 512, as said below
- first_gain: float32 [1024], replicated, may hold values from 0.5 to 1.5
- query_weight: bfloat16 [1024, 1024], P(None, 'mp'), may hold values from -0.1875 to 0.1875
- key_weight: bfloat16 [1024, 1024], P(None, 'mp'), may hold values from -0.1875 to 0.1875
- value_weight: bfloat16 [1024, 1024], P(None, 'mp'), may hold values from -0.1875 to 0.1875
- relative_bias: float32 [8, 22], P('mp'), may hold values from -1.5 to 1.5
- output_weight: bfloat16 [1024, 1024], P('mp'), may hold values from -1.5 to 1.5
- second_gain: float32 [1024], replicated, may hold values from 0.5 to 1.5
- up_weight: bfloat16 [1024, 4096], P(None, 'mp'), may hold values from -0.1875 to 0.1875
- down_weight: bfloat16 [4096, 1024], P('mp'), may hold values from -0.09375 to 0.09375
- compress_weight: bfloat16 [2048, 1024], P(None, 'mp'), may hold values from -0.125 to 0.125
- grad_output: bfloat16 [16, 512, 1024], P('dp'), may hold values from -6 to 6
- grad_compressed: bfloat16 [16, 256, 1024], P('dp', None, 'mp'), may hold values from -6 to 6
Outputs:
- outputs: bfloat16 [16, 512, 1024], P('dp')
- compressed: bfloat16 [16, 256, 1024], P('dp', None, 'mp')
- grad_inputs: bfloat16 [16, 512, 1024], P('dp')
- grad_first_gain: float32 [1024], replicated
- grad_query: float32 [1024, 1024], P(None, 'mp')
- grad_key: float32 [1024, 1024], P(None, 'mp')
- grad_value: float32 [1024, 1024], P(None, 'mp')
- grad_relative: float32 [8, 22], P('mp')
- grad_output_weight: float32 [1024, 1024], P('mp')
- grad_second_gain: float32 [1024], replicated
- grad_up: float32 [1024, 4096], P(None, 'mp')
- grad_down: float32 [4096, 1024], P('mp')
- grad_compress: float32 [2048, 1024], P(None, 'mp')
Inputs may be any that keep to these rules, and one draw needn't show every extreme that they name: `memory_fill`: some stream has a full memory and some stream an empty one. `compressed_fill`: some stream has a full compressed memory and some stream an empty one.
All inputs are finite; a program needn't handle non-finite values.
Results may differ from a plain program's by a relative error of at most 0.023.
Values sent between devices are 32-bit elements; how exact they have to be, the bound alone decides.
A program may use at most 320 MiB of HBM per device.

v0:
```python
import math

import jax
import jax.numpy as jnp
from jax import lax
from jax.sharding import PartitionSpec as P

reach_marks = (
    1,
    2,
    3,
    4,
    5,
    6,
    7,
    8,
    12,
    16,
    24,
    32,
    48,
    64,
    96,
    128,
    192,
    256,
    384,
    512,
    768,
    1024,
)
epsilon = 1e-06


def rms_scale(source, gain):
    return source * lax.rsqrt(jnp.mean(source * source, axis=-1, keepdims=True) + epsilon) * gain


def low_product(left, right):
    return jnp.dot(left, right, preferred_element_type=jnp.float32)


def weight_grad(left, right):
    return lax.dot_general(
        left, right, (((0,), (0,)), ((), ())), preferred_element_type=jnp.float32
    )


def back_product(left, right):
    return lax.dot_general(
        left, right, (((1,), (1,)), ((), ())), preferred_element_type=jnp.float32
    )


def gelu_tanh(source):
    return jax.nn.gelu(source, approximate=True)


def body(
    inputs,
    memory,
    compressed_memory,
    memory_fill,
    compressed_fill,
    first_gain,
    query_weight,
    key_weight,
    value_weight,
    relative_bias,
    output_weight,
    second_gain,
    up_weight,
    down_weight,
    compress_weight,
    grad_output,
    grad_compressed,
):
    seg_len = inputs.shape[1]
    mem_len = memory.shape[1]
    packed_len = compressed_memory.shape[1]
    model_width = inputs.shape[2]
    kept_count = packed_len + mem_len
    key_count = kept_count + seg_len
    heads_here = relative_bias.shape[0]
    head_dim = query_weight.shape[1] // heads_here
    compress_count = grad_compressed.shape[1]
    score_scale = 1.0 / math.sqrt(head_dim)
    distance = (
        jnp.arange(seg_len, dtype=jnp.int32)[:, None]
        + kept_count
        - jnp.arange(key_count, dtype=jnp.int32)[None, :]
    )
    causal = distance >= 0
    bias_table = jnp.zeros((heads_here, seg_len, key_count), jnp.float32)
    for position, mark_value in enumerate(reach_marks):
        bias_table = (
            bias_table
            + relative_bias[:, position][:, None, None]
            * (distance >= mark_value).astype(jnp.float32)[None]
        )

    def split_heads(source):
        return source.reshape(source.shape[0], heads_here, head_dim)

    def score_grid(queries, key_rows, allowed):
        raw_scores = (
            jnp.einsum(
                "shd,khd->hsk",
                split_heads(queries),
                split_heads(key_rows),
                preferred_element_type=jnp.float32,
            )
            * score_scale
            + bias_table
        )
        return jnp.where(allowed[None], raw_scores, -1e30)

    def attend(seg_rows, memory_rows, packed_rows, memory_count, packed_count):
        stacked = jnp.concatenate([packed_rows, memory_rows, seg_rows], axis=0).astype(jnp.float32)
        unit_rows = rms_scale(stacked, first_gain).astype(jnp.bfloat16)
        queries = low_product(unit_rows[kept_count:], query_weight).astype(jnp.bfloat16)
        key_rows = low_product(unit_rows, key_weight).astype(jnp.bfloat16)
        value_rows = low_product(unit_rows, value_weight).astype(jnp.bfloat16)
        valid_keys = jnp.concatenate(
            [
                jnp.arange(packed_len, dtype=jnp.int32) >= packed_len - packed_count,
                jnp.arange(mem_len, dtype=jnp.int32) >= mem_len - memory_count,
                jnp.ones((seg_len,), jnp.bool_),
            ]
        )
        allowed = causal & valid_keys[None, :]
        masked = score_grid(queries, key_rows, allowed)
        top_score = jnp.max(masked, axis=-1, keepdims=True)
        log_total = top_score + jnp.log(
            jnp.sum(jnp.exp(masked - top_score), axis=-1, keepdims=True)
        )
        prob_low = jnp.exp(masked - log_total).astype(jnp.bfloat16)
        mixed_heads = jnp.einsum(
            "hsk,khd->shd", prob_low, split_heads(value_rows), preferred_element_type=jnp.float32
        )
        mixed_heads = mixed_heads.reshape(seg_len, heads_here * head_dim).astype(jnp.bfloat16)
        attended = lax.psum(low_product(mixed_heads, output_weight), "mp")
        residual = seg_rows.astype(jnp.float32) + attended
        return (
            stacked,
            unit_rows,
            queries,
            key_rows,
            value_rows,
            allowed,
            log_total,
            mixed_heads,
            residual,
        )

    def feed(residual):
        ffn_input = rms_scale(residual, second_gain).astype(jnp.bfloat16)
        pre_act = low_product(ffn_input, up_weight)
        activated = gelu_tanh(pre_act).astype(jnp.bfloat16)
        return (ffn_input, pre_act, activated)

    def stream_step(totals, stream_item):
        seg_rows, memory_rows, packed_rows, memory_count, packed_count, grad_rows, grad_packed = (
            stream_item
        )
        saved = attend(seg_rows, memory_rows, packed_rows, memory_count, packed_count)
        ffn_input, pre_act, activated = feed(saved[8])
        branch_out = lax.psum(low_product(activated, down_weight), "mp")
        result = (saved[8] + branch_out).astype(jnp.bfloat16)
        again = lax.optimization_barrier((seg_rows, memory_rows, packed_rows, result))
        saved = attend(again[0], again[1], again[2], memory_count, packed_count)
        ffn_input, pre_act, activated = feed(saved[8])
        (
            stacked,
            unit_rows,
            queries,
            key_rows,
            value_rows,
            allowed,
            log_total,
            mixed_heads,
            residual,
        ) = saved
        slot_index = jnp.arange(mem_len, dtype=jnp.int32)
        live_rows = jnp.where(
            (slot_index >= mem_len - memory_count)[:, None],
            memory_rows,
            jnp.zeros_like(memory_rows),
        )
        evicted = live_rows.reshape(compress_count, 2 * model_width)
        packed_new = low_product(evicted, compress_weight).astype(jnp.bfloat16)
        grad_down = weight_grad(activated, grad_rows)
        _, gelu_back = jax.vjp(gelu_tanh, pre_act)
        grad_pre = gelu_back(back_product(grad_rows, down_weight))[0].astype(jnp.bfloat16)
        grad_up = weight_grad(ffn_input, grad_pre)
        grad_ffn_input = lax.psum(back_product(grad_pre, up_weight), "mp")
        _, second_back = jax.vjp(rms_scale, residual, second_gain)
        grad_res_norm, grad_second = second_back(grad_ffn_input)
        grad_residual = grad_rows.astype(jnp.float32) + grad_res_norm
        grad_attended = grad_residual.astype(jnp.bfloat16)
        grad_out_weight = weight_grad(mixed_heads, grad_attended)
        grad_mixed = back_product(grad_attended, output_weight).astype(jnp.bfloat16)
        masked = score_grid(queries, key_rows, allowed)
        attend_prob = jnp.exp(masked - log_total)
        grad_prob = jnp.einsum(
            "shd,khd->hsk",
            split_heads(grad_mixed),
            split_heads(value_rows),
            preferred_element_type=jnp.float32,
        )
        grad_score = (
            attend_prob * (grad_prob - jnp.sum(grad_prob * attend_prob, axis=-1, keepdims=True))
        ).astype(jnp.bfloat16)
        score_wide = grad_score.astype(jnp.float32)
        grad_relative = jnp.stack(
            [
                jnp.sum(jnp.where((distance >= mark_value)[None], score_wide, 0.0), axis=(1, 2))
                for mark_value in reach_marks
            ],
            axis=1,
        )
        grad_queries = (
            (
                jnp.einsum(
                    "hsk,khd->shd",
                    grad_score,
                    split_heads(key_rows),
                    preferred_element_type=jnp.float32,
                )
                * score_scale
            )
            .reshape(seg_len, heads_here * head_dim)
            .astype(jnp.bfloat16)
        )
        grad_keys = (
            (
                jnp.einsum(
                    "hsk,shd->khd",
                    grad_score,
                    split_heads(queries),
                    preferred_element_type=jnp.float32,
                )
                * score_scale
            )
            .reshape(key_count, heads_here * head_dim)
            .astype(jnp.bfloat16)
        )
        grad_values = (
            jnp.einsum(
                "hsk,shd->khd",
                attend_prob.astype(jnp.bfloat16),
                split_heads(grad_mixed),
                preferred_element_type=jnp.float32,
            )
            .reshape(key_count, heads_here * head_dim)
            .astype(jnp.bfloat16)
        )
        grad_query_w = weight_grad(unit_rows[kept_count:], grad_queries)
        grad_key_w = weight_grad(unit_rows, grad_keys)
        grad_value_w = weight_grad(unit_rows, grad_values)
        grad_unit = back_product(grad_keys, key_weight) + back_product(grad_values, value_weight)
        grad_unit_seg = grad_unit[kept_count:] + back_product(grad_queries, query_weight)
        _, kept_back = jax.vjp(rms_scale, stacked[:kept_count], first_gain)
        grad_first_kept = kept_back(grad_unit[:kept_count])[1]
        grad_unit_seg, grad_first_kept = lax.psum((grad_unit_seg, grad_first_kept), "mp")
        _, seg_back = jax.vjp(rms_scale, stacked[kept_count:], first_gain)
        grad_seg_norm, grad_first_seg = seg_back(grad_unit_seg)
        grad_seg = (grad_residual + grad_seg_norm).astype(jnp.bfloat16)
        grad_compress_w = weight_grad(evicted, grad_packed)
        gradients = (
            grad_first_kept + grad_first_seg,
            grad_query_w,
            grad_key_w,
            grad_value_w,
            grad_relative,
            grad_out_weight,
            grad_second,
            grad_up,
            grad_down,
            grad_compress_w,
        )
        totals = tuple((total + grad_item for total, grad_item in zip(totals, gradients)))
        return (totals, (result, packed_new, grad_seg))

    initial = tuple(
        (
            jnp.zeros(item.shape, jnp.float32)
            for item in (
                first_gain,
                query_weight,
                key_weight,
                value_weight,
                relative_bias,
                output_weight,
                second_gain,
                up_weight,
                down_weight,
                compress_weight,
            )
        )
    )
    stream_items = (
        inputs,
        memory,
        compressed_memory,
        memory_fill,
        compressed_fill,
        grad_output,
        grad_compressed,
    )
    totals, (results, packed_all, grad_all) = lax.scan(stream_step, initial, stream_items)
    totals = lax.psum(totals, "dp")
    return (results, packed_all, grad_all) + tuple(totals)


def solution(mesh):
    in_specs = (
        P("dp", None, None),
        P("dp", None, None),
        P("dp", None, None),
        P("dp"),
        P("dp"),
        P(),
        P(None, "mp"),
        P(None, "mp"),
        P(None, "mp"),
        P("mp", None),
        P("mp", None),
        P(),
        P(None, "mp"),
        P("mp", None),
        P(None, "mp"),
        P("dp", None, None),
        P("dp", None, "mp"),
    )
    out_specs = (
        P("dp", None, None),
        P("dp", None, "mp"),
        P("dp", None, None),
        P(),
        P(None, "mp"),
        P(None, "mp"),
        P(None, "mp"),
        P("mp", None),
        P("mp", None),
        P(),
        P(None, "mp"),
        P("mp", None),
        P(None, "mp"),
    )
    return jax.shard_map(body, mesh=mesh, in_specs=in_specs, out_specs=out_specs, check_vma=False)
```

profile of v0, /device:TPU:0, one launch (start us, length us, event | category | flops | bytes accessed | tf_op | source)
XLA Modules:
  0.0 1445.7 jit_solution(14084164727525014909)
XLA Ops:
  11.6 22.1 %fusion.144 = (f32[512,1536]{1,0:T(8,128)}, f32[512,1536]{1,0:T(8,128)}, f32[512,1536]{1,0:T(8,128)}, f32[512,1536]{1,0:T(8,128)}, f32[512,1536]{1,0:T(8,128)}, ...) fusion(s32[512]{0:T(512)S(1)} %iota_add_fusion), kind=kLoop, calls=%fused_computation.240 | loop fusion | flops 35389440 | bytes 69208064 | tf_op jit(solution)/shard_map/convert_element_type | solution.py:99
  33.8 1186.6 %while.40 = (s32[]{:T(128)}, f32[1024]{0:T(1024)S(1)}, f32[1024,256]{1,0:T(8,128)}, f32[1024,256]{1,0:T(8,128)}, f32[1024,256]{1,0:T(8,128)}, /*index=5*/f32[2,2...) while((s32[]{:T(128)}, f32[1024]{0:T(1024)S(1)}, ...), condition=%wide.region_45.46_spmd.clone.clone.clone.clone, body=%wide.region_0.45_spmd.clone.clone.clone.clone.sunk | while | flops 20195917824 | bytes 935102208 | solution.py:311
  41.1 6.1 fusion.369
  50.8 12.6 fusion.370
  63.4 25.3 %multiply_add_fusion.4 = f32[2,512,1536]{2,1,0:T(8,128)} fusion(f32[512,1536]{1,0:T(8,128)} %get-tuple-element.2286, f32[2]{0:T(128)S(1)} %get-tuple-element.2287, f32[512,1536]{1,0:T(8,128)} %get-tuple-element.2284, f32[2]{0:T(128)S(1)} %get-tuple-element.2285, f32[512,1536]{1,0:T(8,128)} %get-tuple-element.2282, f32[2]{0:T(128)S(1)} %get-tuple-element.2283, ...), kind=kLoop, calls=%fused_computation.52.clone.1 | loop fusion | flops 67633152 | bytes 75497648 | tf_op jit(solution)/shard_map/add | solution.py:97
  88.8 5.0 fusion.371
  98.1 89.3 %all-reduce.11.cloned.1.call-done = f32[512,1024]{1,0:T(8,128)} async-done(((f32[512,1024]{1,0:T(8,128)}), f32[512,1024]{1,0:T(8,128)}) %all-reduce.11.cloned.1.call-update) | async-done | bytes 2097168 | tf_op jit(solution)/shard_map/while/body/eval_jaxpr/psum | solution.py:142
  189.3 6.6 fusion.374
  196.0 85.6 %all-reduce.13.cloned.1.call-done = f32[512,1024]{1,0:T(8,128)} async-done(((f32[512,1024]{1,0:T(8,128)}), f32[512,1024]{1,0:T(8,128)}) %all-reduce.13.cloned.1.call-update) | async-done | bytes 2097168 | tf_op jit(solution)/shard_map/while/body/eval_jaxpr/psum | solution.py:168
  281.6 3.8 bitcast_dynamic-update-slice_fusion.2
  286.8 6.1 multiply_convert_fusion.23
  308.7 2.4 squeeze.76
  316.9 2.3 copy.139
  320.7 2.4 fusion.389
  324.9 67.0 %all-reduce.15.cloned.1.call-done = f32[512,1024]{1,0:T(8,128)} async-done(((f32[512,1024]{1,0:T(8,128)}), f32[512,1024]{1,0:T(8,128)}) %all-reduce.15.cloned.1.call-update) | async-done | bytes 2097168 | tf_op jit(solution)/shard_map/while/body/eval_jaxpr/psum | solution.py:142
  397.8 2.4 fusion.379
  401.1 2.7 fusion.380
  405.3 2.6 copy-done.1
  408.8 3.4 select_add_fusion.13
  412.3 3.6 select_add_fusion.14
  415.8 73.6 %all-reduce.17.cloned.1.call-done = f32[512,1024]{1,0:T(8,128)} async-done(((f32[512,1024]{1,0:T(8,128)}), f32[512,1024]{1,0:T(8,128)}) %all-reduce.17.cloned.1.call-update) | async-done | bytes 2097168 | tf_op jit(solution)/shard_map/while/body/eval_jaxpr/psum | solution.py:196
  491.7 2.5 fusion.381
  501.3 25.2 %fusion.382 = (f32[2]{0:T(128)}, f32[2]{0:T(128)S(1)}, f32[2]{0:T(128)S(1)}, f32[2]{0:T(128)}, f32[2]{0:T(128)}, /*index=5*/f32[2]{0:T(128)}, f32[2]{0:T(128)}, ...) fusion(pred[512,1536]{1,0:T(8,128)(4,1)S(1)} %copy-done.19, ...), kind=kLoop, calls=%fused_computation.51.clone.1 | loop fusion | flops 64487408 | bytes 29892752 | tf_op jit(solution)/shard_map/while/body/eval_jaxpr/reduce_sum | solution.py:217
  530.8 2.6 copy-done.6
  535.3 6.7 fusion.388
  542.2 2.9 fusion.385
  547.3 10.8 psum.174
  558.1 2.9 convolution_add_fusion.13
  565.9 55.6 %all-reduce.19.cloned.1.call-done = f32[512,1024]{1,0:T(8,128)} async-done(((f32[512,1024]{1,0:T(8,128)}), f32[512,1024]{1,0:T(8,128)}) %all-reduce.19.cloned.1.call-update) | async-done | bytes 2097168 | tf_op jit(solution)/shard_map/while/body/eval_jaxpr/psum | solution.py:265
  621.5 2.9 multiply_reduce_fusion.25
  635.8 6.1 fusion.369
  645.4 12.6 fusion.370
  658.1 25.2 %multiply_add_fusion.4 = f32[2,512,1536]{2,1,0:T(8,128)} fusion(f32[512,1536]{1,0:T(8,128)} %get-tuple-element.2286, f32[2]{0:T(128)S(1)} %get-tuple-element.2287, f32[512,1536]{1,0:T(8,128)} %get-tuple-element.2284, f32[2]{0:T(128)S(1)} %get-tuple-element.2285, f32[512,1536]{1,0:T(8,128)} %get-tuple-element.2282, f32[2]{0:T(128)S(1)} %get-tuple-element.2283, ...), kind=kLoop, calls=%fused_computation.52.clone.1 | loop fusion | flops 67633152 | bytes 75497648 | tf_op jit(solution)/shard_map/add | solution.py:97
  683.3 5.0 fusion.371
  692.6 85.6 %all-reduce.11.cloned.1.call-done = f32[512,1024]{1,0:T(8,128)} async-done(((f32[512,1024]{1,0:T(8,128)}), f32[512,1024]{1,0:T(8,128)}) %all-reduce.11.cloned.1.call-update) | async-done | bytes 2097168 | tf_op jit(solution)/shard_map/while/body/eval_jaxpr/psum | solution.py:142
  780.1 6.6 fusion.374
  786.8 85.6 %all-reduce.13.cloned.1.call-done = f32[512,1024]{1,0:T(8,128)} async-done(((f32[512,1024]{1,0:T(8,128)}), f32[512,1024]{1,0:T(8,128)}) %all-reduce.13.cloned.1.call-update) | async-done | bytes 2097168 | tf_op jit(solution)/shard_map/while/body/eval_jaxpr/psum | solution.py:168
  872.4 3.8 bitcast_dynamic-update-slice_fusion.2
  877.4 6.1 multiply_convert_fusion.23
  899.3 2.4 squeeze.76
  907.5 2.3 copy.139
  911.2 2.4 fusion.389
  913.6 3.5 convolution_add_fusion.17
  917.1 65.4 %all-reduce.15.cloned.1.call-done = f32[512,1024]{1,0:T(8,128)} async-done(((f32[512,1024]{1,0:T(8,128)}), f32[512,1024]{1,0:T(8,128)}) %all-reduce.15.cloned.1.call-update) | async-done | bytes 2097168 | tf_op jit(solution)/shard_map/while/body/eval_jaxpr/psum | solution.py:142
  988.4 2.4 fusion.379
  991.7 2.7 fusion.380
  995.8 2.6 copy-done.1
  999.4 5.8 select_add_fusion.13
  1005.2 5.8 select_add_fusion.14
  1011.0 69.0 %all-reduce.17.cloned.1.call-done = f32[512,1024]{1,0:T(8,128)} async-done(((f32[512,1024]{1,0:T(8,128)}), f32[512,1024]{1,0:T(8,128)}) %all-reduce.17.cloned.1.call-update) | async-done | bytes 2097168 | tf_op jit(solution)/shard_map/while/body/eval_jaxpr/psum | solution.py:196
  1082.3 2.5 fusion.381
  1091.9 25.2 %fusion.382 = (f32[2]{0:T(128)}, f32[2]{0:T(128)S(1)}, f32[2]{0:T(128)S(1)}, f32[2]{0:T(128)}, f32[2]{0:T(128)}, /*index=5*/f32[2]{0:T(128)}, f32[2]{0:T(128)}, ...) fusion(pred[512,1536]{1,0:T(8,128)(4,1)S(1)} %copy-done.19, ...), kind=kLoop, calls=%fused_computation.51.clone.1 | loop fusion | flops 64487408 | bytes 29892752 | tf_op jit(solution)/shard_map/while/body/eval_jaxpr/reduce_sum | solution.py:217
  1121.4 2.6 copy-done.6
  1125.9 6.7 fusion.388
  1132.8 2.9 fusion.385
  1137.9 10.8 psum.174
  1148.7 3.2 convolution_add_fusion.13
  1153.4 3.4 convolution_add_fusion.15
  1158.2 53.9 %all-reduce.19.cloned.1.call-done = f32[512,1024]{1,0:T(8,128)} async-done(((f32[512,1024]{1,0:T(8,128)}), f32[512,1024]{1,0:T(8,128)}) %all-reduce.19.cloned.1.call-update) | async-done | bytes 2097168 | tf_op jit(solution)/shard_map/while/body/eval_jaxpr/psum | solution.py:265
  1212.2 2.9 multiply_reduce_fusion.25
  1221.0 14.8 %all-reduce = (f32[1024]{0:T(1024)}, f32[2,22]{1,0:T(2,128)}, f32[1024]{0:T(1024)}) all-reduce(f32[1024]{0:T(1024)S(1)} %get-tuple-element.2353, f32[2,22]{1,0:T(2,128)S(1)} %get-tuple-element.2357, f32[1024]{0:T(1024)S(1)} %get-tuple-element.2359), channel_id=1, replica_groups=mesh['dp'=8,'mp'=4] {'dp'}, use_global_device_ids=true, to_apply=%region_46.47 | all-reduce | flops 2092 | bytes 16736 | tf_op jit(solution)/shard_map/psum | solution.py:312
  1235.8 187.3 %all-reduce.9.cloned.1.call-done = (f32[1024,256]{1,0:T(8,128)}, f32[1024,256]{1,0:T(8,128)}, f32[1024,256]{1,0:T(8,128)}, f32[256,1024]{1,0:T(8,128)}, f32[1024...) async-done(((f32[1024,256]{1,0:T(8,128)}, f32[1024,256]{1,0:T(8,128)}, f32[1024,256]{1,0:T(8,128)}, f32[256,1024]{1,0:T(8,128)}, f32[1024,1024]{1,0:T(8,128)}, ...) | async-done | bytes 14680080 | tf_op jit(solution)/shard_map/psum | solution.py:312
  1423.1 2.4 copy.198
  1425.5 2.4 copy.199
  (603 shorter events, 164.0 us)
Async XLA Ops:
  11.6 22.2 %copy-start.66 = (f32[1024]{0:T(1024)S(1)}, f32[1024]{0:T(1024)}, u32[]{:S(2)}) copy-start(f32[1024]{0:T(1024)} %param.24) | copy-start | bytes 12292
  11.6 22.2 %copy-start.71 = (f32[1024]{0:T(1024)S(1)}, f32[1024]{0:T(1024)}, u32[]{:S(2)}) copy-start(f32[1024]{0:T(1024)} %param.30) | copy-start | bytes 12292
  11.6 22.2 %copy-start.94 = (s32[2]{0:T(128)S(1)}, s32[2]{0:T(128)}, u32[]{:S(2)}) copy-start(s32[2]{0:T(128)} %param.23) | copy-start | bytes 28
  34.0 153.4 %all-reduce.11.cloned.1.call-start = ((), (), s32[]{:S(2)}) async-start(), calls=%async_computation.1 | async-start | bytes 4194304 | tf_op jit(solution)/shard_map/while/body/eval_jaxpr/psum | solution.py:142
  41.1 6.2 copy-start.51
  41.1 6.7 copy-start.54
  63.4 25.4 %copy-start.9 = (pred[512,1536]{1,0:T(8,128)(4,1)}, pred[512,1536]{1,0:T(8,128)(4,1)S(1)}, u32[]{:S(2)}) copy-start(pred[512,1536]{1,0:T(8,128)(4,1)S(1)} %get-tuple-element.1992) | copy-start | bytes 2359300 | tf_op jit(solution)/shard_map/while
  98.0 183.6 %all-reduce.13.cloned.1.call-start = ((), (), s32[]{:S(2)}) async-start(), calls=%async_computation.2 | async-start | bytes 4194304 | tf_op jit(solution)/shard_map/while/body/eval_jaxpr/psum | solution.py:168
  196.0 195.9 %all-reduce.15.cloned.1.call-start = ((), (), s32[]{:S(2)}) async-start(), calls=%async_computation.3 | async-start | bytes 4194304 | tf_op jit(solution)/shard_map/while/body/eval_jaxpr/psum | solution.py:142
  286.8 6.2 copy-start.52
  286.8 6.7 copy-start.60
  296.0 4.9 copy-start.41
  306.3 183.1 %all-reduce.17.cloned.1.call-start = ((), (), s32[]{:S(2)}) async-start(), calls=%async_computation.4 | async-start | bytes 4194304 | tf_op jit(solution)/shard_map/while/body/eval_jaxpr/psum | solution.py:196
  316.9 6.1 copy-start.65
  395.5 4.6 copy-start.96
  403.8 217.7 %all-reduce.19.cloned.1.call-start = ((), (), s32[]{:S(2)}) async-start(), calls=%async_computation.5 | async-start | bytes 4194304 | tf_op jit(solution)/shard_map/while/body/eval_jaxpr/psum | solution.py:265
  489.4 5.4 slice-start
  496.2 33.5 %copy-start.37 = (bf16[2,128,1536]{2,1,0:T(8,128)(2,1)}, bf16[2,128,1536]{2,1,0:T(8,128)(2,1)S(1)}, u32[]{:S(2)}) copy-start(bf16[2,128,1536]{2,1,0:T(8,128)(2,1)S(1)} %convolution_convert_fusion.27) | copy-start | bytes 2359300 | tf_op jit(solution)/shard_map/while
  496.3 4.7 copy-start.34
  496.3 4.9 copy-start.35
  501.3 25.2 %copy-start.40 = (bf16[1536,256]{0,1:T(8,128)(2,1)S(1)}, bf16[1536,256]{0,1:T(8,128)(2,1)}, u32[]{:S(2)}) copy-start(bf16[1536,256]{0,1:T(8,128)(2,1)} %copy-done.39) | copy-start | bytes 2359300 | tf_op jit(solution)/shard_map/while
  535.3 6.7 copy-start.7
  542.1 4.6 copy-start.76
  542.1 4.6 copy-start.75
  542.1 4.7 copy-start.74
  542.1 4.8 copy-start.73
  542.2 4.9 copy-start.72
  545.0 15.9 %copy-start.3 = (f32[512,1024]{1,0:T(8,128)S(1)}, f32[512,1024]{1,0:T(8,128)}, u32[]{:S(2)}) copy-start(f32[512,1024]{1,0:T(8,128)} %copy-done.2) | copy-start | bytes 6291460 | tf_op jit(solution)/shard_map/while
  545.1 15.9 %copy-start.44 = (bf16[2,128,512]{2,1,0:T(8,128)(2,1)S(1)}, bf16[2,128,512]{2,1,0:T(8,128)(2,1)}, u32[]{:S(2)}) copy-start(bf16[2,128,512]{2,1,0:T(8,128)(2,1)} %copy-done.43) | copy-start | bytes 786436 | tf_op jit(solution)/shard_map/while
  565.9 61.2 %copy-start.68 = (f32[1024,256]{1,0:T(8,128)}, f32[1024,256]{1,0:T(8,128)S(1)}, u32[]{:S(2)}) copy-start(f32[1024,256]{1,0:T(8,128)S(1)} %convolution_add_fusion.14) | copy-start | bytes 3145732 | tf_op jit(solution)/shard_map/while
  628.6 149.5 %all-reduce.11.cloned.1.call-start = ((), (), s32[]{:S(2)}) async-start(), calls=%async_computation.1 | async-start | bytes 4194304 | tf_op jit(solution)/shard_map/while/body/eval_jaxpr/psum | solution.py:142
  635.7 6.2 copy-start.51
  635.7 6.7 copy-start.54
  658.1 25.2 %copy-start.9 = (pred[512,1536]{1,0:T(8,128)(4,1)}, pred[512,1536]{1,0:T(8,128)(4,1)S(1)}, u32[]{:S(2)}) copy-start(pred[512,1536]{1,0:T(8,128)(4,1)S(1)} %get-tuple-element.1992) | copy-start | bytes 2359300 | tf_op jit(solution)/shard_map/while
  692.5 179.8 %all-reduce.13.cloned.1.call-start = ((), (), s32[]{:S(2)}) async-start(), calls=%async_computation.2 | async-start | bytes 4194304 | tf_op jit(solution)/shard_map/while/body/eval_jaxpr/psum | solution.py:168
  786.8 195.8 %all-reduce.15.cloned.1.call-start = ((), (), s32[]{:S(2)}) async-start(), calls=%async_computation.3 | async-start | bytes 4194304 | tf_op jit(solution)/shard_map/while/body/eval_jaxpr/psum | solution.py:142
  877.4 6.2 copy-start.52
  877.4 6.7 copy-start.60
  886.6 4.9 copy-start.41
  896.9 183.1 %all-reduce.17.cloned.1.call-start = ((), (), s32[]{:S(2)}) async-start(), calls=%async_computation.4 | async-start | bytes 4194304 | tf_op jit(solution)/shard_map/while/body/eval_jaxpr/psum | solution.py:196
  907.5 6.1 copy-start.65
  986.1 4.6 copy-start.96
  994.4 217.8 %all-reduce.19.cloned.1.call-start = ((), (), s32[]{:S(2)}) async-start(), calls=%async_computation.5 | async-start | bytes 4194304 | tf_op jit(solution)/shard_map/while/body/eval_jaxpr/psum | solution.py:265
  999.4 5.8 copy-start.58
  999.4 5.8 copy-start.97
  1080.0 5.4 slice-start
  1086.8 33.5 %copy-start.37 = (bf16[2,128,1536]{2,1,0:T(8,128)(2,1)}, bf16[2,128,1536]{2,1,0:T(8,128)(2,1)S(1)}, u32[]{:S(2)}) copy-start(bf16[2,128,1536]{2,1,0:T(8,128)(2,1)S(1)} %convolution_convert_fusion.27) | copy-start | bytes 2359300 | tf_op jit(solution)/shard_map/while
  1086.9 4.7 copy-start.34
  1086.9 4.9 copy-start.35
  1091.9 25.2 %copy-start.40 = (bf16[1536,256]{0,1:T(8,128)(2,1)S(1)}, bf16[1536,256]{0,1:T(8,128)(2,1)}, u32[]{:S(2)}) copy-start(bf16[1536,256]{0,1:T(8,128)(2,1)} %copy-done.39) | copy-start | bytes 2359300 | tf_op jit(solution)/shard_map/while
  1125.9 6.7 copy-start.7
  1132.7 4.6 copy-start.76
  1132.7 4.6 copy-start.75
  1132.7 4.7 copy-start.74
  1132.7 4.8 copy-start.73
  1132.7 4.9 copy-start.72
  1135.6 16.3 %copy-start.3 = (f32[512,1024]{1,0:T(8,128)S(1)}, f32[512,1024]{1,0:T(8,128)}, u32[]{:S(2)}) copy-start(f32[512,1024]{1,0:T(8,128)} %copy-done.2) | copy-start | bytes 6291460 | tf_op jit(solution)/shard_map/while
  1135.6 16.3 %copy-start.44 = (bf16[2,128,512]{2,1,0:T(8,128)(2,1)S(1)}, bf16[2,128,512]{2,1,0:T(8,128)(2,1)}, u32[]{:S(2)}) copy-start(bf16[2,128,512]{2,1,0:T(8,128)(2,1)} %copy-done.43) | copy-start | bytes 786436 | tf_op jit(solution)/shard_map/while
  1148.7 4.7 copy-start.12
  1148.7 4.7 copy-start.38
  1158.2 59.5 %copy-start.68 = (f32[1024,256]{1,0:T(8,128)}, f32[1024,256]{1,0:T(8,128)S(1)}, u32[]{:S(2)}) copy-start(f32[1024,256]{1,0:T(8,128)S(1)} %convolution_add_fusion.14) | copy-start | bytes 3145732 | tf_op jit(solution)/shard_map/while
  1220.4 202.7 %all-reduce.9.cloned.1.call-start = ((), (), s32[]{:S(2)}) async-start(), calls=%async_computation | async-start | bytes 29360128 | tf_op jit(solution)/shard_map/psum | solution.py:312
  1423.1 4.8 copy-start.70
  1423.1 5.8 copy-start.69
  (143 other events, 419.5 us)
Sparse Core Ops, SparseCore 0:
  98.2 89.1 all-reduce.10
  196.1 85.4 all-reduce.12
  306.4 85.4 all-reduce.14
  403.9 85.4 all-reduce.16
  535.4 86.0 all-reduce.18
  692.7 85.4 all-reduce.10
  786.9 85.4 all-reduce.12
  897.0 85.4 all-reduce.14
  994.5 85.4 all-reduce.16
  1126.0 86.1 all-reduce.18
Sparse Core Ops, SparseCore 1:
  1227.0 196.1 all-reduce.8
where the time goes:
time: 1450 us
  waiting for transfers between devices  919 us (63%)
  other arithmetic  246 us (17%)
  matrix products  127 us (9%)
  local copies, waits for them, and re-layouts  94.7 us (7%)
  blocking collectives  36.4 us (3%)
  between operations  15.9 us (1%)
    psum x4, waiting for transfers between devices, attend(): attended = lax.psum(low_product(mixed_heads, output_weight), 'mp')  307 us
    psum x1, waiting for transfers between devices, body(): totals = lax.psum(totals, 'dp')  187 us
    psum x2, waiting for transfers between devices, stream_step(): branch_out = lax.psum(low_product(activated, down_weight), 'mp')  171 us
    psum x2, waiting for transfers between devices, stream_step(): grad_ffn_input = lax.psum(back_product(grad_pre, up_weight), 'mp')  143 us
    psum x2, waiting for transfers between devices, stream_step(): lax.psum((grad_unit_seg, grad_first_kept), 'mp')  110 us
    reduce_sum x4, other arithmetic, stream_step(): jnp.sum(jnp.where((distance >= mark_value)[None], score_wide, 0.0), axis=...  63.7 us
    add x2, other arithmetic, body(): bias_table + relative_bias[:, position][:, None, None] * (distance >= mar...  50.5 us
    while x380, local copies, waits for them, and re-layouts  43.6 us
  transfers between devices with their start and end apart: 11, of which 11 were waited for; matrix products, arithmetic and copies ran while one was open for 7% of the time, Pallas kernels for 0%

commit v1 on v0

v1 whole, which is shorter than its diff:
```python
import functools
import math

import jax
import jax.numpy as jnp
from jax import lax
from jax.experimental import pallas as pl
from jax.experimental.pallas import tpu as pltpu
from jax.sharding import PartitionSpec as P

reach_marks = (1, 2, 3, 4, 5, 6, 7, 8, 12, 16, 24, 32, 48, 64, 96, 128, 192, 256, 384, 512, 768, 1024)
epsilon = 1e-06
masked_score = -1e30
block = 128
query_block = 256
f32 = jnp.float32
bf16 = jnp.bfloat16


def mm(left, right):
    return jnp.dot(left, right, preferred_element_type=f32)


def mm_t0(left, right):
    return lax.dot_general(left, right, (((0,), (0,)), ((), ())), preferred_element_type=f32)


def mm_t1(left, right):
    return lax.dot_general(left, right, (((1,), (1,)), ((), ())), preferred_element_type=f32)


def row_scale(source):
    return lax.rsqrt(jnp.mean(source * source, axis=-1, keepdims=True) + epsilon)


def diagonal_count(seg_len, kept_count):
    return (seg_len + kept_count) // block + 1


def diagonal_of(seg_len, kept_count, column):
    return (seg_len + kept_count) // block - 1 - column


def strip_start(seg_len, sub_block):
    return (seg_len // block - 1 - sub_block) * block


def bias_block(bias_ref, head, diagonal, transposed):
    rows = lax.broadcasted_iota(jnp.int32, (block, block), 0)
    cols = lax.broadcasted_iota(jnp.int32, (block, block), 1)
    distance = diagonal * block + ((cols - rows) if transposed else (rows - cols))
    lowest, highest = diagonal * block - block + 1, diagonal * block + block - 1
    base = jnp.float32(0.0)
    for position, mark_value in enumerate(reach_marks):
        if mark_value <= lowest:
            base = base + bias_ref[head, position]
    value = jnp.full((block, block), base, f32)
    for position, mark_value in enumerate(reach_marks):
        if lowest < mark_value <= highest:
            value = value + jnp.where(distance >= mark_value, bias_ref[head, position], 0.0)
    if lowest < 0:
        value = jnp.where(distance >= 0, value, masked_score)
    return value


def live_mask(shape, axis, packed_len, mem_len, packed_count, memory_count):
    slot = lax.broadcasted_iota(jnp.int32, shape, axis)
    dead_packed = (slot < packed_len) & (slot < packed_len - packed_count)
    dead_memory = (slot >= packed_len) & (slot < packed_len + mem_len - memory_count)
    return jnp.where(dead_packed | dead_memory, masked_score, 0.0).astype(f32)


def attend_kernel(
    sizes,
    memory_fill,
    packed_fill,
    bias_ref,
    seg_ref,
    memory_ref,
    packed_ref,
    gain_ref,
    wq_ref,
    wk_ref,
    wv_ref,
    unit_ref,
    q_ref,
    k_ref,
    v_ref,
    mixed_ref,
    log_ref,
    strip,
    live,
):
    seg_len, mem_len, packed_len, heads, head_dim = sizes
    kept = mem_len + packed_len
    keys = kept + seg_len
    stream = pl.program_id(0)
    scale = 1.0 / math.sqrt(head_dim)
    gain = gain_ref[...]
    start = 0
    for part_ref, size in ((packed_ref, packed_len), (memory_ref, mem_len), (seg_ref, seg_len)):
        rows = part_ref[0].astype(f32)
        unit = (rows * row_scale(rows) * gain).astype(bf16)
        unit_ref[0, start : start + size, :] = unit
        k_ref[0, start : start + size, :] = mm(unit, wk_ref[...]).astype(bf16)
        v_ref[0, start : start + size, :] = mm(unit, wv_ref[...]).astype(bf16)
        if start == kept:
            q_ref[0] = mm(unit, wq_ref[...]).astype(bf16)
        start += size
    live[...] = live_mask((8, kept), 1, packed_len, mem_len, packed_fill[stream], memory_fill[stream])
    for head in range(heads):
        lanes = slice(head * head_dim, (head + 1) * head_dim)
        for column in range(diagonal_count(seg_len, kept)):
            strip[:, column * block : (column + 1) * block] = bias_block(
                bias_ref, head, diagonal_of(seg_len, kept, column), False
            )
        for index in range(seg_len // query_block):
            reach = kept + (index + 1) * query_block
            rows = slice(index * query_block, (index + 1) * query_block)
            score = mm_t1(q_ref[0, rows, lanes], k_ref[0, :reach, lanes]) * scale
            parts = []
            for sub in range(query_block // block):
                first = strip_start(seg_len, index * (query_block // block) + sub)
                parts.append(strip[:, first : first + reach])
            score = score + jnp.concatenate(parts, axis=0)
            score = jnp.concatenate([score[:, :kept] + live[0:1, :], score[:, kept:]], axis=1)
            top = jnp.max(score, axis=-1, keepdims=True)
            weight = jnp.exp(score - top)
            total = jnp.sum(weight, axis=-1, keepdims=True)
            log_ref[0, head, rows, :] = top + jnp.log(total)
            mixed = mm(weight.astype(bf16), v_ref[0, :reach, lanes]) * (1.0 / total)
            mixed_ref[0, rows, lanes] = mixed.astype(bf16)


def attend(inputs, memory, packed, memory_fill, packed_fill, gain, wq, wk, wv, bias):
    streams, seg_len, width = inputs.shape
    mem_len, packed_len = memory.shape[1], packed.shape[1]
    heads = bias.shape[0]
    local = wq.shape[1]
    keys = seg_len + mem_len + packed_len
    sizes = (seg_len, mem_len, packed_len, heads, local // heads)
    smem = pl.BlockSpec(memory_space=pltpu.SMEM)

    def rows_of(count, columns):
        return pl.BlockSpec((1, count, columns), lambda s: (s, 0, 0))

    def whole(shape):
        return pl.BlockSpec(shape, lambda s: (0,) * len(shape))

    return pl.pallas_call(
        functools.partial(attend_kernel, sizes),
        grid=(streams,),
        in_specs=[
            smem,
            smem,
            smem,
            rows_of(seg_len, width),
            rows_of(mem_len, width),
            rows_of(packed_len, width),
            whole((1, width)),
            whole(wq.shape),
            whole(wk.shape),
            whole(wv.shape),
        ],
        out_specs=[
            rows_of(keys, width),
            rows_of(seg_len, local),
            rows_of(keys, local),
            rows_of(keys, local),
            rows_of(seg_len, local),
            pl.BlockSpec((1, heads, seg_len, 1), lambda s: (s, 0, 0, 0)),
        ],
        out_shape=[
            jax.ShapeDtypeStruct((streams, keys, width), bf16),
            jax.ShapeDtypeStruct((streams, seg_len, local), bf16),
            jax.ShapeDtypeStruct((streams, keys, local), bf16),
            jax.ShapeDtypeStruct((streams, keys, local), bf16),
            jax.ShapeDtypeStruct((streams, seg_len, local), bf16),
            jax.ShapeDtypeStruct((streams, heads, seg_len, 1), f32),
        ],
        scratch_shapes=[
            pltpu.VMEM((block, diagonal_count(seg_len, mem_len + packed_len) * block), f32),
            pltpu.VMEM((8, mem_len + packed_len), f32),
        ],
        compiler_params=pltpu.CompilerParams(vmem_limit_bytes=60 << 20),
        cost_estimate=pl.CostEstimate(
            flops=streams * (2 * keys * width * local * 3 + 4 * seg_len * keys * local),
            bytes_accessed=streams * keys * (width * 4 + local * 6),
            transcendentals=streams * heads * seg_len * keys,
        ),
        name="attend",
    )(memory_fill, packed_fill, bias, inputs, memory, packed, gain[None, :], wq, wk, wv)


def attend_back_kernel(
    sizes,
    memory_fill,
    packed_fill,
    bias_ref,
    unit_ref,
    q_ref,
    k_ref,
    v_ref,
    log_ref,
    gm_ref,
    wq_ref,
    wk_ref,
    wv_ref,
    gunit_ref,
    gq_ref,
    gk_ref,
    gv_ref,
    rel_ref,
    strip,
    live,
    dk_sum,
    dv_sum,
    dq_low,
    dk_low,
    dv_low,
    strip_sum,
):
    seg_len, mem_len, packed_len, heads, head_dim = sizes
    kept = mem_len + packed_len
    keys = kept + seg_len
    stream = pl.program_id(0)
    scale = 1.0 / math.sqrt(head_dim)

    @pl.when(stream == 0)
    def _():
        strip_sum[...] = jnp.zeros_like(strip_sum)
        gq_ref[...] = jnp.zeros_like(gq_ref)
        gk_ref[...] = jnp.zeros_like(gk_ref)
        gv_ref[...] = jnp.zeros_like(gv_ref)

    live[...] = live_mask((kept, block), 0, packed_len, mem_len, packed_fill[stream], memory_fill[stream])
    subs = query_block // block
    for head in range(heads):
        lanes = slice(head * head_dim, (head + 1) * head_dim)
        for column in range(diagonal_count(seg_len, kept)):
            strip[column * block : (column + 1) * block, :] = bias_block(
                bias_ref, head, diagonal_of(seg_len, kept, column), True
            )
        for index in range(seg_len // query_block):
            reach = kept + (index + 1) * query_block
            rows = slice(index * query_block, (index + 1) * query_block)
            queries = q_ref[0, rows, lanes]
            grads = gm_ref[0, rows, lanes]
            key_rows = k_ref[0, :reach, lanes]
            score = mm_t1(key_rows, queries) * scale
            firsts = [strip_start(seg_len, index * subs + sub) for sub in range(subs)]
            score = score + jnp.concatenate([strip[first : first + reach, :] for first in firsts], axis=1)
            live_wide = jnp.concatenate([live[...]] * subs, axis=1)
            score = jnp.concatenate([score[:kept] + live_wide, score[kept:]], axis=0)
            prob = jnp.exp(score - log_ref[0, head, :, rows])
            grad_prob = mm_t1(v_ref[0, :reach, lanes], grads)
            delta = jnp.sum(prob * grad_prob, axis=0, keepdims=True)
            grad_score = (prob * (grad_prob - delta)).astype(bf16)
            dk_part = mm(grad_score, queries)
            dv_part = mm(prob.astype(bf16), grads)
            if index == seg_len // query_block - 1:
                earlier = kept + index * query_block
                if index:
                    dk_sum[:earlier] += dk_part[:earlier]
                    dv_sum[:earlier] += dv_part[:earlier]
                    dk_sum[earlier:] = dk_part[earlier:]
                    dv_sum[earlier:] = dv_part[earlier:]
                else:
                    dk_sum[...] = dk_part
                    dv_sum[...] = dv_part
            elif index:
                earlier = kept + index * query_block
                dk_sum[:earlier] += dk_part[:earlier]
                dv_sum[:earlier] += dv_part[:earlier]
                dk_sum[earlier:reach] = dk_part[earlier:]
                dv_sum[earlier:reach] = dv_part[earlier:]
            else:
                dk_sum[:reach] = dk_part
                dv_sum[:reach] = dv_part
            dq_low[rows, lanes] = (mm_t0(grad_score, key_rows) * scale).astype(bf16)
            for sub in range(subs):
                strip_sum[head, firsts[sub] : firsts[sub] + reach, :] += grad_score[
                    :, sub * block : (sub + 1) * block
                ].astype(f32)
        dk_low[:, lanes] = (dk_sum[...] * scale).astype(bf16)
        dv_low[:, lanes] = dv_sum[...].astype(bf16)
    gq_ref[...] += mm_t0(dq_low[...], unit_ref[0, kept:, :])
    gk_ref[...] += mm_t0(dk_low[...], unit_ref[0])
    gv_ref[...] += mm_t0(dv_low[...], unit_ref[0])
    gunit_ref[0] = (
        mm_t1(dq_low[...], wq_ref[...])
        + mm_t1(dk_low[kept:, :], wk_ref[...])
        + mm_t1(dv_low[kept:, :], wv_ref[...])
    )

    @pl.when(stream == pl.num_programs(0) - 1)
    def _():
        rows = lax.broadcasted_iota(jnp.int32, (block, block), 0)
        cols = lax.broadcasted_iota(jnp.int32, (block, block), 1)
        for head in range(heads):
            blocks = []
            for column in range(diagonal_count(seg_len, kept)):
                blocks.append(strip_sum[head, column * block : (column + 1) * block, :])
            for position, mark_value in enumerate(reach_marks):
                total = jnp.zeros((1, block), f32)
                for column, value in enumerate(blocks):
                    diagonal = diagonal_of(seg_len, kept, column)
                    lowest, highest = diagonal * block - block + 1, diagonal * block + block - 1
                    if mark_value <= lowest:
                        total = total + jnp.sum(value, axis=0, keepdims=True)
                    elif mark_value <= highest:
                        distance = diagonal * block + cols - rows
                        total = total + jnp.sum(
                            jnp.where(distance >= mark_value, value, 0.0), axis=0, keepdims=True
                        )
                rel_ref[head, position : position + 1, :] = total


def attend_back(unit, q, k, v, log_total, grad_mixed, memory_fill, packed_fill, wq, wk, wv, bias, mem_len, packed_len):
    streams, keys, width = unit.shape
    seg_len, local = q.shape[1:]
    heads = bias.shape[0]
    kept = mem_len + packed_len
    sizes = (seg_len, mem_len, packed_len, heads, local // heads)
    smem = pl.BlockSpec(memory_space=pltpu.SMEM)
    strip_len = diagonal_count(seg_len, kept) * block

    def rows_of(count, columns):
        return pl.BlockSpec((1, count, columns), lambda s: (s, 0, 0))

    def whole(shape):
        return pl.BlockSpec(shape, lambda s: (0,) * len(shape))

    return pl.pallas_call(
        functools.partial(attend_back_kernel, sizes),
        grid=(streams,),
        in_specs=[
            smem,
            smem,
            smem,
            rows_of(keys, width),
            rows_of(seg_len, local),
            rows_of(keys, local),
            rows_of(keys, local),
            pl.BlockSpec((1, heads, 1, seg_len), lambda s: (s, 0, 0, 0)),
            rows_of(seg_len, local),
            whole(wq.shape),
            whole(wk.shape),
            whole(wv.shape),
        ],
        out_specs=[
            rows_of(seg_len, width),
            whole((local, width)),
            whole((local, width)),
            whole((local, width)),
            whole((heads, 24, block)),
        ],
        out_shape=[
            jax.ShapeDtypeStruct((streams, seg_len, width), f32),
            jax.ShapeDtypeStruct((local, width), f32),
            jax.ShapeDtypeStruct((local, width), f32),
            jax.ShapeDtypeStruct((local, width), f32),
            jax.ShapeDtypeStruct((heads, 24, block), f32),
        ],
        scratch_shapes=[
            pltpu.VMEM((strip_len, block), f32),
            pltpu.VMEM((kept, block), f32),
            pltpu.VMEM((keys, local // heads), f32),
            pltpu.VMEM((keys, local // heads), f32),
            pltpu.VMEM((seg_len, local), bf16),
            pltpu.VMEM((keys, local), bf16),
            pltpu.VMEM((keys, local), bf16),
            pltpu.VMEM((heads, strip_len, block), f32),
        ],
        compiler_params=pltpu.CompilerParams(vmem_limit_bytes=60 << 20),
        cost_estimate=pl.CostEstimate(
            flops=streams * (8 * keys * width * local + 10 * seg_len * keys * local),
            bytes_accessed=streams * keys * (width * 2 + local * 6),
            transcendentals=streams * heads * seg_len * keys,
        ),
        name="attend_back",
    )(
        memory_fill,
        packed_fill,
        bias,
        unit,
        q,
        k,
        v,
        log_total.reshape(streams, heads, 1, seg_len),
        grad_mixed,
        wq,
        wk,
        wv,
    )


def line_gather(shard, size):
    me = lax.axis_index("mp")
    to_right = to_left = shard
    from_left, from_right = [], []
    for step in range(1, size):
        to_right = lax.ppermute(to_right, "mp", [(i, i + 1) for i in range(step - 1, size - 1)])
        to_left = lax.ppermute(to_left, "mp", [(i, i - 1) for i in range(1, size - step + 1)])
        from_left.append(to_right)
        from_right.append(to_left)
    ordered = jnp.stack(from_left[::-1] + [shard] + from_right)
    return lax.dynamic_slice_in_dim(ordered, size - 1 - me, size, 0)


def line_scatter(parts, size):
    me = lax.axis_index("mp")

    def pick(index):
        return lax.dynamic_index_in_dim(parts, jnp.clip(index, 0, size - 1), 0, keepdims=False)

    from_left = from_right = None
    for step in range(size - 1):
        rightward = pick(size - 1 - (step - me))
        leftward = pick(step - (size - 1 - me))
        if step:
            rightward = rightward + from_left
            leftward = leftward + from_right
        pairs = [(i, i + 1) for i in range(size - 1) if step >= i and size - 1 - (step - i) > i]
        from_left = lax.ppermute(rightward, "mp", pairs)
        from_right = lax.ppermute(leftward, "mp", [(size - 1 - a, size - 1 - b) for a, b in pairs])
    return pick(me) + from_left + from_right


def body(
    inputs,
    memory,
    compressed_memory,
    memory_fill,
    compressed_fill,
    first_gain,
    query_weight,
    key_weight,
    value_weight,
    relative_bias,
    output_weight,
    second_gain,
    up_weight,
    down_weight,
    compress_weight,
    grad_output,
    grad_compressed,
    *,
    mp_size,
):
    streams, seg_len, width = inputs.shape
    mem_len = memory.shape[1]
    packed_len = compressed_memory.shape[1]
    heads_here = relative_bias.shape[0]
    local = query_weight.shape[1]
    compress_count = grad_compressed.shape[1]
    rows = streams * seg_len
    shard_rows = rows // mp_size
    me = lax.axis_index("mp")

    def own_rows(source):
        return lax.dynamic_slice_in_dim(source, me * shard_rows, shard_rows, 0)

    nothing = jnp.minimum(jnp.abs(first_gain[0]), 0.0)
    full_out = (line_gather(output_weight.astype(f32), mp_size) + nothing).reshape(width, width).astype(bf16)

    slot_index = jnp.arange(mem_len, dtype=jnp.int32)
    live_rows = jnp.where(
        (slot_index[None, :] >= mem_len - memory_fill[:, None])[:, :, None], memory, jnp.zeros_like(memory)
    )
    evicted = live_rows.reshape(streams * compress_count, 2 * width)
    packed_new = mm(evicted, compress_weight).astype(bf16).reshape(streams, compress_count, -1)
    grad_compress_w = mm_t0(evicted, grad_compressed.reshape(streams * compress_count, -1))

    unit, q, k, v, mixed, log_total = attend(
        inputs,
        memory,
        compressed_memory,
        memory_fill,
        compressed_fill,
        first_gain,
        query_weight,
        key_weight,
        value_weight,
        relative_bias,
    )
    mixed_all = line_gather(mixed.reshape(rows, local).astype(f32), mp_size)
    mixed_all = (mixed_all + nothing).transpose(1, 0, 2).reshape(rows, width).astype(bf16)
    seg_rows = inputs.reshape(rows, width)
    grad_rows = grad_output.reshape(rows, width)
    residual = seg_rows.astype(f32) + mm(mixed_all, full_out)
    second_scale = row_scale(residual)
    ffn_input = (residual * second_scale * second_gain).astype(bf16)
    pre_act = mm(ffn_input, up_weight)
    inner = math.sqrt(2.0 / math.pi)
    squared = pre_act * pre_act
    tanh = jnp.tanh(inner * (pre_act + 0.044715 * pre_act * squared))
    activated = (0.5 * pre_act * (1.0 + tanh)).astype(bf16)
    slope = 0.5 * (1.0 + tanh) + 0.5 * pre_act * (1.0 - tanh * tanh) * (
        inner * (1.0 + 3.0 * 0.044715 * squared)
    )
    grad_pre = (slope * mm_t1(grad_rows, down_weight)).astype(bf16)
    grad_ffn = mm_t1(grad_pre, up_weight)
    grad_ffn = line_scatter(grad_ffn.reshape(mp_size, shard_rows, width), mp_size)

    own_residual = own_rows(residual)
    own_scale = own_rows(second_scale)
    own_grad = own_rows(grad_rows).astype(f32)
    normed = own_residual * own_scale
    grad_second = jnp.sum(grad_ffn * normed, axis=0)
    weighted = grad_ffn * second_gain
    grad_residual = own_grad + own_scale * (
        weighted - normed * jnp.mean(weighted * normed, axis=-1, keepdims=True)
    )
    grad_attended = grad_residual.astype(bf16)
    grad_mixed_rows = mm_t1(grad_attended, full_out).astype(bf16)
    exchanged = lax.all_to_all(
        grad_mixed_rows.astype(f32).reshape(shard_rows, mp_size, local).transpose(1, 0, 2), "mp", 0, 0
    )
    grad_mixed = (exchanged + nothing).reshape(streams, seg_len, local).astype(bf16)
    grad_out_full = mm_t0(own_rows(mixed_all), grad_attended)

    branch = mm(activated, down_weight)
    branch_own = line_scatter(branch.reshape(mp_size, shard_rows, width), mp_size)
    result_own = (own_residual + branch_own).astype(bf16)
    grad_down = mm_t0(activated, grad_rows)
    grad_up = mm_t0(ffn_input, grad_pre)

    grad_unit, gq, gk, gv, rel = attend_back(
        unit,
        q,
        k,
        v,
        log_total,
        grad_mixed,
        memory_fill,
        compressed_fill,
        query_weight,
        key_weight,
        value_weight,
        relative_bias,
        mem_len,
        packed_len,
    )
    grad_relative = jnp.sum(rel, axis=-1)[:, : len(reach_marks)]
    grad_unit = line_scatter(grad_unit.reshape(mp_size, shard_rows, width), mp_size)
    own_seg = own_rows(seg_rows).astype(f32)
    seg_scale = row_scale(own_seg)
    seg_normed = own_seg * seg_scale
    seg_weighted = grad_unit * first_gain
    grad_seg_own = (
        grad_residual
        + seg_scale * (seg_weighted - seg_normed * jnp.mean(seg_weighted * seg_normed, axis=-1, keepdims=True))
    ).astype(bf16)

    result = (line_gather(result_own.astype(f32), mp_size) + nothing).reshape(inputs.shape).astype(bf16)
    grad_seg = (line_gather(grad_seg_own.astype(f32), mp_size) + nothing).reshape(inputs.shape).astype(bf16)

    grad_out_w = lax.psum_scatter(grad_out_full, "mp", scatter_dimension=0, tiled=True)
    gq, gk, gv, grad_out_w, grad_up, grad_down, grad_compress_w, grad_relative = lax.psum(
        (gq, gk, gv, grad_out_w, grad_up, grad_down, grad_compress_w, grad_relative), "dp"
    )
    grad_query_w, grad_key_w, grad_value_w = gq.T, gk.T, gv.T
    grad_first = (
        jnp.sum(
            grad_query_w * query_weight.astype(f32)
            + grad_key_w * key_weight.astype(f32)
            + grad_value_w * value_weight.astype(f32),
            axis=1,
        )
        / first_gain
    )
    grad_first = lax.psum(grad_first, "mp")
    grad_second = lax.psum(grad_second, ("dp", "mp"))
    return (
        result,
        packed_new,
        grad_seg,
        grad_first,
        grad_query_w,
        grad_key_w,
        grad_value_w,
        grad_relative,
        grad_out_w,
        grad_second,
        grad_up,
        grad_down,
        grad_compress_w,
    )


def solution(mesh):
    in_specs = (
        P("dp", None, None),
        P("dp", None, None),
        P("dp", None, None),
        P("dp"),
        P("dp"),
        P(),
        P(None, "mp"),
        P(None, "mp"),
        P(None, "mp"),
        P("mp", None),
        P("mp", None),
        P(),
        P(None, "mp"),
        P("mp", None),
        P(None, "mp"),
        P("dp", None, None),
        P("dp", None, "mp"),
    )
    out_specs = (
        P("dp", None, None),
        P("dp", None, "mp"),
        P("dp", None, None),
        P(),
        P(None, "mp"),
        P(None, "mp"),
        P(None, "mp"),
        P("mp", None),
        P("mp", None),
        P(),
        P(None, "mp"),
        P("mp", None),
        P(None, "mp"),
    )
    return jax.shard_map(
        functools.partial(body, mp_size=mesh.shape["mp"]),
        mesh=mesh,
        in_specs=in_specs,
        out_specs=out_specs,
        check_vma=False,
    )
```

time: 1450 us -> 800 us (0.55)
  waiting for transfers between devices: 919 us -> 363 us
  other arithmetic: 246 us -> 49.1 us
  starting transfers between devices: 0.47 us -> 121 us
  matrix products: 127 us -> 35.1 us
  blocking collectives: 36.4 us -> 104 us
  Pallas kernels: 0 us -> 39.8 us
  local copies, waits for them, and re-layouts: 94.7 us -> 63.6 us
    psum x11 -> x1, waiting for transfers between devices: 918 us -> 0.01 us  [body(): lax.psum((gq, gk, gv, grad_out_w, grad_up, grad_down, grad_compress_w, gr...]
    ppermute x0 -> x42, waiting for transfers between devices: none -> 313 us  [the longest x12 134 us: line_gather(): lax.ppermute(to_left, 'mp', [(i, i - 1) for i in range(1, size - step + 1)])]
    ppermute x0 -> x42, starting transfers between devices: none -> 103 us  [the longest x9 37.4 us: line_scatter(): from_left = lax.ppermute(rightward, 'mp', pairs)]
    dot_general x64 -> x11, matrix products: 127 us -> 35.1 us  [the longest x4 15.4 us: mm_t0(): lax.dot_general(left, right, (((0,), (0,)), ((), ())), preferred_element_...]
    reduce_sum x26 -> x5, other arithmetic: 97.2 us -> 8.22 us  [the longest x1 2.6 us: body(): grad_second = jnp.sum(grad_ffn * normed, axis=0)]
    psum x3, blocking collectives: 36.4 us -> 104 us  [the longest x1 80.9 us: body(): grad_second = lax.psum(grad_second, ('dp', 'mp'))]
    all_to_all x0 -> x1, waiting for transfers between devices: none -> 49.9 us  [body(): lax.all_to_all(grad_mixed_rows.astype(f32).reshape(shard_rows, mp_size, l...]
    while x380 -> x0, local copies, waits for them, and re-layouts: 43.6 us -> none
  transfers between devices with their start and end apart: 11 -> 45, of which waited for: 11 -> 25; matrix products, arithmetic and copies ran while one was open for 7% -> 13% of each run, Pallas kernels for 0% -> 3%
where the time goes in v1:
time: 800 us; the launch traced here: 791 us
  waiting for transfers between devices  363 us (45%)
  starting transfers between devices  121 us (15%)
  blocking collectives  104 us (13%)
  local copies, waits for them, and re-layouts  63.6 us (8%)
  other arithmetic  49.1 us (6%)
  Pallas kernels  39.8 us (5%)
  matrix products  35.1 us (4%)
  between operations  15.8 us (2%)
    ppermute x12, waiting for transfers between devices, line_gather(): lax.ppermute(to_left, 'mp', [(i, i - 1) for i in range(1, size - step + 1)])  134 us
    ppermute x9, waiting for transfers between devices, line_scatter(): from_left = lax.ppermute(rightward, 'mp', pairs)  125 us
    psum x1, blocking collectives, body(): grad_second = lax.psum(grad_second, ('dp', 'mp'))  80.9 us
    unnamed x99, local copies, waits for them, and re-layouts  50.1 us
    all_to_all x1, waiting for transfers between devices, body(): lax.all_to_all(grad_mixed_rows.astype(f32).reshape(shard_rows, mp_size, l...  49.9 us
    ppermute x12, waiting for transfers between devices, line_gather(): lax.ppermute(to_right, 'mp', [(i, i + 1) for i in range(step - 1, size -...  38.2 us
    ppermute x9, starting transfers between devices, line_scatter(): from_left = lax.ppermute(rightward, 'mp', pairs)  37.4 us
    ppermute x12, starting transfers between devices, line_gather(): lax.ppermute(to_right, 'mp', [(i, i + 1) for i in range(step - 1, size -...  36.9 us
  transfers between devices with their start and end apart: 45, of which 25 were waited for; matrix products, arithmetic and copies ran while one was open for 13% of the time, Pallas kernels for 3%

profile of v1, /device:TPU:0, one launch (start us, length us, event | category | flops | bytes accessed | tf_op | source)
XLA Modules:
  0.0 790.8 jit_solution(9204408342312434294)
XLA Ops:
  7.3 16.2 %attend.1 = (bf16[2,1536,1024]{2,1,0:T(8,128)(2,1)}, bf16[2,512,256]{2,1,0:T(8,128)(2,1)}, bf16[2,1536,256]{2,1,0:T(8,128)(2,1)}, bf16[2,1536,256]{2,1,0:T(8,128...) custom-call(s32[2]{0:T(128)} %memory_fill.3, s32[2]{0:T(128)} %packed_fill.3, f32[2,22]{1,0:T(2,128)} %bias_ref.3, ...), custom_call_target="tpu_custom_call" | custom-call | flops 6442450944 | bytes 17301504 | tf_op jit(solution)/shard_map/attend/pallas_call | solution.py:150
  24.6 5.0 collective-permute-start
  31.0 5.5 collective-permute-start.6
  37.8 15.2 %collective-permute-done = f32[1024,256]{1,0:T(8,128)S(1)} collective-permute-done((f32[1024,256]{1,0:T(8,128)S(1)}, f32[1024,256]{1,0:T(8,128)S(1)}, u32[]{:S(2)}, u32[]{:S(2)}) %collective-permute-start) | collective-permute-done | bytes 1048608 | tf_op jit(solution)/shard_map/ppermute | solution.py:403
  54.7 3.0 collective-permute-done.3
  59.0 15.4 %collective-permute-done.6 = f32[256,1024]{1,0:T(8,128)} collective-permute-done((f32[256,1024]{1,0:T(8,128)S(1)}, f32[256,1024]{1,0:T(8,128)}, u32[]{:S(2)}, u32[]{:S(2)}) %collective-permute-start.6) | collective-permute-done | bytes 1048608 | tf_op jit(solution)/shard_map/ppermute | solution.py:403
  76.1 4.1 collective-permute-done.9
  84.3 18.3 %collective-permute-done.4 = f32[1024,256]{1,0:T(8,128)} collective-permute-done((f32[1024,256]{1,0:T(8,128)}, f32[1024,256]{1,0:T(8,128)}, u32[]{:S(2)}, u32[]{:S(2)}) %collective-permute-start.4) | collective-permute-done | bytes 1048608 | tf_op jit(solution)/shard_map/ppermute | solution.py:404
  104.6 20.4 %collective-permute-done.10 = f32[256,1024]{1,0:T(8,128)} collective-permute-done((f32[256,1024]{1,0:T(8,128)}, f32[256,1024]{1,0:T(8,128)}, u32[]{:S(2)}, u32[]{:S(2)}) %collective-permute-start.10) | collective-permute-done | bytes 1048608 | tf_op jit(solution)/shard_map/ppermute | solution.py:404
  132.0 15.5 %collective-permute-done.5 = f32[1024,256]{1,0:T(8,128)S(1)} collective-permute-done((f32[1024,256]{1,0:T(8,128)}, f32[1024,256]{1,0:T(8,128)S(1)}, u32[]{:S(2)}, u32[]{:S(2)}) %collective-permute-start.5) | collective-permute-done | bytes 1048608 | tf_op jit(solution)/shard_map/ppermute | solution.py:404
  154.1 14.3 %collective-permute-done.11 = f32[256,1024]{1,0:T(8,128)S(1)} collective-permute-done((f32[256,1024]{1,0:T(8,128)}, f32[256,1024]{1,0:T(8,128)S(1)}, u32[]{:S(2)}, u32[]{:S(2)}) %collective-permute-start.11) | collective-permute-done | bytes 1048608 | tf_op jit(solution)/shard_map/ppermute | solution.py:404
  169.2 2.5 multiply_reduce_fusion
  176.2 4.4 multiply_convert_fusion
  184.5 2.5 collective-permute-start.24
  187.0 4.6 fusion.26
  193.3 2.7 collective-permute-start.12
  197.7 12.2 %collective-permute-done.24 = f32[256,1024]{1,0:T(8,128)} collective-permute-done((f32[256,1024]{1,0:T(8,128)}, f32[256,1024]{1,0:T(8,128)}, u32[]{:S(2)}, u32[]{:S(2)}) %collective-permute-start.24) | collective-permute-done | bytes 1048608 | tf_op jit(solution)/shard_map/ppermute | solution.py:425
  209.9 2.7 bitcast_add_fusion.8
  212.6 5.4 collective-permute-start.25
  219.6 12.7 %collective-permute-done.12 = f32[256,1024]{1,0:T(8,128)} collective-permute-done((f32[256,1024]{1,0:T(8,128)S(1)}, f32[256,1024]{1,0:T(8,128)}, u32[]{:S(2)}, u32[]{:S(2)}) %collective-permute-start.12) | collective-permute-done | bytes 1048608 | tf_op jit(solution)/shard_map/ppermute | solution.py:425
  234.0 5.5 collective-permute-start.13
  239.4 15.4 %collective-permute-done.25 = f32[256,1024]{1,0:T(8,128)} collective-permute-done((f32[256,1024]{1,0:T(8,128)}, f32[256,1024]{1,0:T(8,128)}, u32[]{:S(2)}, u32[]{:S(2)}) %collective-permute-start.25) | collective-permute-done | bytes 1048608 | tf_op jit(solution)/shard_map/ppermute | solution.py:425
  254.9 4.0 bitcast_add_fusion.9
  260.5 14.3 %collective-permute-done.13 = f32[256,1024]{1,0:T(8,128)} collective-permute-done((f32[256,1024]{1,0:T(8,128)S(1)}, f32[256,1024]{1,0:T(8,128)}, u32[]{:S(2)}, u32[]{:S(2)}) %collective-permute-start.13) | collective-permute-done | bytes 1048608 | tf_op jit(solution)/shard_map/ppermute | solution.py:425
  274.8 4.1 bitcast_add_fusion.14
  280.6 5.1 collective-permute-start.26
  285.8 2.7 bitcast_add_fusion.7
  289.8 4.6 collective-permute-start.14
  294.4 2.7 bitcast_add_fusion.12
  300.8 7.9 collective-permute-done.26
  308.7 8.1 %collective-permute-done.29 = f32[256,1024]{1,0:T(8,128)} collective-permute-done((f32[256,1024]{1,0:T(8,128)}, f32[256,1024]{1,0:T(8,128)}, u32[]{:S(2)}, u32[]{:S(2)}) %collective-permute-start.29) | collective-permute-done | bytes 1048608 | tf_op jit(solution)/shard_map/ppermute | solution.py:426
  316.8 2.6 multiply_reduce_fusion.1
  319.4 8.5 %collective-permute-done.14 = f32[256,1024]{1,0:T(8,128)S(1)} collective-permute-done((f32[256,1024]{1,0:T(8,128)}, f32[256,1024]{1,0:T(8,128)S(1)}, u32[]{:S(2)}, u32[]{:S(2)}) %collective-permute-start.14) | collective-permute-done | bytes 1048608 | tf_op jit(solution)/shard_map/ppermute | solution.py:425
  327.8 7.8 collective-permute-done.17
  335.6 3.4 multiply_add_fusion
  339.0 3.9 fusion.18
  344.8 17.1 %all-to-all-start = ((f32[4,256,256]{2,1,0:T(8,128)}), f32[4,256,256]{2,1,0:T(8,128)S(1)}, u32[]{:S(2)}, u32[]{:S(2)}) async-start(f32[4,256,256]{2,1,0:T(8,128)} %bitcast.157), calls=%async_computation | async-start | bytes 2097152 | tf_op jit(solution)/shard_map/all_to_all | solution.py:517
  362.9 49.9 %all-to-all-done = f32[4,256,256]{2,1,0:T(8,128)S(1)} async-done(((f32[4,256,256]{2,1,0:T(8,128)}), f32[4,256,256]{2,1,0:T(8,128)S(1)}, u32[]{:S(2)}, u32[]{:S(2)}) %all-to-all-start) | async-done | bytes 1048608 | tf_op jit(solution)/shard_map/all_to_all | solution.py:517
  413.6 23.7 %attend_back.1 = (f32[2,512,1024]{2,1,0:T(8,128)}, f32[256,1024]{1,0:T(8,128)}, f32[256,1024]{1,0:T(8,128)}, f32[256,1024]{1,0:T(8,128)}, f32[2,24,128]{2,1,0:T(8,128)}) custom-call(s32[2]{0:T(128)} %memory_fill.3, s32[2]{0:T(128)} %packed_fill.3, f32[2,22]{1,0:T(2,128)} %bias_ref.3, bf16[2,1536,1024]{2,1,0:T(8,128)(2,1)} %get-tuple-element.25.unit_ref, ...), custom_call_target="tpu_custom_call" | custom-call | flops 10468982784 | bytes 11010048 | tf_op jit(solution)/shard_map/attend_back/pallas_call | solution.py:334
  437.4 2.9 dynamic-slice_bitcast_fusion.1
  443.6 22.5 %collective-permute-done.30 = f32[256,1024]{1,0:T(8,128)S(1)} collective-permute-done((f32[256,1024]{1,0:T(8,128)S(1)}, f32[256,1024]{1,0:T(8,128)S(1)}, u32[]{:S(2)}, u32[]{:S(2)}) %collective-permute-start.30) | collective-permute-done | bytes 1048608 | tf_op jit(solution)/shard_map/ppermute | solution.py:425
  468.5 5.3 collective-permute-start.31
  475.5 2.7 reshape.152
  478.2 15.3 %collective-permute-done.31 = f32[256,1024]{1,0:T(8,128)} collective-permute-done((f32[256,1024]{1,0:T(8,128)}, f32[256,1024]{1,0:T(8,128)}, u32[]{:S(2)}, u32[]{:S(2)}) %collective-permute-start.31) | collective-permute-done | bytes 1048608 | tf_op jit(solution)/shard_map/ppermute | solution.py:425
  493.5 3.6 bitcast_add_fusion.4
  500.2 4.8 fusion.25
  505.0 6.1 collective-permute-start.18
  511.1 4.6 collective-permute-start.32
  519.3 4.6 fusion.23
  526.5 7.5 collective-permute-done.18
  535.7 16.6 %collective-permute-done.32 = f32[256,1024]{1,0:T(8,128)} collective-permute-done((f32[256,1024]{1,0:T(8,128)}, f32[256,1024]{1,0:T(8,128)}, u32[]{:S(2)}, u32[]{:S(2)}) %collective-permute-start.32) | collective-permute-done | bytes 1048608 | tf_op jit(solution)/shard_map/ppermute | solution.py:425
  552.3 2.5 fusion.4
  557.1 8.8 %collective-permute-start.36 = (f32[256,1024]{1,0:T(8,128)}, f32[256,1024]{1,0:T(8,128)S(1)}, u32[]{:S(2)}, u32[]{:S(2)}) collective-permute-start(f32[256,1024]{1,0:T(8,128)} %fusion.17), channel_id=1, source_target_pairs={{0,1},{1,2},{2,3},{4,5},{5,6},{6,7},{8,9},{9,10},{10,11},{12,13},{... | collective-permute-start | bytes 3145736 | tf_op jit(solution)/shard_map/ppermute | solution.py:403
  566.0 4.1 collective-permute-done.21
  582.1 2.7 convolution_convert_fusion.1
  584.8 80.9 %psum.76 = f32[1024]{0:T(1024)} all-reduce(f32[1024]{0:T(1024)S(1)} %get-tuple-element.61), channel_id=1, replica_groups=mesh['dp'=8,'mp'=4] {'dp','mp'}, use_global_device_ids=true, to_apply=%region_14.15 | all-reduce | flops 1024 | bytes 8192 | tf_op jit(solution)/shard_map/psum | solution.py:574
  665.8 13.9 %psum.74 = f32[2,22]{1,0:T(2,128)} all-reduce(f32[2,22]{1,0:T(2,128)S(1)} %bitcast.191), channel_id=1, replica_groups=mesh['dp'=8,'mp'=4] {'dp'}, use_global_device_ids=true, to_apply=%region_10.11 | all-reduce | flops 44 | bytes 352 | tf_op jit(solution)/shard_map/psum | solution.py:560
  690.9 17.0 %collective-permute-done.23 = f32[256,1024]{1,0:T(8,128)S(1)} collective-permute-done((f32[256,1024]{1,0:T(8,128)}, f32[256,1024]{1,0:T(8,128)S(1)}, u32[]{:S(2)}, u32[]{:S(2)}) %collective-permute-start.23) | collective-permute-done | bytes 1048608 | tf_op jit(solution)/shard_map/ppermute | solution.py:404
  709.9 18.1 %collective-permute-done.40 = f32[256,1024]{1,0:T(8,128)S(1)} collective-permute-done((f32[256,1024]{1,0:T(8,128)}, f32[256,1024]{1,0:T(8,128)S(1)}, u32[]{:S(2)}, u32[]{:S(2)}) %collective-permute-start.40) | collective-permute-done | bytes 1048608 | tf_op jit(solution)/shard_map/ppermute | solution.py:404
  733.7 19.0 %collective-permute-done.41 = f32[256,1024]{1,0:T(8,128)S(1)} collective-permute-done((f32[256,1024]{1,0:T(8,128)S(1)}, f32[256,1024]{1,0:T(8,128)S(1)}, u32[]{:S(2)}, u32[]{:S(2)}) %collective-permute-start.41) | collective-permute-done | bytes 1048608 | tf_op jit(solution)/shard_map/ppermute | solution.py:404
  754.7 2.7 copy.43
  757.4 2.5 copy.44
  763.1 9.0 %psum.73 = f32[1024]{0:T(1024)} all-reduce(f32[1024]{0:T(1024)S(1)} %div.23), channel_id=1, replica_groups=mesh['dp'=8,'mp'=4] {'mp'}, use_global_device_ids=true, to_apply=%region_8.9 | all-reduce | flops 1024 | bytes 8192 | tf_op jit(solution)/shard_map/psum | solution.py:573
  774.4 4.9 copy.81
  (189 shorter events, 118.6 us)
Async XLA Ops:
  7.2 164.5 %copy-start = (bf16[1024,1024]{1,0:T(8,128)(2,1)S(1)}, bf16[1024,1024]{1,0:T(8,128)(2,1)}, u32[]{:S(2)}) copy-start(bf16[1024,1024]{1,0:T(8,128)(2,1)} %param.29) | copy-start | bytes 6291460
  7.2 516.7 %reduce-scatter.2.cloned.1.call-start = ((), (), s32[]{:S(2)}) async-start(), calls=%async_computation.2 | async-start | bytes 5242880 | tf_op jit(solution)/shard_map/reduce_scatter | solution.py:559
  7.2 23.6 %copy-start.11 = (bf16[256,1024]{1,0:T(8,128)(2,1)S(1)}, bf16[256,1024]{1,0:T(8,128)(2,1)}, u32[]{:S(2)}) copy-start(bf16[256,1024]{1,0:T(8,128)(2,1)} %param.27) | copy-start | bytes 1572868
  7.3 75.8 %copy-start.26 = (f32[1024]{0:T(1024)S(1)}, f32[1024]{0:T(1024)}, u32[]{:S(2)}) copy-start(f32[1024]{0:T(1024)} %param.22) | copy-start | bytes 12292
  24.6 28.5 %collective-permute-start = (f32[1024,256]{1,0:T(8,128)S(1)}, f32[1024,256]{1,0:T(8,128)S(1)}, u32[]{:S(2)}, u32[]{:S(2)}) collective-permute-start(f32[1024,256]{1,0:T(8,128)S(1)} %bitcast.171), channel_id=1, source_target_pairs={{0,1},{1,2},{2,3},{4,5},{5,6},{6,7},{8,9},{9,10},{10,11},{12,13},{... | collective-permute-start | bytes 3145736 | tf_op jit(solution)/shard_map/ppermute | solution.py:403
  29.6 28.1 %collective-permute-start.3 = (f32[1024,256]{1,0:T(8,128)S(1)}, f32[1024,256]{1,0:T(8,128)}, u32[]{:S(2)}, u32[]{:S(2)}) collective-permute-start(f32[1024,256]{1,0:T(8,128)S(1)} %bitcast.172), channel_id=1, source_target_pairs={{1,0},{2,1},{3,2},{5,4},{6,5},{7,6},{9,8},{10,9},{11,10},{13,12},{... | collective-permute-start | bytes 3145736 | tf_op jit(solution)/shard_map/ppermute | solution.py:404
  31.0 43.4 %collective-permute-start.6 = (f32[256,1024]{1,0:T(8,128)S(1)}, f32[256,1024]{1,0:T(8,128)}, u32[]{:S(2)}, u32[]{:S(2)}) collective-permute-start(f32[256,1024]{1,0:T(8,128)S(1)} %convert_element_type.112), channel_id=1, source_target_pairs={{0,1},{1,2},{2,3},{4,5},{5,6},{6,7},{8,9},{9,10},{10,11},{12,13},{... | collective-permute-start | bytes 3145736 | tf_op jit(solution)/shard_map/ppermute | solution.py:403
  36.5 43.6 %collective-permute-start.9 = (f32[256,1024]{1,0:T(8,128)S(1)}, f32[256,1024]{1,0:T(8,128)}, u32[]{:S(2)}, u32[]{:S(2)}) collective-permute-start(f32[256,1024]{1,0:T(8,128)S(1)} %convert_element_type.112), channel_id=1, source_target_pairs={{1,0},{2,1},{3,2},{5,4},{6,5},{7,6},{9,8},{10,9},{11,10},{13,12},{... | collective-permute-start | bytes 3145736 | tf_op jit(solution)/shard_map/ppermute | solution.py:404
  53.1 27.1 %copy-start.19 = (f32[1024,256]{1,0:T(8,128)}, f32[1024,256]{1,0:T(8,128)S(1)}, u32[]{:S(2)}) copy-start(f32[1024,256]{1,0:T(8,128)S(1)} %collective-permute-done) | copy-start | bytes 3145732
  53.1 28.4 %collective-permute-start.1 = (f32[1024,256]{1,0:T(8,128)S(1)}, f32[1024,256]{1,0:T(8,128)}, u32[]{:S(2)}, u32[]{:S(2)}) collective-permute-start(f32[1024,256]{1,0:T(8,128)S(1)} %collective-permute-done), channel_id=1, source_target_pairs={{1,2},{2,3},{5,6},{6,7},{9,10},{10,11},{13,14},{14,15},{17,18},{18... | collective-permute-start | bytes 3145736 | tf_op jit(solution)/shard_map/ppermute | solution.py:403
  57.7 44.9 %collective-permute-start.4 = (f32[1024,256]{1,0:T(8,128)}, f32[1024,256]{1,0:T(8,128)}, u32[]{:S(2)}, u32[]{:S(2)}) collective-permute-start(f32[1024,256]{1,0:T(8,128)} %collective-permute-done.3), channel_id=1, source_target_pairs={{1,0},{2,1},{5,4},{6,5},{9,8},{10,9},{13,12},{14,13},{17,16},{18,1... | collective-permute-start | bytes 3145736 | tf_op jit(solution)/shard_map/ppermute | solution.py:404
  74.4 29.5 %collective-permute-start.7 = (f32[256,1024]{1,0:T(8,128)}, f32[256,1024]{1,0:T(8,128)}, u32[]{:S(2)}, u32[]{:S(2)}) collective-permute-start(f32[256,1024]{1,0:T(8,128)} %collective-permute-done.6), channel_id=1, source_target_pairs={{1,2},{2,3},{5,6},{6,7},{9,10},{10,11},{13,14},{14,15},{17,18},{18... | collective-permute-start | bytes 3145736 | tf_op jit(solution)/shard_map/ppermute | solution.py:403
  80.1 44.9 %collective-permute-start.10 = (f32[256,1024]{1,0:T(8,128)}, f32[256,1024]{1,0:T(8,128)}, u32[]{:S(2)}, u32[]{:S(2)}) collective-permute-start(f32[256,1024]{1,0:T(8,128)} %collective-permute-done.9), channel_id=1, source_target_pairs={{1,0},{2,1},{5,4},{6,5},{9,8},{10,9},{13,12},{14,13},{17,16},{18,1... | collective-permute-start | bytes 3145736 | tf_op jit(solution)/shard_map/ppermute | solution.py:404
  81.4 45.1 %collective-permute-start.2 = (f32[1024,256]{1,0:T(8,128)}, f32[1024,256]{1,0:T(8,128)}, u32[]{:S(2)}, u32[]{:S(2)}) collective-permute-start(f32[1024,256]{1,0:T(8,128)} %collective-permute-done.1), channel_id=1, source_target_pairs={{2,3},{6,7},{10,11},{14,15},{18,19},{22,23},{26,27},{30,31}} | collective-permute-start | bytes 3145736 | tf_op jit(solution)/shard_map/ppermute | solution.py:403
  84.3 44.9 %copy-start.20 = (f32[1024,256]{1,0:T(8,128)S(1)}, f32[1024,256]{1,0:T(8,128)}, u32[]{:S(2)}) copy-start(f32[1024,256]{1,0:T(8,128)} %copy-done.19) | copy-start | bytes 3145732
  102.6 44.8 %collective-permute-start.5 = (f32[1024,256]{1,0:T(8,128)}, f32[1024,256]{1,0:T(8,128)S(1)}, u32[]{:S(2)}, u32[]{:S(2)}) collective-permute-start(f32[1024,256]{1,0:T(8,128)} %collective-permute-done.4), channel_id=1, source_target_pairs={{1,0},{5,4},{9,8},{13,12},{17,16},{21,20},{25,24},{29,28}} | collective-permute-start | bytes 3145736 | tf_op jit(solution)/shard_map/ppermute | solution.py:404
  103.9 44.0 %collective-permute-start.8 = (f32[256,1024]{1,0:T(8,128)}, f32[256,1024]{1,0:T(8,128)S(1)}, u32[]{:S(2)}, u32[]{:S(2)}) collective-permute-start(f32[256,1024]{1,0:T(8,128)} %collective-permute-done.7), channel_id=1, source_target_pairs={{2,3},{6,7},{10,11},{14,15},{18,19},{22,23},{26,27},{30,31}} | collective-permute-start | bytes 3145736 | tf_op jit(solution)/shard_map/ppermute | solution.py:403
  125.1 43.4 %collective-permute-start.11 = (f32[256,1024]{1,0:T(8,128)}, f32[256,1024]{1,0:T(8,128)S(1)}, u32[]{:S(2)}, u32[]{:S(2)}) collective-permute-start(f32[256,1024]{1,0:T(8,128)} %collective-permute-done.10), channel_id=1, source_target_pairs={{1,0},{5,4},{9,8},{13,12},{17,16},{21,20},{25,24},{29,28}} | collective-permute-start | bytes 3145736 | tf_op jit(solution)/shard_map/ppermute | solution.py:404
  147.9 21.3 %copy-start.5 = (bf16[1024,4,256]{2,0,1:T(8,128)(2,1)}, bf16[1024,4,256]{2,0,1:T(8,128)(2,1)S(1)}, u32[]{:S(2)}) copy-start(bf16[1024,4,256]{2,0,1:T(8,128)(2,1)S(1)} %fusion) | copy-start | bytes 6291460
  154.1 15.0 %copy-start.15 = (bf16[2,512,1024]{2,1,0:T(8,128)(2,1)S(1)}, bf16[2,512,1024]{2,1,0:T(8,128)(2,1)}, u32[]{:S(2)}) copy-start(bf16[2,512,1024]{2,1,0:T(8,128)(2,1)} %seg_ref.1) | copy-start | bytes 6291460
  174.1 12.9 %copy-start.29 = (f32[1024,1024]{1,0:T(8,128)}, f32[1024,1024]{1,0:T(8,128)S(1)}, u32[]{:S(2)}) copy-start(f32[1024,1024]{1,0:T(8,128)S(1)} %fusion.24) | copy-start | bytes 12582916
  183.1 10.2 %copy-start.2 = (f32[1024,1024]{1,0:T(8,128)}, f32[1024,1024]{1,0:T(8,128)S(1)}, u32[]{:S(2)}) copy-start(f32[1024,1024]{1,0:T(8,128)S(1)} %fusion.29) | copy-start | bytes 12582916
  184.5 25.4 %collective-permute-start.24 = (f32[256,1024]{1,0:T(8,128)}, f32[256,1024]{1,0:T(8,128)}, u32[]{:S(2)}, u32[]{:S(2)}) collective-permute-start(f32[256,1024]{1,0:T(8,128)} %get-tuple-element.81), channel_id=1, source_target_pairs={{0,1},{4,5},{8,9},{12,13},{16,17},{20,21},{24,25},{28,29}} | collective-permute-start | bytes 3145736 | tf_op jit(solution)/shard_map/ppermute | solution.py:425
  193.3 39.0 %collective-permute-start.12 = (f32[256,1024]{1,0:T(8,128)S(1)}, f32[256,1024]{1,0:T(8,128)}, u32[]{:S(2)}, u32[]{:S(2)}) collective-permute-start(f32[256,1024]{1,0:T(8,128)S(1)} %get-tuple-element.85), channel_id=1, source_target_pairs={{0,1},{4,5},{8,9},{12,13},{16,17},{20,21},{24,25},{28,29}} | collective-permute-start | bytes 3145736 | tf_op jit(solution)/shard_map/ppermute | solution.py:425
  196.0 43.4 %collective-permute-start.27 = (f32[256,1024]{1,0:T(8,128)S(1)}, f32[256,1024]{1,0:T(8,128)}, u32[]{:S(2)}, u32[]{:S(2)}) collective-permute-start(f32[256,1024]{1,0:T(8,128)S(1)} %get-tuple-element.82), channel_id=1, source_target_pairs={{3,2},{7,6},{11,10},{15,14},{19,18},{23,22},{27,26},{31,30}} | collective-permute-start | bytes 3145736 | tf_op jit(solution)/shard_map/ppermute | solution.py:426
  212.6 42.2 %collective-permute-start.25 = (f32[256,1024]{1,0:T(8,128)}, f32[256,1024]{1,0:T(8,128)}, u32[]{:S(2)}, u32[]{:S(2)}) collective-permute-start(f32[256,1024]{1,0:T(8,128)} %bitcast_add_fusion.8), channel_id=1, source_target_pairs={{0,1},{1,2},{4,5},{5,6},{8,9},{9,10},{12,13},{13,14},{16,17},{17,1... | collective-permute-start | bytes 3145736 | tf_op jit(solution)/shard_map/ppermute | solution.py:425
  218.0 42.6 %collective-permute-start.15 = (f32[256,1024]{1,0:T(8,128)S(1)}, f32[256,1024]{1,0:T(8,128)}, u32[]{:S(2)}, u32[]{:S(2)}) collective-permute-start(f32[256,1024]{1,0:T(8,128)S(1)} %get-tuple-element.86), channel_id=1, source_target_pairs={{3,2},{7,6},{11,10},{15,14},{19,18},{23,22},{27,26},{31,30}} | collective-permute-start | bytes 3145736 | tf_op jit(solution)/shard_map/ppermute | solution.py:426
  234.0 40.9 %collective-permute-start.13 = (f32[256,1024]{1,0:T(8,128)S(1)}, f32[256,1024]{1,0:T(8,128)}, u32[]{:S(2)}, u32[]{:S(2)}) collective-permute-start(f32[256,1024]{1,0:T(8,128)S(1)} %bitcast_add_fusion.13), channel_id=1, source_target_pairs={{0,1},{1,2},{4,5},{5,6},{8,9},{9,10},{12,13},{13,14},{16,17},{17,1... | collective-permute-start | bytes 3145736 | tf_op jit(solution)/shard_map/ppermute | solution.py:425
  258.9 26.9 %collective-permute-start.28 = (f32[256,1024]{1,0:T(8,128)}, f32[256,1024]{1,0:T(8,128)}, u32[]{:S(2)}, u32[]{:S(2)}) collective-permute-start(f32[256,1024]{1,0:T(8,128)} %get-tuple-element.80), channel_id=1, source_target_pairs={{3,2},{2,1},{7,6},{6,5},{11,10},{10,9},{15,14},{14,13},{19,18},{18... | collective-permute-start | bytes 3145736 | tf_op jit(solution)/shard_map/ppermute | solution.py:426
  278.9 19.5 %copy-start.6 = (bf16[1024,4,256]{2,0,1:T(8,128)(2,1)S(1)}, bf16[1024,4,256]{2,0,1:T(8,128)(2,1)}, u32[]{:S(2)}) copy-start(bf16[1024,4,256]{2,0,1:T(8,128)(2,1)} %copy-done.5) | copy-start | bytes 6291460
  278.9 15.5 %collective-permute-start.16 = (f32[256,1024]{1,0:T(8,128)}, f32[256,1024]{1,0:T(8,128)}, u32[]{:S(2)}, u32[]{:S(2)}) collective-permute-start(f32[256,1024]{1,0:T(8,128)} %get-tuple-element.84), channel_id=1, source_target_pairs={{3,2},{2,1},{7,6},{6,5},{11,10},{10,9},{15,14},{14,13},{19,18},{18... | collective-permute-start | bytes 3145736 | tf_op jit(solution)/shard_map/ppermute | solution.py:426
  280.6 28.1 %collective-permute-start.26 = (f32[256,1024]{1,0:T(8,128)}, f32[256,1024]{1,0:T(8,128)}, u32[]{:S(2)}, u32[]{:S(2)}) collective-permute-start(f32[256,1024]{1,0:T(8,128)} %get-tuple-element.79), channel_id=1, source_target_pairs={{0,1},{1,2},{2,3},{4,5},{5,6},{6,7},{8,9},{9,10},{10,11},{12,13},{... | collective-permute-start | bytes 3145736 | tf_op jit(solution)/shard_map/ppermute | solution.py:425
  288.5 28.3 %collective-permute-start.29 = (f32[256,1024]{1,0:T(8,128)}, f32[256,1024]{1,0:T(8,128)}, u32[]{:S(2)}, u32[]{:S(2)}) collective-permute-start(f32[256,1024]{1,0:T(8,128)} %bitcast_add_fusion.7), channel_id=1, source_target_pairs={{3,2},{2,1},{1,0},{7,6},{6,5},{5,4},{11,10},{10,9},{9,8},{15,14},{... | collective-permute-start | bytes 3145736 | tf_op jit(solution)/shard_map/ppermute | solution.py:426
  289.8 38.1 %collective-permute-start.14 = (f32[256,1024]{1,0:T(8,128)}, f32[256,1024]{1,0:T(8,128)S(1)}, u32[]{:S(2)}, u32[]{:S(2)}) collective-permute-start(f32[256,1024]{1,0:T(8,128)} %get-tuple-element.83), channel_id=1, source_target_pairs={{0,1},{1,2},{2,3},{4,5},{5,6},{6,7},{8,9},{9,10},{10,11},{12,13},{... | collective-permute-start | bytes 3145736 | tf_op jit(solution)/shard_map/ppermute | solution.py:425
  297.1 38.5 %collective-permute-start.17 = (f32[256,1024]{1,0:T(8,128)}, f32[256,1024]{1,0:T(8,128)}, u32[]{:S(2)}, u32[]{:S(2)}) collective-permute-start(f32[256,1024]{1,0:T(8,128)} %bitcast_add_fusion.12), channel_id=1, source_target_pairs={{3,2},{2,1},{1,0},{7,6},{6,5},{5,4},{11,10},{10,9},{9,8},{15,14},{... | collective-permute-start | bytes 3145736 | tf_op jit(solution)/shard_map/ppermute | solution.py:426
  343.7 18.2 %copy-start.18 = (f32[2,2,512,1]{3,2,1,0:T(8,128)S(1)}, f32[2,2,512,1]{3,2,1,0:T(8,128)}, u32[]{:S(2)}) copy-start(f32[2,2,512,1]{3,2,1,0:T(8,128)} %get-tuple-element.29) | copy-start | bytes 24580
  344.8 68.0 %all-to-all-start = ((f32[4,256,256]{2,1,0:T(8,128)}), f32[4,256,256]{2,1,0:T(8,128)S(1)}, u32[]{:S(2)}, u32[]{:S(2)}) async-start(f32[4,256,256]{2,1,0:T(8,128)} %bitcast.157), calls=%async_computation | async-start | bytes 2097152 | tf_op jit(solution)/shard_map/all_to_all | solution.py:517
  361.9 392.7 %all-reduce.3.cloned.1.call-start = ((), (), s32[]{:S(2)}) async-start(), calls=%async_computation.3 | async-start | bytes 29360128 | tf_op jit(solution)/shard_map/psum | solution.py:560
  437.3 36.5 %copy-start.28 = (s32[2]{0:T(128)S(1)}, s32[2]{0:T(128)}, u32[]{:S(2)}) copy-start(s32[2]{0:T(128)} %memory_fill.3) | copy-start | bytes 28
  437.3 36.6 %copy-start.14 = (bf16[2,512,1024]{2,1,0:T(8,128)(2,1)S(1)}, bf16[2,512,1024]{2,1,0:T(8,128)(2,1)}, u32[]{:S(2)}) copy-start(bf16[2,512,1024]{2,1,0:T(8,128)(2,1)} %memory_ref.1) | copy-start | bytes 6291460
  440.2 25.9 %collective-permute-start.30 = (f32[256,1024]{1,0:T(8,128)S(1)}, f32[256,1024]{1,0:T(8,128)S(1)}, u32[]{:S(2)}, u32[]{:S(2)}) collective-permute-start(f32[256,1024]{1,0:T(8,128)S(1)} %get-tuple-element.75), channel_id=1, source_target_pairs={{0,1},{4,5},{8,9},{12,13},{16,17},{20,21},{24,25},{28,29}} | collective-permute-start | bytes 3145736 | tf_op jit(solution)/shard_map/ppermute | solution.py:425
  441.9 36.3 %collective-permute-start.33 = (f32[256,1024]{1,0:T(8,128)}, f32[256,1024]{1,0:T(8,128)}, u32[]{:S(2)}, u32[]{:S(2)}) collective-permute-start(f32[256,1024]{1,0:T(8,128)} %get-tuple-element.76), channel_id=1, source_target_pairs={{3,2},{7,6},{11,10},{15,14},{19,18},{23,22},{27,26},{31,30}} | collective-permute-start | bytes 3145736 | tf_op jit(solution)/shard_map/ppermute | solution.py:426
  468.5 25.0 %collective-permute-start.31 = (f32[256,1024]{1,0:T(8,128)}, f32[256,1024]{1,0:T(8,128)}, u32[]{:S(2)}, u32[]{:S(2)}) collective-permute-start(f32[256,1024]{1,0:T(8,128)} %bitcast_add_fusion.3), channel_id=1, source_target_pairs={{0,1},{1,2},{4,5},{5,6},{8,9},{9,10},{12,13},{13,14},{16,17},{17,1... | collective-permute-start | bytes 3145736 | tf_op jit(solution)/shard_map/ppermute | solution.py:425
  478.1 20.0 %copy-start.21 = (bf16[2,256,256]{2,1,0:T(8,128)(2,1)S(1)}, bf16[2,256,256]{2,1,0:T(8,128)(2,1)}, u32[]{:S(2)}) copy-start(bf16[2,256,256]{2,1,0:T(8,128)(2,1)} %param.33) | copy-start | bytes 786436
  497.1 18.5 %collective-permute-start.34 = (f32[256,1024]{1,0:T(8,128)S(1)}, f32[256,1024]{1,0:T(8,128)S(1)}, u32[]{:S(2)}, u32[]{:S(2)}) collective-permute-start(f32[256,1024]{1,0:T(8,128)S(1)} %get-tuple-element.74), channel_id=1, source_target_pairs={{3,2},{2,1},{7,6},{6,5},{11,10},{10,9},{15,14},{14,13},{19,18},{18... | collective-permute-start | bytes 3145736 | tf_op jit(solution)/shard_map/ppermute | solution.py:426
  500.2 19.1 %copy-start.17 = (f32[1024,1024]{1,0:T(8,128)S(1)}, f32[1024,1024]{1,0:T(8,128)}, u32[]{:S(2)}) copy-start(f32[1024,1024]{1,0:T(8,128)} %copy-done.16) | copy-start | bytes 12582916
  500.2 19.1 %copy-start.32 = (bf16[1024,1024]{1,0:T(8,128)(2,1)S(1)}, bf16[1024,1024]{1,0:T(8,128)(2,1)}, u32[]{:S(2)}) copy-start(bf16[1024,1024]{1,0:T(8,128)(2,1)} %copy-done.31) | copy-start | bytes 6291460
  505.0 29.0 %collective-permute-start.18 = (f32[256,1024]{1,0:T(8,128)}, f32[256,1024]{1,0:T(8,128)}, u32[]{:S(2)}, u32[]{:S(2)}) collective-permute-start(f32[256,1024]{1,0:T(8,128)} %get-tuple-element.78), channel_id=1, source_target_pairs={{0,1},{1,2},{2,3},{4,5},{5,6},{6,7},{8,9},{9,10},{10,11},{12,13},{... | collective-permute-start | bytes 3145736 | tf_op jit(solution)/shard_map/ppermute | solution.py:403
  511.1 41.2 %collective-permute-start.32 = (f32[256,1024]{1,0:T(8,128)}, f32[256,1024]{1,0:T(8,128)}, u32[]{:S(2)}, u32[]{:S(2)}) collective-permute-start(f32[256,1024]{1,0:T(8,128)} %get-tuple-element.73), channel_id=1, source_target_pairs={{0,1},{1,2},{2,3},{4,5},{5,6},{6,7},{8,9},{9,10},{10,11},{12,13},{... | collective-permute-start | bytes 3145736 | tf_op jit(solution)/shard_map/ppermute | solution.py:425
  518.0 34.3 %collective-permute-start.35 = (f32[256,1024]{1,0:T(8,128)}, f32[256,1024]{1,0:T(8,128)}, u32[]{:S(2)}, u32[]{:S(2)}) collective-permute-start(f32[256,1024]{1,0:T(8,128)} %bitcast_add_fusion.2), channel_id=1, source_target_pairs={{3,2},{2,1},{1,0},{7,6},{6,5},{5,4},{11,10},{10,9},{9,8},{15,14},{... | collective-permute-start | bytes 3145736 | tf_op jit(solution)/shard_map/ppermute | solution.py:426
  525.2 44.9 %collective-permute-start.21 = (f32[256,1024]{1,0:T(8,128)}, f32[256,1024]{1,0:T(8,128)}, u32[]{:S(2)}, u32[]{:S(2)}) collective-permute-start(f32[256,1024]{1,0:T(8,128)} %get-tuple-element.78), channel_id=1, source_target_pairs={{1,0},{2,1},{3,2},{5,4},{6,5},{7,6},{9,8},{10,9},{11,10},{13,12},{... | collective-permute-start | bytes 3145736 | tf_op jit(solution)/shard_map/ppermute | solution.py:404
  534.0 37.3 %collective-permute-start.19 = (f32[256,1024]{1,0:T(8,128)}, f32[256,1024]{1,0:T(8,128)}, u32[]{:S(2)}, u32[]{:S(2)}) collective-permute-start(f32[256,1024]{1,0:T(8,128)} %collective-permute-done.18), channel_id=1, source_target_pairs={{1,2},{2,3},{5,6},{6,7},{9,10},{10,11},{13,14},{14,15},{17,18},{18... | collective-permute-start | bytes 3145736 | tf_op jit(solution)/shard_map/ppermute | solution.py:403
  557.1 108.6 %copy-start.24 = (f32[2,24,128]{2,1,0:T(8,128)S(1)}, f32[2,24,128]{2,1,0:T(8,128)}, u32[]{:S(2)}) copy-start(f32[2,24,128]{2,1,0:T(8,128)} %get-tuple-element.34) | copy-start | bytes 73732
  557.1 23.4 %collective-permute-start.36 = (f32[256,1024]{1,0:T(8,128)}, f32[256,1024]{1,0:T(8,128)S(1)}, u32[]{:S(2)}, u32[]{:S(2)}) collective-permute-start(f32[256,1024]{1,0:T(8,128)} %fusion.17), channel_id=1, source_target_pairs={{0,1},{1,2},{2,3},{4,5},{5,6},{6,7},{8,9},{9,10},{10,11},{12,13},{... | collective-permute-start | bytes 3145736 | tf_op jit(solution)/shard_map/ppermute | solution.py:403
  570.0 109.7 %collective-permute-start.22 = (f32[256,1024]{1,0:T(8,128)}, f32[256,1024]{1,0:T(8,128)}, u32[]{:S(2)}, u32[]{:S(2)}) collective-permute-start(f32[256,1024]{1,0:T(8,128)} %collective-permute-done.21), channel_id=1, source_target_pairs={{1,0},{2,1},{5,4},{6,5},{9,8},{10,9},{13,12},{14,13},{17,16},{18,1... | collective-permute-start | bytes 3145736 | tf_op jit(solution)/shard_map/ppermute | solution.py:404
  571.3 109.7 %collective-permute-start.20 = (f32[256,1024]{1,0:T(8,128)}, f32[256,1024]{1,0:T(8,128)}, u32[]{:S(2)}, u32[]{:S(2)}) collective-permute-start(f32[256,1024]{1,0:T(8,128)} %collective-permute-done.19), channel_id=1, source_target_pairs={{2,3},{6,7},{10,11},{14,15},{18,19},{22,23},{26,27},{30,31}} | collective-permute-start | bytes 3145736 | tf_op jit(solution)/shard_map/ppermute | solution.py:403
  579.2 105.8 %collective-permute-start.39 = (f32[256,1024]{1,0:T(8,128)}, f32[256,1024]{1,0:T(8,128)}, u32[]{:S(2)}, u32[]{:S(2)}) collective-permute-start(f32[256,1024]{1,0:T(8,128)} %fusion.17), channel_id=1, source_target_pairs={{1,0},{2,1},{3,2},{5,4},{6,5},{7,6},{9,8},{10,9},{11,10},{13,12},{... | collective-permute-start | bytes 3145736 | tf_op jit(solution)/shard_map/ppermute | solution.py:404
  580.5 105.8 %collective-permute-start.37 = (f32[256,1024]{1,0:T(8,128)S(1)}, f32[256,1024]{1,0:T(8,128)}, u32[]{:S(2)}, u32[]{:S(2)}) collective-permute-start(f32[256,1024]{1,0:T(8,128)S(1)} %collective-permute-done.36), channel_id=1, source_target_pairs={{1,2},{2,3},{5,6},{6,7},{9,10},{10,11},{13,14},{14,15},{17,18},{18... | collective-permute-start | bytes 3145736 | tf_op jit(solution)/shard_map/ppermute | solution.py:403
  679.7 28.2 %collective-permute-start.23 = (f32[256,1024]{1,0:T(8,128)}, f32[256,1024]{1,0:T(8,128)S(1)}, u32[]{:S(2)}, u32[]{:S(2)}) collective-permute-start(f32[256,1024]{1,0:T(8,128)} %collective-permute-done.22), channel_id=1, source_target_pairs={{1,0},{5,4},{9,8},{13,12},{17,16},{21,20},{25,24},{29,28}} | collective-permute-start | bytes 3145736 | tf_op jit(solution)/shard_map/ppermute | solution.py:404
  684.9 43.0 %collective-permute-start.40 = (f32[256,1024]{1,0:T(8,128)}, f32[256,1024]{1,0:T(8,128)S(1)}, u32[]{:S(2)}, u32[]{:S(2)}) collective-permute-start(f32[256,1024]{1,0:T(8,128)} %collective-permute-done.39), channel_id=1, source_target_pairs={{1,0},{2,1},{5,4},{6,5},{9,8},{10,9},{13,12},{14,13},{17,16},{18,1... | collective-permute-start | bytes 3145736 | tf_op jit(solution)/shard_map/ppermute | solution.py:404
  686.3 43.2 %collective-permute-start.38 = (f32[256,1024]{1,0:T(8,128)}, f32[256,1024]{1,0:T(8,128)S(1)}, u32[]{:S(2)}, u32[]{:S(2)}) collective-permute-start(f32[256,1024]{1,0:T(8,128)} %collective-permute-done.37), channel_id=1, source_target_pairs={{2,3},{6,7},{10,11},{14,15},{18,19},{22,23},{26,27},{30,31}} | collective-permute-start | bytes 3145736 | tf_op jit(solution)/shard_map/ppermute | solution.py:403
  728.0 24.7 %collective-permute-start.41 = (f32[256,1024]{1,0:T(8,128)S(1)}, f32[256,1024]{1,0:T(8,128)S(1)}, u32[]{:S(2)}, u32[]{:S(2)}) collective-permute-start(f32[256,1024]{1,0:T(8,128)S(1)} %collective-permute-done.40), channel_id=1, source_target_pairs={{1,0},{5,4},{9,8},{13,12},{17,16},{21,20},{25,24},{29,28}} | collective-permute-start | bytes 3145736 | tf_op jit(solution)/shard_map/ppermute | solution.py:404
  754.7 6.5 copy-start.9
  754.7 6.5 copy-start.10
  (14 other events, 48.9 us)
Sparse Core Ops, SparseCore 0:
  343.1 107.1 reduce-scatter.1
  524.1 207.6 all-reduce.2

commit v2 on v1

--- a/solution.py
+++ b/solution.py
@@ -13,6 +13,7 @@
 masked_score = -1e30
 block = 128
 query_block = 256
+chunk_count = 8
 f32 = jnp.float32
 bf16 = jnp.bfloat16
 
@@ -395,36 +396,907 @@
     )
 
 
-def line_gather(shard, size):
-    me = lax.axis_index("mp")
-    to_right = to_left = shard
-    from_left, from_right = [], []
-    for step in range(1, size):
-        to_right = lax.ppermute(to_right, "mp", [(i, i + 1) for i in range(step - 1, size - 1)])
-        to_left = lax.ppermute(to_left, "mp", [(i, i - 1) for i in range(1, size - step + 1)])
-        from_left.append(to_right)
-        from_right.append(to_left)
-    ordered = jnp.stack(from_left[::-1] + [shard] + from_right)
-    return lax.dynamic_slice_in_dim(ordered, size - 1 - me, size, 0)
-
-
-def line_scatter(parts, size):
-    me = lax.axis_index("mp")
-
-    def pick(index):
-        return lax.dynamic_index_in_dim(parts, jnp.clip(index, 0, size - 1), 0, keepdims=False)
-
-    from_left = from_right = None
-    for step in range(size - 1):
-        rightward = pick(size - 1 - (step - me))
-        leftward = pick(step - (size - 1 - me))
-        if step:
-            rightward = rightward + from_left
-            leftward = leftward + from_right
-        pairs = [(i, i + 1) for i in range(size - 1) if step >= i and size - 1 - (step - i) > i]
-        from_left = lax.ppermute(rightward, "mp", pairs)
-        from_right = lax.ppermute(leftward, "mp", [(size - 1 - a, size - 1 - b) for a, b in pairs])
-    return pick(me) + from_left + from_right
+def remote(source, target, send_sems, recv_sems, source_slot, target_slot, send_slot, recv_slot, peer):
+    return pltpu.make_async_remote_copy(
+        src_ref=source.at[source_slot],
+        dst_ref=target.at[target_slot],
+        send_sem=send_sems.at[send_slot],
+        recv_sem=recv_sems.at[recv_slot],
+        device_id=peer,
+        device_id_type=pl.DeviceIdType.MESH,
+    )
+
+
+class Line:
+    def __init__(self, size, chunks, hop):
+        self.me = lax.axis_index("mp")
+        self.size, self.chunks, self.hop = size, chunks, hop
+        self.reach = size - 1
+
+    def place(self, right):
+        return self.me if right else self.reach - self.me
+
+    def peer(self, right):
+        return {"mp": self.me + 1 if right else self.me - 1}
+
+    def copy(self, source, target, sems, slot, right):
+        return remote(source, target, sems[0], sems[1], slot, slot, slot, slot, self.peer(right))
+
+    def chunk_at(self, tick):
+        positive = jnp.maximum(tick, 0)
+        chunk = positive // self.reach
+        return chunk, (tick >= 0) & (positive == chunk * self.reach) & (chunk < self.chunks)
+
+    def scatter_step(self, tick, part, lanes):
+        for right, held, sems in lanes:
+            place = self.place(right)
+            late = tick - self.hop * place
+            positive = jnp.maximum(late, 0)
+            chunk = positive // self.reach
+            goal = self.reach - (positive - self.reach * chunk)
+            active = (late >= 0) & (chunk < self.chunks) & (goal > place)
+            slot = chunk * self.size + (goal if right else self.reach - goal)
+
+            @pl.when(active & (place == 0))
+            def _():
+                self.copy(part, held, sems, slot, right).start()
+
+            @pl.when(active & (place > 0))
+            def _():
+                self.copy(held, held, sems, slot, right).wait_recv()
+                held[slot] = held[slot] + part[slot]
+                self.copy(held, held, sems, slot, right).start()
+
+    def scatter_sum(self, chunk, part, lanes, total):
+        slot = chunk * self.size + self.me
+        total[...] = part[slot]
+        for right, held, sems in lanes:
+
+            @pl.when(self.place(right) > 0)
+            def _():
+                self.copy(held, held, sems, slot, right).wait_recv()
+                total[...] = total[...] + held[slot]
+
+    def gather_start(self, chunk, whole, lanes):
+        slot = chunk * self.size + self.me
+        for right, sems in lanes:
+
+            @pl.when(self.place(right) < self.reach)
+            def _():
+                self.copy(whole, whole, sems, slot, right).start()
+
+    def gather_step(self, tick, whole, lanes, landed=None):
+        for right, sems in lanes:
+            place = self.place(right)
+            for distance in range(1, self.size):
+                chunk, due = self.chunk_at(tick - self.hop * distance)
+
+                @pl.when(due & (distance <= place))
+                def _():
+                    slot = chunk * self.size + (self.me - distance if right else self.me + distance)
+                    self.copy(whole, whole, sems, slot, right).wait_recv()
+
+                    @pl.when(place < self.reach)
+                    def _():
+                        self.copy(whole, whole, sems, slot, right).start()
+
+                    if landed is not None:
+                        landed(slot)
+
+    def scatter_drain(self, chunk, part, lanes):
+        for right, held, sems in lanes:
+            for goal in range(1, self.size):
+
+                @pl.when(goal > self.place(right))
+                def _():
+                    slot = chunk * self.size + (goal if right else self.reach - goal)
+                    self.copy(part, held, sems, slot, right).wait_send()
+
+    def gather_drain(self, chunk, whole, lanes):
+        for right, sems in lanes:
+            place = self.place(right)
+            for distance in range(self.size):
+
+                @pl.when((distance <= place) & (place < self.reach))
+                def _():
+                    slot = chunk * self.size + (self.me - distance if right else self.me + distance)
+                    self.copy(whole, whole, sems, slot, right).wait_send()
+
+
+def greet(peers):
+    barrier = pltpu.get_barrier_semaphore()
+    for peer in peers:
+        pl.semaphore_signal(barrier, inc=1, device_id=peer, device_id_type=pl.DeviceIdType.MESH)
+    pl.semaphore_wait(barrier, len(peers))
+
+
+def feed_kernel(
+    size,
+    group,
+    chunks,
+    hop,
+    delay,
+    stages,
+    mixed_ref,
+    seg_ref,
+    grad_ref,
+    up_ref,
+    down_ref,
+    out_ref,
+    gain_ref,
+    gm_ref,
+    gres_ref,
+    res_ref,
+    branch_ref,
+    gdown_ref,
+    gup_ref,
+    gout_ref,
+    gsecond_ref,
+    heads_in,
+    part,
+    held_right,
+    held_left,
+    swap_out,
+    swap_in,
+    weights_in,
+    weights,
+    chunk_rows,
+    total,
+    own_mixed,
+    own_grad,
+    *sems,
+):
+    line = Line(size, chunks, hop)
+    me = line.me
+    mine = lax.axis_index("dp")
+    (hr_s, hr_r, hl_s, hl_r, sr_s, sr_r, sl_s, sl_r, x_s, x_r, wz_s, wz_r, wd_s, wd_r) = sems
+    gather_lanes = ((True, (hr_s, hr_r)), (False, (hl_s, hl_r)))
+    scatter_lanes = ((True, held_right, (sr_s, sr_r)), (False, held_left, (sl_s, sl_r)))
+    bits = group.bit_length() - 1
+    piece, width = weights_in.shape[2:]
+    rows = total.shape[0]
+    local = mixed_ref.shape[-1]
+    spot = jnp.int32(0)
+    for bit in range(bits):
+        spot = spot + ((mine // (1 << bit)) % 2) * (1 << (bits - 1 - bit))
+
+    def others(offset):
+        return {"mp": lax.rem(me + offset, size)}
+
+    def partner(level):
+        step = 1 << (bits - 1 - level)
+        return {"dp": mine + step - 2 * step * ((mine // step) % 2)}
+
+    greet([others(offset) for offset in range(1, size)] + [partner(level) for level in range(bits)])
+
+    weights_in[spot, me] = out_ref[pl.ds(pl.multiple_of(mine * piece, piece), piece), :].astype(f32)
+
+    def weight_across(offset, arriving):
+        origin = lax.rem(me - offset + size, size) if arriving else me
+        return pltpu.make_async_remote_copy(
+            src_ref=weights_in.at[spot, origin],
+            dst_ref=weights_in.at[spot, origin],
+            send_sem=wz_s.at[offset],
+            recv_sem=wz_r.at[offset],
+            device_id=others(offset),
+            device_id_type=pl.DeviceIdType.MESH,
+        )
+
+    def weight_within(level, arriving):
+        count = 1 << level
+        start = (spot // count) * count
+        if arriving:
+            start = start + count - 2 * count * ((spot // count) % 2)
+        return pltpu.make_async_remote_copy(
+            src_ref=weights_in.at[pl.ds(start, count)],
+            dst_ref=weights_in.at[pl.ds(start, count)],
+            send_sem=wd_s.at[level],
+            recv_sem=wd_r.at[level],
+            device_id=partner(level),
+            device_id_type=pl.DeviceIdType.MESH,
+        )
+
+    for offset in range(1, size):
+        weight_across(offset, False).start()
+
+    def stage_heads(chunk, _):
+        heads_in[chunk * size + me] = mixed_ref[chunk].astype(f32)
+        return 0
+
+    lax.fori_loop(0, chunks, stage_heads, 0)
+    gsecond_ref[...] = jnp.zeros_like(gsecond_ref)
+    gdown_ref[...] = jnp.zeros_like(gdown_ref)
+    gup_ref[...] = jnp.zeros_like(gup_ref)
+
+    def weight_step(tick):
+        @pl.when(tick == stages[0])
+        def _():
+            for offset in range(1, size):
+                weight_across(offset, True).wait_recv()
+            weight_within(0, False).start()
+
+        for level in range(1, bits):
+
+            @pl.when(tick == stages[min(level, len(stages) - 1)] + max(0, level - len(stages) + 1))
+            def _():
+                weight_within(level - 1, True).wait_recv()
+                weight_within(level, False).start()
+
+    def weight_finish():
+        weight_within(bits - 1, True).wait_recv()
+        for index in range(size):
+            pieces = []
+            for member in range(group):
+                place = sum(((member >> bit) & 1) << (bits - 1 - bit) for bit in range(bits))
+                pieces.append(weights_in[place, index])
+            weights[index * group * piece : (index + 1) * group * piece, :] = jnp.concatenate(
+                pieces, axis=0
+            ).astype(bf16)
+
+    own = pl.ds(pl.multiple_of(me * rows, rows), rows)
+
+    def feed_chunk(chunk):
+        heads = [heads_in[chunk * size + index].astype(bf16) for index in range(size)]
+        for index in range(size):
+            own_mixed[chunk, :, index * local : (index + 1) * local] = heads_in[
+                chunk * size + index, own, :
+            ].astype(bf16)
+        residual = seg_ref[chunk].astype(f32) + mm(jnp.concatenate(heads, axis=1), weights[...])
+        chunk_rows[...] = residual
+        res_ref[chunk] = chunk_rows[own, :]
+        ffn_input = (residual * row_scale(residual) * gain_ref[...]).astype(bf16)
+        pre_act = mm(ffn_input, up_ref[...])
+        inner = math.sqrt(2.0 / math.pi)
+        squared = pre_act * pre_act
+        tanh = jnp.tanh(inner * (pre_act + 0.044715 * pre_act * squared))
+        activated = (0.5 * pre_act * (1.0 + tanh)).astype(bf16)
+        slope = 0.5 * (1.0 + tanh) + 0.5 * pre_act * (1.0 - tanh * tanh) * (
+            inner * (1.0 + 3.0 * 0.044715 * squared)
+        )
+        grads = grad_ref[chunk]
+        grad_pre = (slope * mm_t1(grads, down_ref[...])).astype(bf16)
+        first = pl.ds(chunk * size, size)
+        part[first] = mm_t1(grad_pre, up_ref[...]).reshape(size, rows, width)
+        branch_ref[first] = mm(activated, down_ref[...]).reshape(size, rows, width)
+        gdown_ref[...] += mm_t0(activated, grads)
+        gup_ref[...] += mm_t0(ffn_input, grad_pre)
+
+    def swap(chunk, offset, arriving):
+        target = lax.rem(me + offset, size)
+        origin = lax.rem(me - offset + size, size)
+        landing = chunk * size + (origin if arriving else me)
+        return remote(
+            swap_out,
+            swap_in,
+            x_s,
+            x_r,
+            chunk * size + target,
+            landing,
+            chunk * size + target,
+            landing,
+            {"mp": target},
+        )
+
+    def settle(chunk):
+        line.scatter_sum(chunk, part, scatter_lanes, total)
+        grad_ffn = total[...]
+        residual = res_ref[chunk]
+        scale = row_scale(residual)
+        normed = residual * scale
+        gsecond_ref[...] += jnp.sum(grad_ffn * normed, axis=0, keepdims=True)
+        weighted = grad_ffn * gain_ref[...]
+        own_rows = grad_ref[chunk, own, :].astype(f32)
+        grad_residual = own_rows + scale * (
+            weighted - normed * jnp.mean(weighted * normed, axis=-1, keepdims=True)
+        )
+        gres_ref[chunk] = grad_residual
+        low = grad_residual.astype(bf16)
+        own_grad[chunk] = low
+        grad_mixed = mm_t1(low, weights[...]).astype(bf16).astype(f32)
+        for index in range(size):
+            swap_out[chunk * size + index] = grad_mixed[:, index * local : (index + 1) * local]
+        for offset in range(1, size):
+            swap(chunk, offset, False).start()
+
+    feed_at = hop * line.reach + delay
+
+    def step(tick, _):
+        weight_step(tick)
+
+        @pl.when(tick == feed_at)
+        def _():
+            weight_finish()
+
+        chunk, due = line.chunk_at(tick)
+
+        @pl.when(due)
+        def _():
+            line.gather_start(chunk, heads_in, gather_lanes)
+
+        line.gather_step(tick, heads_in, gather_lanes)
+        chunk_f, due_f = line.chunk_at(tick - feed_at)
+
+        @pl.when(due_f)
+        def _():
+            feed_chunk(chunk_f)
+
+        line.scatter_step(tick - feed_at, part, scatter_lanes)
+        chunk_s, due_s = line.chunk_at(tick - feed_at - hop * line.reach)
+
+        @pl.when(due_s)
+        def _():
+            settle(chunk_s)
+
+        return 0
+
+    lax.fori_loop(0, feed_at + line.reach * (chunks - 1) + hop * line.reach + 1, step, 0)
+    gout_ref[...] = mm_t0(
+        own_mixed[...].reshape(chunks * rows, width), own_grad[...].reshape(chunks * rows, width)
+    )
+
+    def finish(chunk, _):
+        for offset in range(1, size):
+            swap(chunk, offset, True).wait_recv()
+        for index in range(size):
+
+            @pl.when(index == me)
+            def _():
+                gm_ref[chunk * size + index] = swap_out[chunk * size + index].astype(bf16)
+
+            @pl.when(index != me)
+            def _():
+                gm_ref[chunk * size + index] = swap_in[chunk * size + index].astype(bf16)
+
+        line.gather_drain(chunk, heads_in, gather_lanes)
+        line.scatter_drain(chunk, part, scatter_lanes)
+        for offset in range(1, size):
+            swap(chunk, offset, False).wait_send()
+        return 0
+
+    lax.fori_loop(0, chunks, finish, 0)
+    for offset in range(1, size):
+        weight_across(offset, False).wait_send()
+    for level in range(bits):
+        weight_within(level, False).wait_send()
+
+
+def feed(mixed, seg_rows, grad_rows, up, down, out, gain, size, group, chunks):
+    rows, width = seg_rows.shape
+    local = mixed.shape[1]
+    chunk = rows // chunks
+    piece = chunk // size
+    hidden = up.shape[1]
+    vmem = pl.BlockSpec(memory_space=pltpu.VMEM)
+    slots = pltpu.SemaphoreType.DMA((chunks * size,))
+    bits = group.bit_length() - 1
+    return pl.pallas_call(
+        functools.partial(feed_kernel, size, group, chunks, 2, 10, (3, 6, 10)),
+        in_specs=[vmem] * 7,
+        out_specs=[vmem] * 8,
+        out_shape=[
+            jax.ShapeDtypeStruct((chunks * size, piece, local), bf16),
+            jax.ShapeDtypeStruct((chunks, piece, width), f32),
+            jax.ShapeDtypeStruct((chunks, piece, width), f32),
+            jax.ShapeDtypeStruct((chunks * size, piece, width), f32),
+            jax.ShapeDtypeStruct((hidden, width), f32),
+            jax.ShapeDtypeStruct((width, hidden), f32),
+            jax.ShapeDtypeStruct((width, width), f32),
+            jax.ShapeDtypeStruct((1, width), f32),
+        ],
+        scratch_shapes=[
+            pltpu.VMEM((chunks * size, chunk, local), f32),
+            pltpu.VMEM((chunks * size, piece, width), f32),
+            pltpu.VMEM((chunks * size, piece, width), f32),
+            pltpu.VMEM((chunks * size, piece, width), f32),
+            pltpu.VMEM((chunks * size, piece, local), f32),
+            pltpu.VMEM((chunks * size, piece, local), f32),
+            pltpu.VMEM((group, size, out.shape[0] // group, width), f32),
+            pltpu.VMEM((width, width), bf16),
+            pltpu.VMEM((chunk, width), f32),
+            pltpu.VMEM((piece, width), f32),
+            pltpu.VMEM((chunks, piece, width), bf16),
+            pltpu.VMEM((chunks, piece, width), bf16),
+        ]
+        + [slots] * 10
+        + [pltpu.SemaphoreType.DMA((size,))] * 2
+        + [pltpu.SemaphoreType.DMA((bits,))] * 2,
+        compiler_params=pltpu.CompilerParams(
+            collective_id=0, has_side_effects=True, vmem_limit_bytes=63 << 20
+        ),
+        name="feed",
+    )(
+        mixed.reshape(chunks, chunk, local),
+        seg_rows.reshape(chunks, chunk, width),
+        grad_rows.reshape(chunks, chunk, width),
+        up,
+        down,
+        out,
+        gain[None, :],
+    )
+
+
+class Pieces:
+    def __init__(self, group, rows, crossing, jobs, work, landing, summed, sems):
+        self.mine = lax.axis_index("dp")
+        self.bits = group.bit_length() - 1
+        self.rows, self.crossing, self.jobs = rows, crossing, jobs
+        self.work, self.landing, self.summed = work, landing, summed
+        self.slots = work.shape[0]
+        (self.rs_s, self.rs_r, self.ag_s, self.ag_r, self.load_sem, self.store_sem) = sems
+        self.count = crossing[0] + sum(job[2] for job in jobs)
+
+    def step_of(self, odd, level):
+        even_step = 1 << level
+        odd_step = 1 << ((self.bits - level) % self.bits)
+        return jnp.where(odd == 1, odd_step, even_step)
+
+    def bit_of(self, odd, level):
+        return (self.mine // self.step_of(odd, level)) % 2
+
+    def partner(self, odd, level):
+        step = self.step_of(odd, level)
+        return {"dp": self.mine + step - 2 * step * self.bit_of(odd, level)}
+
+    def start_of(self, odd, level):
+        start = jnp.int32(0)
+        for earlier in range(level):
+            start = start + self.bit_of(odd, earlier) * (self.rows >> (earlier + 1))
+        return start
+
+    def span(self, start, level):
+        length = self.rows >> level
+        return pl.ds(pl.multiple_of(start, self.rows >> self.bits), length)
+
+    def halves(self, odd, level):
+        start, bit, half = self.start_of(odd, level), self.bit_of(odd, level), self.rows >> (level + 1)
+        return self.span(start + bit * half, level + 1), self.span(start + (1 - bit) * half, level + 1)
+
+    def reduce_copy(self, slot, odd, level):
+        _, give = self.halves(odd, level)
+        region = pl.ds(self.rows - (self.rows >> level), self.rows >> (level + 1))
+        return pltpu.make_async_remote_copy(
+            src_ref=self.work.at[slot, give],
+            dst_ref=self.landing.at[slot, region],
+            send_sem=self.rs_s.at[slot * self.bits + level],
+            recv_sem=self.rs_r.at[slot * self.bits + level],
+            device_id=self.partner(odd, level),
+            device_id_type=pl.DeviceIdType.MESH,
+        )
+
+    def absorb(self, slot, odd, level):
+        self.reduce_copy(slot, odd, level).wait_recv()
+        keep, _ = self.halves(odd, level)
+        region = pl.ds(self.rows - (self.rows >> level), self.rows >> (level + 1))
+        self.work[slot, keep, :] = self.work[slot, keep, :] + self.landing[slot, region, :]
+
+    def spread_copy(self, buffer, sems, slot, odd, level, arriving):
+        keep, give = self.halves(odd, level)
+        span = give if arriving else keep
+        return pltpu.make_async_remote_copy(
+            src_ref=buffer.at[slot, span],
+            dst_ref=buffer.at[slot, span],
+            send_sem=sems[0].at[slot * self.bits + level],
+            recv_sem=sems[1].at[slot * self.bits + level],
+            device_id=self.partner(odd, level),
+            device_id_type=pl.DeviceIdType.MESH,
+        )
+
+    def spread(self, slot, odd, level, arriving):
+        return self.spread_copy(self.summed, (self.ag_s, self.ag_r), slot, odd, level, arriving)
+
+    def move(self, piece, slot, store, start):
+        columns = self.work.shape[2]
+        first = self.crossing[0]
+        sources = [(self.crossing[1], None, 0, first)]
+        for source, target, count in self.jobs:
+            sources.append((source, target, first, first + count))
+            first += count
+        for source, target, low, high in sources:
+            if store and target is None:
+                continue
+
+            @pl.when((piece >= low) & (piece < high))
+            def _():
+                across = source.shape[2] // columns
+                index = (piece - low) // across
+                lanes = pl.ds(pl.multiple_of((piece - low - index * across) * columns, columns), columns)
+                inside = self.summed.at[slot] if store else self.work.at[slot]
+                if store:
+                    copy = pltpu.make_async_copy(inside, target.at[index, :, lanes], self.store_sem.at[slot])
+                else:
+                    copy = pltpu.make_async_copy(source.at[index, :, lanes], inside, self.load_sem.at[slot])
+                copy.start() if start else copy.wait()
+
+    def load_first(self):
+        self.move(jnp.int32(0), 0, False, True)
+
+    def step(self, tick, cross):
+        bits = self.bits
+        for age in reversed(range(-1, 2 * bits + 2)):
+            piece = tick - age
+            safe = jnp.maximum(piece, 0)
+            slot, odd = safe % self.slots, safe % 2
+            plain = piece >= self.crossing[0]
+            inside = (piece >= 0) & (piece < self.count)
+            if age == 2 * bits + 1:
+
+                @pl.when(inside)
+                def _():
+                    for level in range(bits):
+                        self.reduce_copy(slot, odd, level).wait_send()
+
+                @pl.when(inside & plain)
+                def _():
+                    for level in range(bits):
+                        self.spread(slot, odd, level, False).wait_send()
+                    self.move(piece, slot, True, False)
+
+                @pl.when(inside & jnp.logical_not(plain))
+                def _():
+                    cross(piece, slot, odd, False)
+
+            elif age == 2 * bits:
+
+                @pl.when(inside & plain)
+                def _():
+                    self.spread(slot, odd, 0, True).wait_recv()
+                    self.move(piece, slot, True, True)
+
+            elif age > bits:
+
+                @pl.when(inside & plain)
+                def _():
+                    self.spread(slot, odd, 2 * bits - age, True).wait_recv()
+                    self.spread(slot, odd, 2 * bits - 1 - age, False).start()
+
+            elif age == bits:
+
+                @pl.when(inside)
+                def _():
+                    self.absorb(slot, odd, bits - 1)
+
+                @pl.when(inside & plain)
+                def _():
+                    own = self.span(self.start_of(odd, bits), bits)
+                    self.summed[slot, own, :] = self.work[slot, own, :]
+                    self.spread(slot, odd, bits - 1, False).start()
+
+                @pl.when(inside & jnp.logical_not(plain))
+                def _():
+                    cross(piece, slot, odd, True)
+
+            elif age > 0:
+
+                @pl.when(inside)
+                def _():
+                    self.absorb(slot, odd, age - 1)
+                    self.reduce_copy(slot, odd, age).start()
+
+            elif age == 0:
+
+                @pl.when(inside)
+                def _():
+                    self.move(piece, slot, False, False)
+                    self.reduce_copy(slot, odd, 0).start()
+
+            else:
+
+                @pl.when(inside)
+                def _():
+                    self.move(piece, slot, False, True)
+
+
+def close_kernel(
+    size,
+    group,
+    chunks,
+    hop,
+    counts,
+    gunit_ref,
+    branch_ref,
+    seg_ref,
+    gres_ref,
+    res_ref,
+    gain_ref,
+    gout_ref,
+    gup_ref,
+    gdown_ref,
+    gq_ref,
+    gk_ref,
+    gv_ref,
+    gpack_ref,
+    small_ref,
+    result_ref,
+    gseg_ref,
+    gout_sum,
+    gup_sum,
+    gdown_sum,
+    gq_sum,
+    gk_sum,
+    gv_sum,
+    gpack_sum,
+    small_sum,
+    whole_seg,
+    whole_out,
+    seg_right,
+    seg_left,
+    out_right,
+    out_left,
+    total,
+    work,
+    landing,
+    summed,
+    cross_in,
+    cross_work,
+    small_cross,
+    small_held,
+    small_in,
+    *sems,
+):
+    line = Line(size, chunks, hop)
+    me = line.me
+    pairs = [sems[2 * index : 2 * index + 2] for index in range(8)]
+    seg_scatter = ((True, seg_right, pairs[0]), (False, seg_left, pairs[1]))
+    out_scatter = ((True, out_right, pairs[2]), (False, out_left, pairs[3]))
+    seg_gather = ((True, pairs[4]), (False, pairs[5]))
+    out_gather = ((True, pairs[6]), (False, pairs[7]))
+    piece_sems = sems[16:22]
+    cross_s, cross_r, tail_s, tail_r, tail_store = sems[22:27]
+    mix_s, mix_r, small_s, small_r = sems[27:31]
+    jobs = [
+        (gup_ref, gup_sum, counts[1]),
+        (gdown_ref, gdown_sum, counts[2]),
+        (gq_ref, gq_sum, counts[3]),
+        (gk_ref, gk_sum, counts[4]),
+        (gv_ref, gv_sum, counts[5]),
+        (gpack_ref, gpack_sum, counts[6]),
+    ]
+    pieces = Pieces(group, work.shape[1], (counts[0], gout_ref), jobs, work, landing, summed, piece_sems)
+    bits = pieces.bits
+    pieces.load_first()
+    greet(
+        [{"mp": lax.rem(me + offset, size)} for offset in range(1, size)]
+        + [{"dp": pieces.mine + (1 << bit) - 2 * (1 << bit) * ((pieces.mine // (1 << bit)) % 2)} for bit in range(bits)]
+    )
+
+    def cross_copy(slot, odd, target, origin):
+        own = pieces.span(pieces.start_of(odd, bits), bits)
+        return pltpu.make_async_remote_copy(
+            src_ref=work.at[slot, own],
+            dst_ref=cross_in.at[odd * size + origin],
+            send_sem=cross_s.at[odd * size + target],
+            recv_sem=cross_r.at[odd * size + origin],
+            device_id={"mp": target},
+            device_id_type=pl.DeviceIdType.MESH,
+        )
+
+    def cross(piece, slot, odd, start):
+        target = piece // 2
+
+        @pl.when(target != me)
+        def _():
+            copy = cross_copy(slot, odd, target, me)
+            copy.start() if start else copy.wait_send()
+
+        if start:
+
+            @pl.when(target == me)
+            def _():
+                own = pieces.span(pieces.start_of(odd, bits), bits)
+                cross_in[odd * size + me] = work[slot, own, :]
+
+    def tail_copy(odd):
+        columns = work.shape[2]
+        return pltpu.make_async_copy(
+            cross_work.at[odd], gout_sum.at[0, :, odd * columns : (odd + 1) * columns], tail_store.at[odd]
+        )
+
+    def tail_step(tick):
+        base = counts[0] + bits + 1
+        for odd in range(2):
+
+            @pl.when(tick == base + odd)
+            def _():
+                for offset in range(1, size):
+                    origin = lax.rem(me + offset, size)
+                    cross_copy(0, odd, me, origin).wait_recv()
+                own = pieces.span(pieces.start_of(odd, bits), bits)
+                cross_work[odd, own, :] = sum(
+                    cross_in[odd * size + index] for index in range(1, size)
+                ) + cross_in[odd * size]
+                pieces.spread_copy(cross_work, (tail_s, tail_r), odd, odd, bits - 1, False).start()
+
+            for level in reversed(range(bits)):
+
+                @pl.when(tick == base + odd + bits - level)
+                def _():
+                    pieces.spread_copy(cross_work, (tail_s, tail_r), odd, odd, level, True).wait_recv()
+                    if level:
+                        pieces.spread_copy(cross_work, (tail_s, tail_r), odd, odd, level - 1, False).start()
+                    else:
+                        tail_copy(odd).start()
+
+    def small_across(offset, arriving):
+        origin = lax.rem(me - offset + size, size) if arriving else me
+        return pltpu.make_async_remote_copy(
+            src_ref=small_cross.at[me],
+            dst_ref=small_cross.at[origin],
+            send_sem=mix_s.at[offset],
+            recv_sem=mix_r.at[offset],
+            device_id={"mp": lax.rem(me + offset, size)},
+            device_id_type=pl.DeviceIdType.MESH,
+        )
+
+    def small_within(level):
+        step = 1 << level
+        return pltpu.make_async_remote_copy(
+            src_ref=small_held.at[level],
+            dst_ref=small_in.at[level],
+            send_sem=small_s.at[level],
+            recv_sem=small_r.at[level],
+            device_id={"dp": pieces.mine + step - 2 * step * ((pieces.mine // step) % 2)},
+            device_id_type=pl.DeviceIdType.MESH,
+        )
+
+    def small_step(tick):
+        @pl.when(tick == 0)
+        def _():
+            small_cross[me] = small_ref[...]
+            for offset in range(1, size):
+                small_across(offset, False).start()
+
+        @pl.when(tick == 2)
+        def _():
+            value = small_ref[...]
+            shared = lax.broadcasted_iota(jnp.int32, value.shape, 0) < 2
+            for offset in range(1, size):
+                small_across(offset, True).wait_recv()
+                origin = lax.rem(me - offset + size, size)
+                value = value + jnp.where(shared, small_cross[origin], 0.0)
+            small_held[0] = value
+            small_within(0).start()
+
+        for level in range(bits):
+
+            @pl.when(tick == 4 + 2 * level)
+            def _():
+                small_within(level).wait_recv()
+                value = small_held[level] + small_in[level]
+                if level + 1 < bits:
+                    small_held[level + 1] = value
+                    small_within(level + 1).start()
+                else:
+                    small_sum[...] = value
+
+    def settle(chunk):
+        slot = chunk * size + me
+        line.scatter_sum(chunk, gunit_ref, seg_scatter, total)
+        rows = seg_ref[slot].astype(f32)
+        scale = row_scale(rows)
+        normed = rows * scale
+        weighted = total[...] * gain_ref[...]
+        grad = gres_ref[chunk] + scale * (
+            weighted - normed * jnp.mean(weighted * normed, axis=-1, keepdims=True)
+        )
+        low = grad.astype(bf16)
+        gseg_ref[slot] = low
+        whole_seg[slot] = low.astype(f32)
+        line.gather_start(chunk, whole_seg, seg_gather)
+        line.scatter_sum(chunk, branch_ref, out_scatter, total)
+        low = (res_ref[chunk] + total[...]).astype(bf16)
+        result_ref[slot] = low
+        whole_out[slot] = low.astype(f32)
+        line.gather_start(chunk, whole_out, out_gather)
+
+    def seg_landed(slot):
+        gseg_ref[slot] = whole_seg[slot].astype(bf16)
+
+    def out_landed(slot):
+        result_ref[slot] = whole_out[slot].astype(bf16)
+
+    settle_at = hop * line.reach
+
+    def step(tick, _):
+        line.scatter_step(tick, gunit_ref, seg_scatter)
+        line.scatter_step(tick, branch_ref, out_scatter)
+        chunk, due = line.chunk_at(tick - settle_at)
+
+        @pl.when(due)
+        def _():
+            settle(chunk)
+
+        line.gather_step(tick - settle_at, whole_seg, seg_gather, seg_landed)
+        line.gather_step(tick - settle_at, whole_out, out_gather, out_landed)
+        small_step(tick)
+
+        def piece_step(beat, _):
+            pieces.step(beat, cross)
+            tail_step(beat)
+            return 0
+
+        lax.fori_loop(beats(tick), beats(tick + 1), piece_step, 0)
+        return 0
+
+    line_ticks = line.reach * (chunks - 1) + 2 * settle_at + 1
+    piece_ticks = pieces.count + 2 * bits + 1
+
+    def beats(tick):
+        return jnp.minimum((tick * piece_ticks + line_ticks - 3) // (line_ticks - 2), piece_ticks)
+
+    lax.fori_loop(0, line_ticks, step, 0)
+
+    def drain(chunk, _):
+        line.scatter_drain(chunk, gunit_ref, seg_scatter)
+        line.scatter_drain(chunk, branch_ref, out_scatter)
+        line.gather_drain(chunk, whole_seg, seg_gather)
+        line.gather_drain(chunk, whole_out, out_gather)
+        return 0
+
+    lax.fori_loop(0, chunks, drain, 0)
+    for odd in range(2):
+        for level in range(bits):
+            pieces.spread_copy(cross_work, (tail_s, tail_r), odd, odd, level, False).wait_send()
+        tail_copy(odd).wait()
+    for offset in range(1, size):
+        small_across(offset, False).wait_send()
+    for level in range(bits):
+        small_within(level).wait_send()
+
+
+def close(grad_unit, branch, seg_rows, grad_residual, residual, gain, grads, small, size, group, chunks):
+    rows, width = seg_rows.shape
+    piece = rows // (chunks * size)
+    vmem = pl.BlockSpec(memory_space=pltpu.VMEM)
+    whole = (chunks * size, piece, width)
+    piece_rows, columns = max(256, 8 * group), width // 2
+    bits = group.bit_length() - 1
+    slots = 2 * bits + 2
+    views = [grad.reshape(-1, piece_rows, grad.shape[1]) for grad in grads]
+    counts = tuple(view.shape[0] * (view.shape[2] // columns) for view in views)
+    anywhere = pl.BlockSpec(memory_space=pl.ANY)
+    dma = pltpu.SemaphoreType.DMA
+    sums = [jax.ShapeDtypeStruct(view.shape, f32) for view in views]
+    sums[0] = jax.ShapeDtypeStruct((1, piece_rows, width), f32)
+    return pl.pallas_call(
+        functools.partial(close_kernel, size, group, chunks, 2, counts),
+        in_specs=[vmem] * 6 + [anywhere] * len(views) + [vmem],
+        out_specs=[vmem] * 2 + [anywhere] * len(views) + [vmem],
+        out_shape=[jax.ShapeDtypeStruct(whole, bf16)] * 2 + sums + [jax.ShapeDtypeStruct(small.shape, f32)],
+        scratch_shapes=[pltpu.VMEM(whole, f32)] * 6
+        + [
+            pltpu.VMEM((piece, width), f32),
+            pltpu.VMEM((slots, piece_rows, columns), f32),
+            pltpu.VMEM((slots, piece_rows, columns), f32),
+            pltpu.VMEM((slots, piece_rows, columns), f32),
+            pltpu.VMEM((2 * size, piece_rows // group, columns), f32),
+            pltpu.VMEM((2, piece_rows, columns), f32),
+            pltpu.VMEM((size, *small.shape), f32),
+            pltpu.VMEM((bits, *small.shape), f32),
+            pltpu.VMEM((bits, *small.shape), f32),
+        ]
+        + [dma((chunks * size,))] * 16
+        + [dma((slots * bits,))] * 4
+        + [dma((slots,))] * 2
+        + [dma((2 * size,))] * 2
+        + [dma((2 * bits,))] * 2
+        + [dma((2,))]
+        + [dma((size,))] * 2
+        + [dma((bits,))] * 2,
+        compiler_params=pltpu.CompilerParams(
+            collective_id=1, has_side_effects=True, vmem_limit_bytes=63 << 20
+        ),
+        cost_estimate=pl.CostEstimate(flops=10**11, bytes_accessed=10**9, transcendentals=0),
+        name="close",
+    )(
+        grad_unit.reshape(whole),
+        branch,
+        seg_rows.reshape(whole),
+        grad_residual,
+        residual,
+        gain[None, :],
+        *views,
+        small,
+    )
 
 
 def body(
@@ -447,6 +1319,7 @@
     grad_compressed,
     *,
     mp_size,
+    dp_size,
 ):
     streams, seg_len, width = inputs.shape
     mem_len = memory.shape[1]
@@ -455,22 +1328,13 @@
     local = query_weight.shape[1]
     compress_count = grad_compressed.shape[1]
     rows = streams * seg_len
-    shard_rows = rows // mp_size
-    me = lax.axis_index("mp")
-
-    def own_rows(source):
-        return lax.dynamic_slice_in_dim(source, me * shard_rows, shard_rows, 0)
-
-    nothing = jnp.minimum(jnp.abs(first_gain[0]), 0.0)
-    full_out = (line_gather(output_weight.astype(f32), mp_size) + nothing).reshape(width, width).astype(bf16)
-
     slot_index = jnp.arange(mem_len, dtype=jnp.int32)
     live_rows = jnp.where(
         (slot_index[None, :] >= mem_len - memory_fill[:, None])[:, :, None], memory, jnp.zeros_like(memory)
     )
     evicted = live_rows.reshape(streams * compress_count, 2 * width)
     packed_new = mm(evicted, compress_weight).astype(bf16).reshape(streams, compress_count, -1)
-    grad_compress_w = mm_t0(evicted, grad_compressed.reshape(streams * compress_count, -1))
+    grad_pack = mm_t0(grad_compressed.reshape(streams * compress_count, -1), evicted)
 
     unit, q, k, v, mixed, log_total = attend(
         inputs,
@@ -484,48 +1348,20 @@
         value_weight,
         relative_bias,
     )
-    mixed_all = line_gather(mixed.reshape(rows, local).astype(f32), mp_size)
-    mixed_all = (mixed_all + nothing).transpose(1, 0, 2).reshape(rows, width).astype(bf16)
     seg_rows = inputs.reshape(rows, width)
-    grad_rows = grad_output.reshape(rows, width)
-    residual = seg_rows.astype(f32) + mm(mixed_all, full_out)
-    second_scale = row_scale(residual)
-    ffn_input = (residual * second_scale * second_gain).astype(bf16)
-    pre_act = mm(ffn_input, up_weight)
-    inner = math.sqrt(2.0 / math.pi)
-    squared = pre_act * pre_act
-    tanh = jnp.tanh(inner * (pre_act + 0.044715 * pre_act * squared))
-    activated = (0.5 * pre_act * (1.0 + tanh)).astype(bf16)
-    slope = 0.5 * (1.0 + tanh) + 0.5 * pre_act * (1.0 - tanh * tanh) * (
-        inner * (1.0 + 3.0 * 0.044715 * squared)
-    )
-    grad_pre = (slope * mm_t1(grad_rows, down_weight)).astype(bf16)
-    grad_ffn = mm_t1(grad_pre, up_weight)
-    grad_ffn = line_scatter(grad_ffn.reshape(mp_size, shard_rows, width), mp_size)
-
-    own_residual = own_rows(residual)
-    own_scale = own_rows(second_scale)
-    own_grad = own_rows(grad_rows).astype(f32)
-    normed = own_residual * own_scale
-    grad_second = jnp.sum(grad_ffn * normed, axis=0)
-    weighted = grad_ffn * second_gain
-    grad_residual = own_grad + own_scale * (
-        weighted - normed * jnp.mean(weighted * normed, axis=-1, keepdims=True)
-    )
-    grad_attended = grad_residual.astype(bf16)
-    grad_mixed_rows = mm_t1(grad_attended, full_out).astype(bf16)
-    exchanged = lax.all_to_all(
-        grad_mixed_rows.astype(f32).reshape(shard_rows, mp_size, local).transpose(1, 0, 2), "mp", 0, 0
-    )
-    grad_mixed = (exchanged + nothing).reshape(streams, seg_len, local).astype(bf16)
-    grad_out_full = mm_t0(own_rows(mixed_all), grad_attended)
-
-    branch = mm(activated, down_weight)
-    branch_own = line_scatter(branch.reshape(mp_size, shard_rows, width), mp_size)
-    result_own = (own_residual + branch_own).astype(bf16)
-    grad_down = mm_t0(activated, grad_rows)
-    grad_up = mm_t0(ffn_input, grad_pre)
-
+    grad_mixed, grad_residual, residual, branch, grad_down, grad_up, grad_out_full, grad_second = feed(
+        mixed.reshape(rows, local),
+        seg_rows,
+        grad_output.reshape(rows, width),
+        up_weight,
+        down_weight,
+        output_weight,
+        second_gain,
+        mp_size,
+        dp_size,
+        chunk_count,
+    )
+    grad_mixed = grad_mixed.reshape(streams, seg_len, local)
     grad_unit, gq, gk, gv, rel = attend_back(
         unit,
         q,
@@ -543,35 +1379,36 @@
         packed_len,
     )
     grad_relative = jnp.sum(rel, axis=-1)[:, : len(reach_marks)]
-    grad_unit = line_scatter(grad_unit.reshape(mp_size, shard_rows, width), mp_size)
-    own_seg = own_rows(seg_rows).astype(f32)
-    seg_scale = row_scale(own_seg)
-    seg_normed = own_seg * seg_scale
-    seg_weighted = grad_unit * first_gain
-    grad_seg_own = (
-        grad_residual
-        + seg_scale * (seg_weighted - seg_normed * jnp.mean(seg_weighted * seg_normed, axis=-1, keepdims=True))
-    ).astype(bf16)
-
-    result = (line_gather(result_own.astype(f32), mp_size) + nothing).reshape(inputs.shape).astype(bf16)
-    grad_seg = (line_gather(grad_seg_own.astype(f32), mp_size) + nothing).reshape(inputs.shape).astype(bf16)
-
-    grad_out_w = lax.psum_scatter(grad_out_full, "mp", scatter_dimension=0, tiled=True)
-    gq, gk, gv, grad_out_w, grad_up, grad_down, grad_compress_w, grad_relative = lax.psum(
-        (gq, gk, gv, grad_out_w, grad_up, grad_down, grad_compress_w, grad_relative), "dp"
-    )
-    grad_query_w, grad_key_w, grad_value_w = gq.T, gk.T, gv.T
-    grad_first = (
-        jnp.sum(
-            grad_query_w * query_weight.astype(f32)
-            + grad_key_w * key_weight.astype(f32)
-            + grad_value_w * value_weight.astype(f32),
-            axis=1,
-        )
-        / first_gain
-    )
-    grad_first = lax.psum(grad_first, "mp")
-    grad_second = lax.psum(grad_second, ("dp", "mp"))
+    local_first = sum(
+        jnp.sum(grad * weight.astype(f32).T, axis=0)
+        for grad, weight in ((gq, query_weight), (gk, key_weight), (gv, value_weight))
+    )
+    flat_relative = jnp.pad(grad_relative.reshape(-1), (0, width - grad_relative.size))
+    small = jnp.pad(jnp.stack([local_first / first_gain, grad_second[0], flat_relative]), ((0, 5), (0, 0)))
+    result, grad_seg, grad_out_w, grad_up, grad_down, gq, gk, gv, grad_pack, small = close(
+        grad_unit,
+        branch,
+        seg_rows,
+        grad_residual,
+        residual,
+        first_gain,
+        (grad_out_full, grad_up, grad_down, gq, gk, gv, grad_pack),
+        small,
+        mp_size,
+        dp_size,
+        chunk_count,
+    )
+    grad_first, grad_second = small[0], small[1]
+    grad_relative = small[2, : grad_relative.size].reshape(grad_relative.shape)
+    result = result.reshape(inputs.shape)
+    grad_seg = grad_seg.reshape(inputs.shape)
+    grad_query_w = gq.reshape(local, width).T
+    grad_key_w = gk.reshape(local, width).T
+    grad_value_w = gv.reshape(local, width).T
+    grad_out_w = grad_out_w.reshape(local, width)
+    grad_compress_w = grad_pack.reshape(-1, 2 * width).T
+    grad_up = grad_up.reshape(up_weight.shape)
+    grad_down = grad_down.reshape(down_weight.shape)
     return (
         result,
         packed_new,
@@ -625,7 +1462,7 @@
         P(None, "mp"),
     )
     return jax.shard_map(
-        functools.partial(body, mp_size=mesh.shape["mp"]),
+        functools.partial(body, mp_size=mesh.shape["mp"], dp_size=mesh.shape["dp"]),
         mesh=mesh,
         in_specs=in_specs,
         out_specs=out_specs,

time: 800 us -> 515 us (0.64); the launches traced: 791 us -> 514 us
  Pallas kernels: 39.8 us -> 470 us
  waiting for transfers between devices: 363 us -> 0 us
  starting transfers between devices: 121 us -> 0 us
  blocking collectives: 104 us -> 0 us
  other arithmetic: 49.1 us -> 6.67 us
  local copies, waits for them, and re-layouts: 63.6 us -> 32.3 us
  matrix products: 35.1 us -> 4.71 us
  between operations: 15.8 us -> 0.83 us
    pallas_call x0 -> x2, Pallas kernels: none -> 430 us  [the longest x1 246 us: close(): pl.pallas_call(functools.partial(close_kernel, size, group, chunks, 2, co...]
    ppermute x42 -> x0, waiting for transfers between devices: 313 us -> none  [the longest x12 134 us: line_gather(): lax.ppermute(to_left, 'mp', [(i, i - 1) for i in range(1, size - step + 1)])]
    psum x3 -> x0, blocking collectives: 104 us -> none  [the longest x1 80.9 us: body(): grad_second = lax.psum(grad_second, ('dp', 'mp'))]
    ppermute x42 -> x0, starting transfers between devices: 103 us -> none  [the longest x9 37.4 us: line_scatter(): from_left = lax.ppermute(rightward, 'mp', pairs)]
    all_to_all x1 -> x0, waiting for transfers between devices: 49.9 us -> none  [body(): lax.all_to_all(grad_mixed_rows.astype(f32).reshape(shard_rows, mp_size, l...]
    add x10 -> x0, other arithmetic: 29.6 us -> none  [the longest x6 18.5 us: line_scatter(): rightward = rightward + from_left]
    unnamed x99 -> x44, local copies, waits for them, and re-layouts: 50.1 us -> 26 us
    all_to_all x1 -> x0, starting transfers between devices: 17.1 us -> none  [body(): lax.all_to_all(grad_mixed_rows.astype(f32).reshape(shard_rows, mp_size, l...]
  transfers between devices with their start and end apart: 45 -> 0, of which waited for: 25 -> 0; matrix products, arithmetic and copies ran while one was open for 13% -> 0% of each run, Pallas kernels for 3% -> 0%
where the time goes in v2:
time: 515 us; the launch traced here: 514 us
  Pallas kernels  470 us (91%)
  local copies, waits for them, and re-layouts  32.3 us (6%)
  other arithmetic  6.67 us (1%)
    pallas_call x1, Pallas kernels, close(): pl.pallas_call(functools.partial(close_kernel, size, group, chunks, 2, co...  246 us
    pallas_call x1, Pallas kernels, feed(): pl.pallas_call(functools.partial(feed_kernel, size, group, chunks, 2, 10,...  184 us
    unnamed x44, local copies, waits for them, and re-layouts  26 us
    pallas_call x1, Pallas kernels, attend_back(): pl.pallas_call(functools.partial(attend_back_kernel, sizes), grid=(stream...  23.7 us
    pallas_call x1, Pallas kernels, attend(): pl.pallas_call(functools.partial(attend_kernel, sizes), grid=(streams,),...  16 us

profile of v2, /device:TPU:0, one launch (start us, length us, event | category | flops | bytes accessed | tf_op | source)
XLA Modules:
  0.0 514.3 jit_solution(3203510966093157109)
XLA Ops:
  0.6 0.0 copy-start
  0.7 0.0 copy-start.6
  0.7 0.9 copy-done
  1.6 0.7 broadcast_subtract_fusion
  2.3 0.1 iota_compare_fusion.1
  2.3 1.2 copy.40
  3.6 2.1 copy.41
  5.6 2.0 copy.42
  7.7 0.0 copy-done.6
  7.7 1.5 broadcast_select_fusion
  9.2 2.7 reshape.126
  11.9 2.6 convolution_convert_fusion
  14.6 2.1 convolution_bitcast_fusion.gpack_ref
  16.6 16.0 %attend.1 = (bf16[2,1536,1024]{2,1,0:T(8,128)(2,1)}, bf16[2,512,256]{2,1,0:T(8,128)(2,1)}, bf16[2,1536,256]{2,1,0:T(8,128)(2,1)}, bf16[2,1536,256]{2,1,0:T(8,128...) custom-call(s32[2]{0:T(128)} %memory_fill.3, s32[2]{0:T(128)} %packed_fill.3, f32[2,22]{1,0:T(2,128)} %bias_ref.3, ...), custom_call_target="tpu_custom_call" | custom-call | flops 6442450944 | bytes 17301504 | tf_op jit(solution)/shard_map/attend/pallas_call | solution.py:151
  32.6 1.6 reduce
  34.2 0.6 reshape.140.log_ref
  34.8 183.8 %feed.1 = (bf16[32,32,256]{2,1,0:T(8,128)(2,1)}, f32[8,32,1024]{2,1,0:T(8,128)}, f32[8,32,1024]{2,1,0:T(8,128)}, f32[32,32,1024]{2,1,0:T(8,128)}, f32[1024,1024]...) custom-call(bf16[8,128,256]{2,1,0:T(8,128)(2,1)} %bitcast.74, ...), custom_call_target="tpu_custom_call" | custom-call | tf_op jit(solution)/shard_map/feed/pallas_call | solution.py:772
  218.6 0.0 copy-start.7
  218.6 0.0 copy-start.8
  218.6 23.7 %attend_back.1 = (f32[2,512,1024]{2,1,0:T(8,128)}, f32[256,1024]{1,0:T(8,128)}, f32[256,1024]{1,0:T(8,128)}, f32[256,1024]{1,0:T(8,128)}, f32[2,24,128]{2,1,0:T(8,128)}) custom-call(s32[2]{0:T(128)} %memory_fill.3, s32[2]{0:T(128)} %packed_fill.3, f32[2,22]{1,0:T(2,128)} %bias_ref.3, bf16[2,1536,1024]{2,1,0:T(8,128)(2,1)} %get-tuple-element.42.unit_ref, ...), custom_call_target="tpu_custom_call" | custom-call | flops 10468982784 | bytes 11010048 | tf_op jit(solution)/shard_map/attend_back/pallas_call | solution.py:335
  242.3 0.0 copy-start.9
  242.3 0.0 copy-done.7
  242.3 0.0 copy-done.8
  242.4 0.0 copy-start.14
  242.4 0.0 copy-start.13
  242.4 0.0 copy-start.15
  242.4 1.9 fusion
  244.3 0.0 copy-done.9
  244.3 0.2 fusion.2
  244.5 0.0 copy-done.14
  244.5 0.0 copy-done.13
  244.5 0.1 reduce_sum.39
  244.6 0.1 reshape.129
  244.7 0.0 copy-done.15
  244.7 0.6 select_maximum_fusion.small_ref
  245.4 246.3 %close.1 = (bf16[32,32,1024]{2,1,0:T(8,128)(2,1)}, bf16[32,32,1024]{2,1,0:T(8,128)(2,1)}, f32[1,256,1024]{2,1,0:T(8,128)}, f32[4,256,1024]{2,1,0:T(8,128)}, f32[...) custom-call(f32[32,32,1024]{2,1,0:T(8,128)} %bitcast.87, ...), custom_call_target="tpu_custom_call" | custom-call | flops 99999997952 | bytes 1000000000 | tf_op jit(solution)/shard_map/close/pallas_call | solution.py:1260
  491.7 0.0 copy-start.12
  491.7 0.8 slice_reduce_fusion
  492.4 1.4 fusion.3
  493.9 0.6 reshape_squeeze.3
  494.5 0.0 copy-start.11
  494.5 2.6 copy.43
  497.1 0.0 copy-done.12
  497.1 1.3 copy.44
  498.5 0.0 copy-done.11
  498.5 1.3 copy.45
  499.8 0.0 copy-start.5
  499.8 3.0 copy.46
  502.8 0.0 copy-done.5
  502.8 0.0 copy-start.4
  502.8 0.0 copy-start.10
  502.8 1.3 copy.53
  504.1 1.0 copy-done.4
  505.1 0.0 copy-start.3
  505.1 1.3 copy.54
  506.5 0.0 copy-done.10
  506.5 1.0 copy.55
  507.4 1.1 copy-done.3
  508.5 0.0 copy-start.2
  508.5 2.1 copy.56
  510.7 1.6 copy-done.2
  512.2 0.0 copy-start.1
  512.2 2.0 copy.57
  514.3 0.0 copy-done.1
  (2 shorter events, 0.0 us)
Async XLA Ops:
  0.6 1.0 copy-start
  0.7 7.0 %copy-start.6 = (bf16[2,512,1024]{2,1,0:T(8,128)(2,1)S(1)}, bf16[2,512,1024]{2,1,0:T(8,128)(2,1)}, u32[]{:S(2)}) copy-start(bf16[2,512,1024]{2,1,0:T(8,128)(2,1)} %memory_ref.1) | copy-start | bytes 6291460
  218.6 23.7 %copy-start.7 = (bf16[1024,256]{0,1:T(8,128)(2,1)S(1)}, bf16[1024,256]{0,1:T(8,128)(2,1)}, u32[]{:S(2)}) copy-start(bf16[1024,256]{0,1:T(8,128)(2,1)} %copy.41) | copy-start | bytes 1572868
  218.6 23.7 %copy-start.8 = (bf16[1024,256]{0,1:T(8,128)(2,1)S(1)}, bf16[1024,256]{0,1:T(8,128)(2,1)}, u32[]{:S(2)}) copy-start(bf16[1024,256]{0,1:T(8,128)(2,1)} %copy.42) | copy-start | bytes 1572868
  242.3 2.0 copy-start.9
  242.4 2.1 copy-start.14
  242.4 2.2 copy-start.13
  242.4 2.3 copy-start.15
  491.7 5.5 %copy-start.12 = (f32[1,256,1024]{2,1,0:T(8,128)S(1)}, f32[1,256,1024]{2,1,0:T(8,128)}, u32[]{:S(2)}) copy-start(f32[1,256,1024]{2,1,0:T(8,128)} %get-tuple-element.65) | copy-start | bytes 3145732
  494.5 3.9 copy-start.11
  499.8 3.0 copy-start.5
  502.8 2.3 copy-start.4
  502.8 3.7 copy-start.10
  505.1 3.4 copy-start.3
  508.5 3.7 copy-start.2
  512.2 2.0 copy-start.1

commit v3 on v2

--- a/solution.py
+++ b/solution.py
@@ -71,8 +71,78 @@
     return jnp.where(dead_packed | dead_memory, masked_score, 0.0).astype(f32)
 
 
+def greet(peers):
+    barrier = pltpu.get_barrier_semaphore()
+    for peer in peers:
+        pl.semaphore_signal(barrier, inc=1, device_id=peer, device_id_type=pl.DeviceIdType.MESH)
+    pl.semaphore_wait(barrier, len(peers))
+
+
+class Spread:
+    def __init__(self, size, group, buffer, sems):
+        self.me, self.mine = lax.axis_index("mp"), lax.axis_index("dp")
+        self.size, self.group, self.buffer = size, group, buffer
+        self.bits = group.bit_length() - 1
+        self.across_s, self.across_r, self.within_s, self.within_r = sems
+        order = list(reversed(range(self.bits)))
+        self.orders = (order, order[1::-1] + order[2:])
+        self.spots = []
+        for order in self.orders:
+            spot = jnp.int32(0)
+            for level, bit in enumerate(order):
+                spot = spot + ((self.mine // (1 << bit)) % 2) * (1 << level)
+            self.spots.append(spot)
+
+    def place_of(self, half, member):
+        return sum(((member >> bit) & 1) << level for level, bit in enumerate(self.orders[half]))
+
+    def others(self, offset):
+        return {"mp": lax.rem(self.me + offset, self.size)}
+
+    def partner(self, half, level):
+        step = 1 << self.orders[half][level]
+        return {"dp": self.mine + step - 2 * step * ((self.mine // step) % 2)}
+
+    def across(self, half, offset, arriving):
+        origin = lax.rem(self.me - offset + self.size, self.size) if arriving else self.me
+        return pltpu.make_async_remote_copy(
+            src_ref=self.buffer.at[half, self.spots[half], origin],
+            dst_ref=self.buffer.at[half, self.spots[half], origin],
+            send_sem=self.across_s.at[half * self.size + offset],
+            recv_sem=self.across_r.at[half * self.size + offset],
+            device_id=self.others(offset),
+            device_id_type=pl.DeviceIdType.MESH,
+        )
+
+    def block(self, half, level, other):
+        count = 1 << level
+        start = (self.spots[half] // count) * count
+        if other:
+            start = start + count - 2 * count * ((self.spots[half] // count) % 2)
+        return pl.ds(start, count)
+
+    def within(self, half, level, arriving):
+        span = self.block(half, level, arriving)
+        return pltpu.make_async_remote_copy(
+            src_ref=self.buffer.at[half, span],
+            dst_ref=self.buffer.at[half, span],
+            send_sem=self.within_s.at[half * self.bits + level],
+            recv_sem=self.within_r.at[half * self.bits + level],
+            device_id=self.partner(half, level),
+            device_id_type=pl.DeviceIdType.MESH,
+        )
+
+    def start_level(self, level):
+        for half in range(2):
+            if level:
+                self.within(half, level - 1, True).wait_recv()
+            self.within(half, level, False).start()
+
+
 def attend_kernel(
     sizes,
+    size,
+    group,
     memory_fill,
     packed_fill,
     bias_ref,
@@ -83,14 +153,23 @@
     wq_ref,
     wk_ref,
     wv_ref,
+    wc_ref,
+    gcomp_ref,
+    wo_ref,
     unit_ref,
     q_ref,
     k_ref,
     v_ref,
     mixed_ref,
     log_ref,
+    packed_new_ref,
+    gpack_ref,
+    begun_ref,
     strip,
     live,
+    mem_rows,
+    spread_in,
+    *sems,
 ):
     seg_len, mem_len, packed_len, heads, head_dim = sizes
     kept = mem_len + packed_len
@@ -98,16 +177,49 @@
     stream = pl.program_id(0)
     scale = 1.0 / math.sqrt(head_dim)
     gain = gain_ref[...]
+    spread = Spread(size, group, spread_in, sems[:4])
+    piece, columns = spread_in.shape[3:]
+    width = gain.shape[1]
+
+    @pl.when(stream == 0)
+    def _():
+        greet(
+            [spread.others(offset) for offset in range(1, size)]
+            + [spread.partner(half, 0) for half in range(2)]
+        )
+        rows = pl.ds(pl.multiple_of(spread.mine * piece, piece), piece)
+        for half in range(2):
+            lanes = slice(half * columns, (half + 1) * columns)
+            spread_in[half, spread.spots[half], spread.me] = wo_ref[rows, lanes].astype(f32)
+            for offset in range(1, size):
+                spread.across(half, offset, False).start()
+        gpack_ref[...] = jnp.zeros_like(gpack_ref)
+
+    slot = lax.broadcasted_iota(jnp.int32, mem_rows.shape[1:], 0)
+    keep = slot >= mem_len - memory_fill[stream]
+    count = packed_new_ref.shape[1]
+    for column in range(mem_rows.shape[0]):
+        lanes = slice(column * block, (column + 1) * block)
+        mem_rows[column] = jnp.where(keep, memory_ref[0, :, lanes].astype(f32), 0.0)
+    packed_new = jnp.zeros(packed_new_ref.shape[1:], f32)
+    for parity in range(2):
+        rows = jnp.concatenate(
+            [mem_rows[column, pl.ds(parity, count, stride=2), :] for column in range(mem_rows.shape[0])], axis=1
+        ).astype(bf16)
+        lanes = slice(parity * width, (parity + 1) * width)
+        packed_new = packed_new + mm(rows, wc_ref[lanes, :])
+        gpack_ref[:, lanes] += mm_t0(gcomp_ref[0], rows)
+    packed_new_ref[0] = packed_new.astype(bf16)
     start = 0
-    for part_ref, size in ((packed_ref, packed_len), (memory_ref, mem_len), (seg_ref, seg_len)):
+    for part_ref, length in ((packed_ref, packed_len), (memory_ref, mem_len), (seg_ref, seg_len)):
         rows = part_ref[0].astype(f32)
         unit = (rows * row_scale(rows) * gain).astype(bf16)
-        unit_ref[0, start : start + size, :] = unit
-        k_ref[0, start : start + size, :] = mm(unit, wk_ref[...]).astype(bf16)
-        v_ref[0, start : start + size, :] = mm(unit, wv_ref[...]).astype(bf16)
+        unit_ref[0, start : start + length, :] = unit
+        k_ref[0, start : start + length, :] = mm(unit, wk_ref[...]).astype(bf16)
+        v_ref[0, start : start + length, :] = mm(unit, wv_ref[...]).astype(bf16)
         if start == kept:
             q_ref[0] = mm(unit, wq_ref[...]).astype(bf16)
-        start += size
+        start += length
     live[...] = live_mask((8, kept), 1, packed_len, mem_len, packed_fill[stream], memory_fill[stream])
     for head in range(heads):
         lanes = slice(head * head_dim, (head + 1) * head_dim)
@@ -128,12 +240,36 @@
             top = jnp.max(score, axis=-1, keepdims=True)
             weight = jnp.exp(score - top)
             total = jnp.sum(weight, axis=-1, keepdims=True)
-            log_ref[0, head, rows, :] = top + jnp.log(total)
+            log_total = jnp.broadcast_to(top + jnp.log(total), (query_block, block))
+            log_ref[0, head, :, rows] = log_total.T[0:1, :]
             mixed = mm(weight.astype(bf16), v_ref[0, :reach, lanes]) * (1.0 / total)
             mixed_ref[0, rows, lanes] = mixed.astype(bf16)
 
-
-def attend(inputs, memory, packed, memory_fill, packed_fill, gain, wq, wk, wv, bias):
+    @pl.when(stream == 0)
+    def _():
+        for half in range(2):
+            for offset in range(1, size):
+                spread.across(half, offset, True).wait_recv()
+        spread.start_level(0)
+
+    @pl.when(stream == pl.num_programs(0) - 1)
+    def _():
+        copies = []
+        for half in range(2):
+            spread.within(half, 0, True).wait_recv()
+            pair = spread_in.at[half, pl.ds((spread.spots[half] // 2) * 2, 2)]
+            copies.append(pltpu.make_async_copy(pair, begun_ref.at[half], sems[4].at[half]))
+            copies[-1].start()
+        for half in range(2):
+            for offset in range(1, size):
+                spread.across(half, offset, False).wait_send()
+            spread.within(half, 0, False).wait_send()
+            copies[half].wait()
+
+
+def attend(
+    inputs, memory, packed, memory_fill, packed_fill, gain, wq, wk, wv, bias, wc, gcomp, wo, size, group
+):
     streams, seg_len, width = inputs.shape
     mem_len, packed_len = memory.shape[1], packed.shape[1]
     heads = bias.shape[0]
@@ -141,6 +277,9 @@
     keys = seg_len + mem_len + packed_len
     sizes = (seg_len, mem_len, packed_len, heads, local // heads)
     smem = pl.BlockSpec(memory_space=pltpu.SMEM)
+    compress_count = gcomp.shape[1]
+    piece = wo.shape[0] // group
+    bits = group.bit_length() - 1
 
     def rows_of(count, columns):
         return pl.BlockSpec((1, count, columns), lambda s: (s, 0, 0))
@@ -149,7 +288,7 @@
         return pl.BlockSpec(shape, lambda s: (0,) * len(shape))
 
     return pl.pallas_call(
-        functools.partial(attend_kernel, sizes),
+        functools.partial(attend_kernel, sizes, size, group),
         grid=(streams,),
         in_specs=[
             smem,
@@ -162,6 +301,9 @@
             whole(wq.shape),
             whole(wk.shape),
             whole(wv.shape),
+            whole(wc.shape),
+            rows_of(compress_count, local),
+            whole(wo.shape),
         ],
         out_specs=[
             rows_of(keys, width),
@@ -169,7 +311,10 @@
             rows_of(keys, local),
             rows_of(keys, local),
             rows_of(seg_len, local),
-            pl.BlockSpec((1, heads, seg_len, 1), lambda s: (s, 0, 0, 0)),
+            pl.BlockSpec((1, heads, 1, seg_len), lambda s: (s, 0, 0, 0)),
+            rows_of(compress_count, local),
+            whole((local, 2 * width)),
+            pl.BlockSpec(memory_space=pl.ANY),
         ],
         out_shape=[
             jax.ShapeDtypeStruct((streams, keys, width), bf16),
@@ -177,20 +322,32 @@
             jax.ShapeDtypeStruct((streams, keys, local), bf16),
             jax.ShapeDtypeStruct((streams, keys, local), bf16),
             jax.ShapeDtypeStruct((streams, seg_len, local), bf16),
-            jax.ShapeDtypeStruct((streams, heads, seg_len, 1), f32),
+            jax.ShapeDtypeStruct((streams, heads, 1, seg_len), f32),
+            jax.ShapeDtypeStruct((streams, compress_count, local), bf16),
+            jax.ShapeDtypeStruct((local, 2 * width), f32),
+            jax.ShapeDtypeStruct((2, 2, size, piece, width // 2), f32),
         ],
         scratch_shapes=[
             pltpu.VMEM((block, diagonal_count(seg_len, mem_len + packed_len) * block), f32),
             pltpu.VMEM((8, mem_len + packed_len), f32),
+            pltpu.VMEM((width // block, mem_len, block), f32),
+            pltpu.VMEM((2, group, size, piece, width // 2), f32),
+            pltpu.SemaphoreType.DMA((2 * size,)),
+            pltpu.SemaphoreType.DMA((2 * size,)),
+            pltpu.SemaphoreType.DMA((2 * bits,)),
+            pltpu.SemaphoreType.DMA((2 * bits,)),
+            pltpu.SemaphoreType.DMA((2,)),
         ],
-        compiler_params=pltpu.CompilerParams(vmem_limit_bytes=60 << 20),
+        compiler_params=pltpu.CompilerParams(
+            collective_id=2, has_side_effects=True, vmem_limit_bytes=60 << 20
+        ),
         cost_estimate=pl.CostEstimate(
             flops=streams * (2 * keys * width * local * 3 + 4 * seg_len * keys * local),
             bytes_accessed=streams * keys * (width * 4 + local * 6),
             transcendentals=streams * heads * seg_len * keys,
         ),
         name="attend",
-    )(memory_fill, packed_fill, bias, inputs, memory, packed, gain[None, :], wq, wk, wv)
+    )(memory_fill, packed_fill, bias, inputs, memory, packed, gain[None, :], wq, wk, wv, wc, gcomp, wo)
 
 
 def attend_back_kernel(
@@ -207,11 +364,13 @@
     wq_ref,
     wk_ref,
     wv_ref,
+    gain_ref,
+    gsecond_ref,
     gunit_ref,
     gq_ref,
     gk_ref,
     gv_ref,
-    rel_ref,
+    small_ref,
     strip,
     live,
     dk_sum,
@@ -298,6 +457,9 @@
     def _():
         rows = lax.broadcasted_iota(jnp.int32, (block, block), 0)
         cols = lax.broadcasted_iota(jnp.int32, (block, block), 1)
+        width = gain_ref.shape[1]
+        lane = lax.broadcasted_iota(jnp.int32, (1, width), 1)
+        relative = jnp.zeros((1, width), f32)
         for head in range(heads):
             blocks = []
             for column in range(diagonal_count(seg_len, kept)):
@@ -314,10 +476,20 @@
                         total = total + jnp.sum(
                             jnp.where(distance >= mark_value, value, 0.0), axis=0, keepdims=True
                         )
-                rel_ref[head, position : position + 1, :] = total
-
-
-def attend_back(unit, q, k, v, log_total, grad_mixed, memory_fill, packed_fill, wq, wk, wv, bias, mem_len, packed_len):
+                total = jnp.sum(total, axis=1, keepdims=True)
+                relative = jnp.where(lane == head * len(reach_marks) + position, total, relative)
+        first = jnp.zeros((1, width), f32)
+        for grad_ref, weight_ref in ((gq_ref, wq_ref), (gk_ref, wk_ref), (gv_ref, wv_ref)):
+            turned = weight_ref[...].astype(f32).T
+            first = first + jnp.sum(grad_ref[...] * turned, axis=0, keepdims=True)
+        small_ref[...] = jnp.concatenate(
+            [first / gain_ref[...], gsecond_ref[...], relative, jnp.zeros((5, width), f32)], axis=0
+        )
+
+
+def attend_back(
+    unit, q, k, v, log_total, grad_mixed, memory_fill, packed_fill, wq, wk, wv, bias, gain, grad_second, mem_len, packed_len
+):
     streams, keys, width = unit.shape
     seg_len, local = q.shape[1:]
     heads = bias.shape[0]
@@ -348,20 +520,22 @@
             whole(wq.shape),
             whole(wk.shape),
             whole(wv.shape),
+            whole((1, width)),
+            whole((1, width)),
         ],
         out_specs=[
             rows_of(seg_len, width),
             whole((local, width)),
             whole((local, width)),
             whole((local, width)),
-            whole((heads, 24, block)),
+            whole((8, width)),
         ],
         out_shape=[
             jax.ShapeDtypeStruct((streams, seg_len, width), f32),
             jax.ShapeDtypeStruct((local, width), f32),
             jax.ShapeDtypeStruct((local, width), f32),
             jax.ShapeDtypeStruct((local, width), f32),
-            jax.ShapeDtypeStruct((heads, 24, block), f32),
+            jax.ShapeDtypeStruct((8, width), f32),
         ],
         scratch_shapes=[
             pltpu.VMEM((strip_len, block), f32),
@@ -388,11 +562,13 @@
         q,
         k,
         v,
-        log_total.reshape(streams, heads, 1, seg_len),
+        log_total,
         grad_mixed,
         wq,
         wk,
         wv,
+        gain[None, :],
+        grad_second,
     )
 
 
@@ -503,26 +679,19 @@
                     self.copy(whole, whole, sems, slot, right).wait_send()
 
 
-def greet(peers):
-    barrier = pltpu.get_barrier_semaphore()
-    for peer in peers:
-        pl.semaphore_signal(barrier, inc=1, device_id=peer, device_id_type=pl.DeviceIdType.MESH)
-    pl.semaphore_wait(barrier, len(peers))
-
-
 def feed_kernel(
     size,
     group,
     chunks,
     hop,
     delay,
-    stages,
+    beat,
     mixed_ref,
     seg_ref,
     grad_ref,
     up_ref,
     down_ref,
-    out_ref,
+    begun_ref,
     gain_ref,
     gm_ref,
     gres_ref,
@@ -548,56 +717,22 @@
 ):
     line = Line(size, chunks, hop)
     me = line.me
-    mine = lax.axis_index("dp")
-    (hr_s, hr_r, hl_s, hl_r, sr_s, sr_r, sl_s, sl_r, x_s, x_r, wz_s, wz_r, wd_s, wd_r) = sems
+    (hr_s, hr_r, hl_s, hl_r, sr_s, sr_r, sl_s, sl_r, x_s, x_r, wd_s, wd_r) = sems
     gather_lanes = ((True, (hr_s, hr_r)), (False, (hl_s, hl_r)))
     scatter_lanes = ((True, held_right, (sr_s, sr_r)), (False, held_left, (sl_s, sl_r)))
-    bits = group.bit_length() - 1
-    piece, width = weights_in.shape[2:]
+    spread = Spread(size, group, weights_in, (None, None, wd_s, wd_r))
+    bits = spread.bits
+    piece, columns = weights_in.shape[3:]
+    width = weights.shape[1]
     rows = total.shape[0]
     local = mixed_ref.shape[-1]
-    spot = jnp.int32(0)
-    for bit in range(bits):
-        spot = spot + ((mine // (1 << bit)) % 2) * (1 << (bits - 1 - bit))
-
-    def others(offset):
-        return {"mp": lax.rem(me + offset, size)}
-
-    def partner(level):
-        step = 1 << (bits - 1 - level)
-        return {"dp": mine + step - 2 * step * ((mine // step) % 2)}
-
-    greet([others(offset) for offset in range(1, size)] + [partner(level) for level in range(bits)])
-
-    weights_in[spot, me] = out_ref[pl.ds(pl.multiple_of(mine * piece, piece), piece), :].astype(f32)
-
-    def weight_across(offset, arriving):
-        origin = lax.rem(me - offset + size, size) if arriving else me
-        return pltpu.make_async_remote_copy(
-            src_ref=weights_in.at[spot, origin],
-            dst_ref=weights_in.at[spot, origin],
-            send_sem=wz_s.at[offset],
-            recv_sem=wz_r.at[offset],
-            device_id=others(offset),
-            device_id_type=pl.DeviceIdType.MESH,
-        )
-
-    def weight_within(level, arriving):
-        count = 1 << level
-        start = (spot // count) * count
-        if arriving:
-            start = start + count - 2 * count * ((spot // count) % 2)
-        return pltpu.make_async_remote_copy(
-            src_ref=weights_in.at[pl.ds(start, count)],
-            dst_ref=weights_in.at[pl.ds(start, count)],
-            send_sem=wd_s.at[level],
-            recv_sem=wd_r.at[level],
-            device_id=partner(level),
-            device_id_type=pl.DeviceIdType.MESH,
-        )
-
-    for offset in range(1, size):
-        weight_across(offset, False).start()
+    greet(
+        [spread.others(offset) for offset in range(1, size)]
+        + [spread.partner(half, level) for half in range(2) for level in range(1, bits)]
+    )
+    for half in range(2):
+        weights_in[half, pl.ds((spread.spots[half] // 2) * 2, 2)] = begun_ref[half]
+        spread.within(half, 1, False).start()
 
     def stage_heads(chunk, _):
         heads_in[chunk * size + me] = mixed_ref[chunk].astype(f32)
@@ -609,29 +744,20 @@
     gup_ref[...] = jnp.zeros_like(gup_ref)
 
     def weight_step(tick):
-        @pl.when(tick == stages[0])
-        def _():
-            for offset in range(1, size):
-                weight_across(offset, True).wait_recv()
-            weight_within(0, False).start()
-
-        for level in range(1, bits):
-
-            @pl.when(tick == stages[min(level, len(stages) - 1)] + max(0, level - len(stages) + 1))
+        for level in range(2, bits):
+
+            @pl.when(tick == beat + level - 2)
             def _():
-                weight_within(level - 1, True).wait_recv()
-                weight_within(level, False).start()
+                spread.start_level(level)
 
     def weight_finish():
-        weight_within(bits - 1, True).wait_recv()
-        for index in range(size):
-            pieces = []
-            for member in range(group):
-                place = sum(((member >> bit) & 1) << (bits - 1 - bit) for bit in range(bits))
-                pieces.append(weights_in[place, index])
-            weights[index * group * piece : (index + 1) * group * piece, :] = jnp.concatenate(
-                pieces, axis=0
-            ).astype(bf16)
+        for half in range(2):
+            spread.within(half, bits - 1, True).wait_recv()
+            for index in range(size):
+                pieces = [weights_in[half, spread.place_of(half, member), index] for member in range(group)]
+                weights[index * group * piece : (index + 1) * group * piece, half * columns : (half + 1) * columns] = (
+                    jnp.concatenate(pieces, axis=0).astype(bf16)
+                )
 
     own = pl.ds(pl.multiple_of(me * rows, rows), rows)
 
@@ -754,13 +880,12 @@
         return 0
 
     lax.fori_loop(0, chunks, finish, 0)
-    for offset in range(1, size):
-        weight_across(offset, False).wait_send()
-    for level in range(bits):
-        weight_within(level, False).wait_send()
-
-
-def feed(mixed, seg_rows, grad_rows, up, down, out, gain, size, group, chunks):
+    for half in range(2):
+        for level in range(1, bits):
+            spread.within(half, level, False).wait_send()
+
+
+def feed(mixed, seg_rows, grad_rows, up, down, begun, gain, size, group, chunks):
     rows, width = seg_rows.shape
     local = mixed.shape[1]
     chunk = rows // chunks
@@ -770,7 +895,7 @@
     slots = pltpu.SemaphoreType.DMA((chunks * size,))
     bits = group.bit_length() - 1
     return pl.pallas_call(
-        functools.partial(feed_kernel, size, group, chunks, 2, 10, (3, 6, 10)),
+        functools.partial(feed_kernel, size, group, chunks, 2, 0, 4),
         in_specs=[vmem] * 7,
         out_specs=[vmem] * 8,
         out_shape=[
@@ -790,7 +915,7 @@
             pltpu.VMEM((chunks * size, piece, width), f32),
             pltpu.VMEM((chunks * size, piece, local), f32),
             pltpu.VMEM((chunks * size, piece, local), f32),
-            pltpu.VMEM((group, size, out.shape[0] // group, width), f32),
+            pltpu.VMEM((2, group, *begun.shape[2:]), f32),
             pltpu.VMEM((width, width), bf16),
             pltpu.VMEM((chunk, width), f32),
             pltpu.VMEM((piece, width), f32),
@@ -798,8 +923,7 @@
             pltpu.VMEM((chunks, piece, width), bf16),
         ]
         + [slots] * 10
-        + [pltpu.SemaphoreType.DMA((size,))] * 2
-        + [pltpu.SemaphoreType.DMA((bits,))] * 2,
+        + [pltpu.SemaphoreType.DMA((2 * bits,))] * 2,
         compiler_params=pltpu.CompilerParams(
             collective_id=0, has_side_effects=True, vmem_limit_bytes=63 << 20
         ),
@@ -810,20 +934,21 @@
         grad_rows.reshape(chunks, chunk, width),
         up,
         down,
-        out,
+        begun,
         gain[None, :],
     )
 
 
 class Pieces:
-    def __init__(self, group, rows, crossing, jobs, work, landing, summed, sems):
+    def __init__(self, group, rows, gap, crossing, jobs, work, landing, summed, sems):
         self.mine = lax.axis_index("dp")
         self.bits = group.bit_length() - 1
-        self.rows, self.crossing, self.jobs = rows, crossing, jobs
+        self.rows, self.gap, self.crossing, self.jobs = rows, gap, crossing, jobs
         self.work, self.landing, self.summed = work, landing, summed
         self.slots = work.shape[0]
         (self.rs_s, self.rs_r, self.ag_s, self.ag_r, self.load_sem, self.store_sem) = sems
         self.count = crossing[0] + sum(job[2] for job in jobs)
+        self.beats = self.count + 2 * self.bits * gap + 2
 
     def step_of(self, odd, level):
         even_step = 1 << level
@@ -913,7 +1038,7 @@
     def step(self, tick, cross):
         bits = self.bits
         for age in reversed(range(-1, 2 * bits + 2)):
-            piece = tick - age
+            piece = tick - (age if age < 0 else min(age * self.gap, 2 * bits * self.gap + 1))
             safe = jnp.maximum(piece, 0)
             slot, odd = safe % self.slots, safe % 2
             plain = piece >= self.crossing[0]
@@ -992,6 +1117,8 @@
     chunks,
     hop,
     counts,
+    gap,
+    lag,
     gunit_ref,
     branch_ref,
     seg_ref,
@@ -1051,7 +1178,7 @@
         (gv_ref, gv_sum, counts[5]),
         (gpack_ref, gpack_sum, counts[6]),
     ]
-    pieces = Pieces(group, work.shape[1], (counts[0], gout_ref), jobs, work, landing, summed, piece_sems)
+    pieces = Pieces(group, work.shape[1], gap, (counts[0], gout_ref), jobs, work, landing, summed, piece_sems)
     bits = pieces.bits
     pieces.load_first()
     greet(
@@ -1059,23 +1186,25 @@
         + [{"dp": pieces.mine + (1 << bit) - 2 * (1 << bit) * ((pieces.mine // (1 << bit)) % 2)} for bit in range(bits)]
     )
 
-    def cross_copy(slot, odd, target, origin):
-        own = pieces.span(pieces.start_of(odd, bits), bits)
+    across, columns = cross_work.shape[0], work.shape[2]
+
+    def cross_copy(slot, column, target, origin):
+        own = pieces.span(pieces.start_of(column % 2, bits), bits)
         return pltpu.make_async_remote_copy(
             src_ref=work.at[slot, own],
-            dst_ref=cross_in.at[odd * size + origin],
-            send_sem=cross_s.at[odd * size + target],
-            recv_sem=cross_r.at[odd * size + origin],
+            dst_ref=cross_in.at[column * size + origin],
+            send_sem=cross_s.at[column * size + target],
+            recv_sem=cross_r.at[column * size + origin],
             device_id={"mp": target},
             device_id_type=pl.DeviceIdType.MESH,
         )
 
     def cross(piece, slot, odd, start):
-        target = piece // 2
+        target, column = piece // across, piece % across
 
         @pl.when(target != me)
         def _():
-            copy = cross_copy(slot, odd, target, me)
+            copy = cross_copy(slot, column, target, me)
             copy.start() if start else copy.wait_send()
 
         if start:
@@ -1083,38 +1212,41 @@
             @pl.when(target == me)
             def _():
                 own = pieces.span(pieces.start_of(odd, bits), bits)
-                cross_in[odd * size + me] = work[slot, own, :]
-
-    def tail_copy(odd):
-        columns = work.shape[2]
+                cross_in[column * size + me] = work[slot, own, :]
+
+    def tail_copy(column):
         return pltpu.make_async_copy(
-            cross_work.at[odd], gout_sum.at[0, :, odd * columns : (odd + 1) * columns], tail_store.at[odd]
+            cross_work.at[column],
+            gout_sum.at[0, :, column * columns : (column + 1) * columns],
+            tail_store.at[column],
         )
 
+    def tail_spread(column, level, arriving):
+        return pieces.spread_copy(cross_work, (tail_s, tail_r), column, column % 2, level, arriving)
+
     def tail_step(tick):
-        base = counts[0] + bits + 1
-        for odd in range(2):
-
-            @pl.when(tick == base + odd)
+        base = counts[0] + bits * gap + gap
+        for column in range(across):
+
+            @pl.when(tick == base + column)
             def _():
                 for offset in range(1, size):
-                    origin = lax.rem(me + offset, size)
-                    cross_copy(0, odd, me, origin).wait_recv()
-                own = pieces.span(pieces.start_of(odd, bits), bits)
-                cross_work[odd, own, :] = sum(
-                    cross_in[odd * size + index] for index in range(1, size)
-                ) + cross_in[odd * size]
-                pieces.spread_copy(cross_work, (tail_s, tail_r), odd, odd, bits - 1, False).start()
+                    cross_copy(0, column, me, lax.rem(me + offset, size)).wait_recv()
+                own = pieces.span(pieces.start_of(column % 2, bits), bits)
+                cross_work[column, own, :] = (
+                    sum(cross_in[column * size + index] for index in range(1, size)) + cross_in[column * size]
+                )
+                tail_spread(column, bits - 1, False).start()
 
             for level in reversed(range(bits)):
 
-                @pl.when(tick == base + odd + bits - level)
+                @pl.when(tick == base + column + (bits - level) * gap)
                 def _():
-                    pieces.spread_copy(cross_work, (tail_s, tail_r), odd, odd, level, True).wait_recv()
+                    tail_spread(column, level, True).wait_recv()
                     if level:
-                        pieces.spread_copy(cross_work, (tail_s, tail_r), odd, odd, level - 1, False).start()
+                        tail_spread(column, level - 1, False).start()
                     else:
-                        tail_copy(odd).start()
+                        tail_copy(column).start()
 
     def small_across(offset, arriving):
         origin = lax.rem(me - offset + size, size) if arriving else me
@@ -1168,7 +1300,7 @@
                 else:
                     small_sum[...] = value
 
-    def settle(chunk):
+    def settle_seg(chunk):
         slot = chunk * size + me
         line.scatter_sum(chunk, gunit_ref, seg_scatter, total)
         rows = seg_ref[slot].astype(f32)
@@ -1182,6 +1314,9 @@
         gseg_ref[slot] = low
         whole_seg[slot] = low.astype(f32)
         line.gather_start(chunk, whole_seg, seg_gather)
+
+    def settle_out(chunk):
+        slot = chunk * size + me
         line.scatter_sum(chunk, branch_ref, out_scatter, total)
         low = (res_ref[chunk] + total[...]).astype(bf16)
         result_ref[slot] = low
@@ -1195,18 +1330,23 @@
         result_ref[slot] = whole_out[slot].astype(bf16)
 
     settle_at = hop * line.reach
+    seg_lag, out_lag = max(-lag, 0), max(lag, 0)
 
     def step(tick, _):
-        line.scatter_step(tick, gunit_ref, seg_scatter)
-        line.scatter_step(tick, branch_ref, out_scatter)
-        chunk, due = line.chunk_at(tick - settle_at)
-
-        @pl.when(due)
-        def _():
-            settle(chunk)
-
-        line.gather_step(tick - settle_at, whole_seg, seg_gather, seg_landed)
-        line.gather_step(tick - settle_at, whole_out, out_gather, out_landed)
+        flows = (
+            (seg_lag, gunit_ref, seg_scatter, settle_seg, whole_seg, seg_gather, seg_landed),
+            (out_lag, branch_ref, out_scatter, settle_out, whole_out, out_gather, out_landed),
+        )
+        for late, part, scatter, settle, whole, gather, landed in flows:
+            line.scatter_step(tick - late, part, scatter)
+            chunk, due = line.chunk_at(tick - late - settle_at)
+
+            @pl.when(due)
+            def _():
+                settle(chunk)
+
+        for late, part, scatter, settle, whole, gather, landed in flows:
+            line.gather_step(tick - late - settle_at, whole, gather, landed)
         small_step(tick)
 
         def piece_step(beat, _):
@@ -1217,11 +1357,10 @@
         lax.fori_loop(beats(tick), beats(tick + 1), piece_step, 0)
         return 0
 
-    line_ticks = line.reach * (chunks - 1) + 2 * settle_at + 1
-    piece_ticks = pieces.count + 2 * bits + 1
+    line_ticks = line.reach * (chunks - 1) + 2 * settle_at + 1 + abs(lag)
 
     def beats(tick):
-        return jnp.minimum((tick * piece_ticks + line_ticks - 3) // (line_ticks - 2), piece_ticks)
+        return jnp.minimum((tick * pieces.beats + line_ticks - 3) // (line_ticks - 2), pieces.beats)
 
     lax.fori_loop(0, line_ticks, step, 0)
 
@@ -1233,10 +1372,10 @@
         return 0
 
     lax.fori_loop(0, chunks, drain, 0)
-    for odd in range(2):
+    for column in range(across):
         for level in range(bits):
-            pieces.spread_copy(cross_work, (tail_s, tail_r), odd, odd, level, False).wait_send()
-        tail_copy(odd).wait()
+            tail_spread(column, level, False).wait_send()
+        tail_copy(column).wait()
     for offset in range(1, size):
         small_across(offset, False).wait_send()
     for level in range(bits):
@@ -1248,9 +1387,9 @@
     piece = rows // (chunks * size)
     vmem = pl.BlockSpec(memory_space=pltpu.VMEM)
     whole = (chunks * size, piece, width)
-    piece_rows, columns = max(256, 8 * group), width // 2
+    piece_rows, columns, gap = max(256, 8 * group), width // 4, 2
     bits = group.bit_length() - 1
-    slots = 2 * bits + 2
+    slots = 2 * bits * gap + 2
     views = [grad.reshape(-1, piece_rows, grad.shape[1]) for grad in grads]
     counts = tuple(view.shape[0] * (view.shape[2] // columns) for view in views)
     anywhere = pl.BlockSpec(memory_space=pl.ANY)
@@ -1258,7 +1397,7 @@
     sums = [jax.ShapeDtypeStruct(view.shape, f32) for view in views]
     sums[0] = jax.ShapeDtypeStruct((1, piece_rows, width), f32)
     return pl.pallas_call(
-        functools.partial(close_kernel, size, group, chunks, 2, counts),
+        functools.partial(close_kernel, size, group, chunks, 2, counts, gap, 3),
         in_specs=[vmem] * 6 + [anywhere] * len(views) + [vmem],
         out_specs=[vmem] * 2 + [anywhere] * len(views) + [vmem],
         out_shape=[jax.ShapeDtypeStruct(whole, bf16)] * 2 + sums + [jax.ShapeDtypeStruct(small.shape, f32)],
@@ -1268,8 +1407,8 @@
             pltpu.VMEM((slots, piece_rows, columns), f32),
             pltpu.VMEM((slots, piece_rows, columns), f32),
             pltpu.VMEM((slots, piece_rows, columns), f32),
-            pltpu.VMEM((2 * size, piece_rows // group, columns), f32),
-            pltpu.VMEM((2, piece_rows, columns), f32),
+            pltpu.VMEM((width // columns * size, piece_rows // group, columns), f32),
+            pltpu.VMEM((width // columns, piece_rows, columns), f32),
             pltpu.VMEM((size, *small.shape), f32),
             pltpu.VMEM((bits, *small.shape), f32),
             pltpu.VMEM((bits, *small.shape), f32),
@@ -1277,9 +1416,9 @@
         + [dma((chunks * size,))] * 16
         + [dma((slots * bits,))] * 4
         + [dma((slots,))] * 2
-        + [dma((2 * size,))] * 2
-        + [dma((2 * bits,))] * 2
-        + [dma((2,))]
+        + [dma((width // columns * size,))] * 2
+        + [dma((width // columns * bits,))] * 2
+        + [dma((width // columns,))]
         + [dma((size,))] * 2
         + [dma((bits,))] * 2,
         compiler_params=pltpu.CompilerParams(
@@ -1324,19 +1463,9 @@
     streams, seg_len, width = inputs.shape
     mem_len = memory.shape[1]
     packed_len = compressed_memory.shape[1]
-    heads_here = relative_bias.shape[0]
     local = query_weight.shape[1]
-    compress_count = grad_compressed.shape[1]
     rows = streams * seg_len
-    slot_index = jnp.arange(mem_len, dtype=jnp.int32)
-    live_rows = jnp.where(
-        (slot_index[None, :] >= mem_len - memory_fill[:, None])[:, :, None], memory, jnp.zeros_like(memory)
-    )
-    evicted = live_rows.reshape(streams * compress_count, 2 * width)
-    packed_new = mm(evicted, compress_weight).astype(bf16).reshape(streams, compress_count, -1)
-    grad_pack = mm_t0(grad_compressed.reshape(streams * compress_count, -1), evicted)
-
-    unit, q, k, v, mixed, log_total = attend(
+    unit, q, k, v, mixed, log_total, packed_new, grad_pack, begun = attend(
         inputs,
         memory,
         compressed_memory,
@@ -1347,6 +1476,11 @@
         key_weight,
         value_weight,
         relative_bias,
+        compress_weight,
+        grad_compressed,
+        output_weight,
+        mp_size,
+        dp_size,
     )
     seg_rows = inputs.reshape(rows, width)
     grad_mixed, grad_residual, residual, branch, grad_down, grad_up, grad_out_full, grad_second = feed(
@@ -1355,14 +1489,14 @@
         grad_output.reshape(rows, width),
         up_weight,
         down_weight,
-        output_weight,
+        begun,
         second_gain,
         mp_size,
         dp_size,
         chunk_count,
     )
     grad_mixed = grad_mixed.reshape(streams, seg_len, local)
-    grad_unit, gq, gk, gv, rel = attend_back(
+    grad_unit, gq, gk, gv, small = attend_back(
         unit,
         q,
         k,
@@ -1375,16 +1509,11 @@
         key_weight,
         value_weight,
         relative_bias,
+        first_gain,
+        grad_second,
         mem_len,
         packed_len,
     )
-    grad_relative = jnp.sum(rel, axis=-1)[:, : len(reach_marks)]
-    local_first = sum(
-        jnp.sum(grad * weight.astype(f32).T, axis=0)
-        for grad, weight in ((gq, query_weight), (gk, key_weight), (gv, value_weight))
-    )
-    flat_relative = jnp.pad(grad_relative.reshape(-1), (0, width - grad_relative.size))
-    small = jnp.pad(jnp.stack([local_first / first_gain, grad_second[0], flat_relative]), ((0, 5), (0, 0)))
     result, grad_seg, grad_out_w, grad_up, grad_down, gq, gk, gv, grad_pack, small = close(
         grad_unit,
         branch,
@@ -1399,7 +1528,7 @@
         chunk_count,
     )
     grad_first, grad_second = small[0], small[1]
-    grad_relative = small[2, : grad_relative.size].reshape(grad_relative.shape)
+    grad_relative = small[2, : relative_bias.size].reshape(relative_bias.shape)
     result = result.reshape(inputs.shape)
     grad_seg = grad_seg.reshape(inputs.shape)
     grad_query_w = gq.reshape(local, width).T

time: 515 us -> 460 us (0.89)
  Pallas kernels: 470 us -> 436 us
  local copies, waits for them, and re-layouts: 32.3 us -> 22.8 us
  other arithmetic: 6.67 us -> 0 us
    pallas_call x2, Pallas kernels: 200 us -> 174 us  [the longest x1 144 us: feed(): pl.pallas_call(functools.partial(feed_kernel, size, group, chunks, 2, 0,...]
    pallas_call x1, Pallas kernels: 246 us -> 237 us  [close(): pl.pallas_call(functools.partial(close_kernel, size, group, chunks, 2, co...]
    unnamed x44 -> x26, local copies, waits for them, and re-layouts: 26 us -> 19.9 us
where the time goes in v3:
time: 460 us
  Pallas kernels  436 us (95%)
  local copies, waits for them, and re-layouts  22.8 us (5%)
    pallas_call x1, Pallas kernels, close(): pl.pallas_call(functools.partial(close_kernel, size, group, chunks, 2, co...  237 us
    pallas_call x1, Pallas kernels, feed(): pl.pallas_call(functools.partial(feed_kernel, size, group, chunks, 2, 0,...  144 us
    pallas_call x1, Pallas kernels, attend(): pl.pallas_call(functools.partial(attend_kernel, sizes, size, group), grid...  30.5 us
    pallas_call x1, Pallas kernels, attend_back(): pl.pallas_call(functools.partial(attend_back_kernel, sizes), grid=(stream...  24.2 us
    unnamed x26, local copies, waits for them, and re-layouts  19.9 us

profile of v3, /device:TPU:0, one launch (start us, length us, event | category | flops | bytes accessed | tf_op | source)
XLA Modules:
  0.0 459.5 jit_solution(534599251633967793)
XLA Ops:
  0.6 30.5 %attend.1 = (bf16[2,1536,1024]{2,1,0:T(8,128)(2,1)}, bf16[2,512,256]{2,1,0:T(8,128)(2,1)}, bf16[2,1536,256]{2,1,0:T(8,128)(2,1)}, bf16[2,1536,256]{2,1,0:T(8,128...) custom-call(s32[2]{0:T(128)} %memory_fill.3, ...), custom_call_target="tpu_custom_call" | custom-call | flops 6442450944 | bytes 17301504 | tf_op jit(solution)/shard_map/attend/pallas_call | solution.py:290
  31.1 143.8 %feed.1 = (bf16[32,32,256]{2,1,0:T(8,128)(2,1)}, f32[8,32,1024]{2,1,0:T(8,128)}, f32[8,32,1024]{2,1,0:T(8,128)}, f32[32,32,1024]{2,1,0:T(8,128)}, f32[1024,1024]...) custom-call(bf16[8,128,256]{2,1,0:T(8,128)(2,1)} %bitcast.46, ...), custom_call_target="tpu_custom_call" | custom-call | tf_op jit(solution)/shard_map/feed/pallas_call | solution.py:897
  175.0 24.2 %attend_back.1 = (f32[2,512,1024]{2,1,0:T(8,128)}, f32[256,1024]{1,0:T(8,128)}, f32[256,1024]{1,0:T(8,128)}, f32[256,1024]{1,0:T(8,128)}, f32[8,1024]{1,0:T(8,128)}) custom-call(s32[2]{0:T(128)} %memory_fill.3, s32[2]{0:T(128)} %packed_fill.3, f32[2,22]{1,0:T(2,128)} %bias_ref.3, bf16[2,1536,1024]{2,1,0:T(8,128)(2,1)} %get-tuple-element.45.unit_ref, ...), custom_call_target="tpu_custom_call" | custom-call | flops 10468982784 | bytes 11010048 | tf_op jit(solution)/shard_map/attend_back/pallas_call | solution.py:507
  199.2 237.5 %close.1 = (bf16[32,32,1024]{2,1,0:T(8,128)(2,1)}, bf16[32,32,1024]{2,1,0:T(8,128)(2,1)}, f32[1,256,1024]{2,1,0:T(8,128)}, f32[4,256,1024]{2,1,0:T(8,128)}, f32[...) custom-call(f32[32,32,1024]{2,1,0:T(8,128)} %bitcast.57, ...), custom_call_target="tpu_custom_call" | custom-call | flops 99999997952 | bytes 1000000000 | tf_op jit(solution)/shard_map/close/pallas_call | solution.py:1399
  436.7 0.0 copy-start.6
  436.7 0.8 slice_reduce_fusion
  437.5 1.4 fusion
  438.9 0.6 reshape_squeeze.3
  439.6 0.0 copy-start.5
  439.6 2.6 copy.30
  442.2 0.0 copy-done.6
  442.2 1.3 copy.31
  443.5 0.0 copy-done.5
  443.5 1.3 copy.32
  444.8 0.0 copy-start.3
  444.8 3.0 copy.33
  447.9 0.0 copy-done.3
  447.9 0.0 copy-start.7
  447.9 0.0 copy-start.2
  447.9 1.3 copy.40
  449.2 0.0 copy-done.7
  449.2 0.0 copy-start.4
  449.2 0.7 copy.41
  449.9 0.5 copy-done.2
  450.4 0.0 copy-start.1
  450.4 1.3 copy.42
  451.7 0.0 copy-done.4
  451.7 1.0 copy.43
  452.7 1.1 copy-done.1
  453.8 0.0 copy-start
  453.8 2.1 copy.44
  455.9 1.6 copy-done
  457.5 2.0 copy.45
Async XLA Ops:
  436.7 5.5 %copy-start.6 = (f32[1,256,1024]{2,1,0:T(8,128)S(1)}, f32[1,256,1024]{2,1,0:T(8,128)}, u32[]{:S(2)}) copy-start(f32[1,256,1024]{2,1,0:T(8,128)} %get-tuple-element.71) | copy-start | bytes 3145732
  439.6 3.9 copy-start.5
  444.8 3.0 copy-start.3
  447.9 1.3 copy-start.7
  447.9 2.5 copy-start.2
  449.2 2.5 copy-start.4
  450.4 3.4 copy-start.1
  453.8 3.7 copy-start

commit v4 on v3

--- a/solution.py
+++ b/solution.py
@@ -14,6 +14,7 @@
 block = 128
 query_block = 256
 chunk_count = 8
+early_chunks = 2
 f32 = jnp.float32
 bf16 = jnp.bfloat16
 
@@ -350,8 +351,143 @@
     )(memory_fill, packed_fill, bias, inputs, memory, packed, gain[None, :], wq, wk, wv, wc, gcomp, wo)
 
 
+class Line:
+    def __init__(self, size, chunks, hop):
+        self.me = lax.axis_index("mp")
+        self.size, self.chunks, self.hop = size, chunks, hop
+        self.reach = size - 1
+
+    def place(self, right):
+        return self.me if right else self.reach - self.me
+
+    def peer(self, right):
+        return {"mp": self.me + 1 if right else self.me - 1}
+
+    def copy(self, source, target, sems, slot, right):
+        return pltpu.make_async_remote_copy(
+            src_ref=source.at[slot],
+            dst_ref=target.at[slot],
+            send_sem=sems[0],
+            recv_sem=sems[1].at[slot],
+            device_id=self.peer(right),
+            device_id_type=pl.DeviceIdType.MESH,
+        )
+
+    def chunk_at(self, tick):
+        positive = jnp.maximum(tick, 0)
+        chunk = positive // self.reach
+        return chunk, (tick >= 0) & (positive == chunk * self.reach) & (chunk < self.chunks)
+
+    def scatter_step(self, tick, part, lanes, first=0):
+        for right, held, sems in lanes:
+            place = self.place(right)
+            late = tick - self.hop * place
+            positive = jnp.maximum(late, 0)
+            chunk = positive // self.reach
+            goal = self.reach - (positive - self.reach * chunk)
+            active = (late >= 0) & (chunk >= first) & (chunk < self.chunks) & (goal > place)
+            slot = chunk * self.size + (goal if right else self.reach - goal)
+
+            @pl.when(active & (place == 0))
+            def _():
+                self.copy(part, held, sems, slot, right).start()
+
+            @pl.when(active & (place > 0))
+            def _():
+                self.copy(held, held, sems, slot, right).wait_recv()
+                held[slot] = held[slot] + part[slot]
+                self.copy(held, held, sems, slot, right).start()
+
+    def scatter_sum(self, chunk, part, lanes, total):
+        slot = chunk * self.size + self.me
+        total[...] = part[slot]
+        for right, held, sems in lanes:
+
+            @pl.when(self.place(right) > 0)
+            def _():
+                self.copy(held, held, sems, slot, right).wait_recv()
+                total[...] = total[...] + held[slot]
+
+    def gather_start(self, chunk, whole, lanes):
+        slot = chunk * self.size + self.me
+        for right, sems in lanes:
+
+            @pl.when(self.place(right) < self.reach)
+            def _():
+                self.copy(whole, whole, sems, slot, right).start()
+
+    def gather_step(self, tick, whole, lanes, landed=None):
+        for right, sems in lanes:
+            place = self.place(right)
+            for distance in range(1, self.size):
+                chunk, due = self.chunk_at(tick - self.hop * distance)
+
+                @pl.when(due & (distance <= place))
+                def _():
+                    slot = chunk * self.size + (self.me - distance if right else self.me + distance)
+                    self.copy(whole, whole, sems, slot, right).wait_recv()
+
+                    @pl.when(place < self.reach)
+                    def _():
+                        self.copy(whole, whole, sems, slot, right).start()
+
+                    if landed is not None:
+                        landed(slot)
+
+    def sent(self, buffer, send_sem, count, right):
+        some = buffer.at[pl.ds(0, count)]
+        return pltpu.make_async_remote_copy(
+            src_ref=some,
+            dst_ref=some,
+            send_sem=send_sem,
+            recv_sem=send_sem,
+            device_id=self.peer(right),
+            device_id_type=pl.DeviceIdType.MESH,
+        )
+
+    def scatter_drain(self, part, lanes, first=0):
+        for right, held, sems in lanes:
+            for place in range(self.reach):
+
+                @pl.when(self.place(right) == place)
+                def _():
+                    self.sent(part, sems[0], (self.reach - place) * (self.chunks - first), right).wait_send()
+
+    def gather_drain(self, whole, lanes):
+        for right, sems in lanes:
+            for place in range(self.reach):
+
+                @pl.when(self.place(right) == place)
+                def _():
+                    self.sent(whole, sems[0], (place + 1) * self.chunks, right).wait_send()
+
+
+def meet(line):
+    barrier = pltpu.get_barrier_semaphore()
+    for right in (True, False):
+
+        @pl.when(line.place(right) < line.reach)
+        def _():
+            pl.semaphore_signal(
+                barrier, inc=1, device_id=line.peer(right), device_id_type=pl.DeviceIdType.MESH
+            )
+
+    inner = (line.me > 0) & (line.me < line.reach)
+
+    @pl.when(inner)
+    def _():
+        pl.semaphore_wait(barrier, 2)
+
+    @pl.when(jnp.logical_not(inner))
+    def _():
+        pl.semaphore_wait(barrier, 1)
+
+
 def attend_back_kernel(
     sizes,
+    size,
+    early,
+    hop,
     memory_fill,
     packed_fill,
     bias_ref,
@@ -366,11 +502,14 @@
     wv_ref,
     gain_ref,
     gsecond_ref,
+    branch_hbm,
+    res_hbm,
     gunit_ref,
     gq_ref,
     gk_ref,
     gv_ref,
     small_ref,
+    early_ref,
     strip,
     live,
     dk_sum,
@@ -379,6 +518,15 @@
     dk_low,
     dv_low,
     strip_sum,
+    branch_ref,
+    res_ref,
+    held_right,
+    held_left,
+    total_ref,
+    load_sem,
+    line_s,
+    right_r,
+    left_r,
 ):
     seg_len, mem_len, packed_len, heads, head_dim = sizes
     kept = mem_len + packed_len
@@ -386,8 +534,38 @@
     stream = pl.program_id(0)
     scale = 1.0 / math.sqrt(head_dim)
 
+    line = Line(size, early, hop)
+    lanes_out = ((True, held_right, (line_s.at[0], right_r)), (False, held_left, (line_s.at[1], left_r)))
+    loads = (
+        pltpu.make_async_copy(branch_hbm.at[pl.ds(0, early * size)], branch_ref, load_sem.at[0]),
+        pltpu.make_async_copy(res_hbm.at[pl.ds(0, early)], res_ref, load_sem.at[1]),
+    )
+    ticks = line.reach * (early - 1) + hop * line.reach + 1
+    spans = heads * (seg_len // query_block)
+
+    def line_step(tick, _):
+        line.scatter_step(tick, branch_ref, lanes_out)
+        chunk, due = line.chunk_at(tick - hop * line.reach)
+
+        @pl.when(due)
+        def _():
+            line.scatter_sum(chunk, branch_ref, lanes_out, total_ref)
+            early_ref[chunk] = (res_ref[chunk] + total_ref[...]).astype(bf16).astype(f32)
+
+        return 0
+
+    def line_span(index):
+        unit = stream * spans + index
+        every = spans * pl.num_programs(0)
+        lax.fori_loop((unit * ticks) // every, ((unit + 1) * ticks) // every, line_step, 0)
+
     @pl.when(stream == 0)
     def _():
+        for load in loads:
+            load.start()
+        meet(line)
+        for load in loads:
+            load.wait()
         strip_sum[...] = jnp.zeros_like(strip_sum)
         gq_ref[...] = jnp.zeros_like(gq_ref)
         gk_ref[...] = jnp.zeros_like(gk_ref)
@@ -402,6 +580,7 @@
                 bias_ref, head, diagonal_of(seg_len, kept, column), True
             )
         for index in range(seg_len // query_block):
+            line_span(head * (seg_len // query_block) + index)
             reach = kept + (index + 1) * query_block
             rows = slice(index * query_block, (index + 1) * query_block)
             queries = q_ref[0, rows, lanes]
@@ -455,6 +634,7 @@
 
     @pl.when(stream == pl.num_programs(0) - 1)
     def _():
+        line.scatter_drain(branch_ref, lanes_out)
         rows = lax.broadcasted_iota(jnp.int32, (block, block), 0)
         cols = lax.broadcasted_iota(jnp.int32, (block, block), 1)
         width = gain_ref.shape[1]
@@ -488,7 +668,8 @@
 
 
 def attend_back(
-    unit, q, k, v, log_total, grad_mixed, memory_fill, packed_fill, wq, wk, wv, bias, gain, grad_second, mem_len, packed_len
+    unit, q, k, v, log_total, grad_mixed, memory_fill, packed_fill, wq, wk, wv, bias, gain, grad_second, mem_len, packed_len,
+    branch, residual, size, early,
 ):
     streams, keys, width = unit.shape
     seg_len, local = q.shape[1:]
@@ -497,6 +678,7 @@
     sizes = (seg_len, mem_len, packed_len, heads, local // heads)
     smem = pl.BlockSpec(memory_space=pltpu.SMEM)
     strip_len = diagonal_count(seg_len, kept) * block
+    part = (early * size, *branch.shape[1:])
 
     def rows_of(count, columns):
         return pl.BlockSpec((1, count, columns), lambda s: (s, 0, 0))
@@ -505,7 +687,7 @@
         return pl.BlockSpec(shape, lambda s: (0,) * len(shape))
 
     return pl.pallas_call(
-        functools.partial(attend_back_kernel, sizes),
+        functools.partial(attend_back_kernel, sizes, size, early, 2),
         grid=(streams,),
         in_specs=[
             smem,
@@ -522,6 +704,8 @@
             whole(wv.shape),
             whole((1, width)),
             whole((1, width)),
+            pl.BlockSpec(memory_space=pl.ANY),
+            pl.BlockSpec(memory_space=pl.ANY),
         ],
         out_specs=[
             rows_of(seg_len, width),
@@ -529,6 +713,7 @@
             whole((local, width)),
             whole((local, width)),
             whole((8, width)),
+            whole((early, *residual.shape[1:])),
         ],
         out_shape=[
             jax.ShapeDtypeStruct((streams, seg_len, width), f32),
@@ -536,6 +721,7 @@
             jax.ShapeDtypeStruct((local, width), f32),
             jax.ShapeDtypeStruct((local, width), f32),
             jax.ShapeDtypeStruct((8, width), f32),
+            jax.ShapeDtypeStruct((early, *residual.shape[1:]), f32),
         ],
         scratch_shapes=[
             pltpu.VMEM((strip_len, block), f32),
@@ -546,8 +732,19 @@
             pltpu.VMEM((keys, local), bf16),
             pltpu.VMEM((keys, local), bf16),
             pltpu.VMEM((heads, strip_len, block), f32),
+            pltpu.VMEM(part, f32),
+            pltpu.VMEM((early, *part[1:]), f32),
+            pltpu.VMEM(part, f32),
+            pltpu.VMEM(part, f32),
+            pltpu.VMEM(part[1:], f32),
+            pltpu.SemaphoreType.DMA((2,)),
+            pltpu.SemaphoreType.DMA((2,)),
+            pltpu.SemaphoreType.DMA((early * size,)),
+            pltpu.SemaphoreType.DMA((early * size,)),
         ],
-        compiler_params=pltpu.CompilerParams(vmem_limit_bytes=60 << 20),
+        compiler_params=pltpu.CompilerParams(
+            collective_id=3, has_side_effects=True, vmem_limit_bytes=60 << 20
+        ),
         cost_estimate=pl.CostEstimate(
             flops=streams * (8 * keys * width * local + 10 * seg_len * keys * local),
             bytes_accessed=streams * keys * (width * 2 + local * 6),
@@ -569,114 +766,9 @@
         wv,
         gain[None, :],
         grad_second,
+        branch,
+        residual,
     )
-
-
-def remote(source, target, send_sems, recv_sems, source_slot, target_slot, send_slot, recv_slot, peer):
-    return pltpu.make_async_remote_copy(
-        src_ref=source.at[source_slot],
-        dst_ref=target.at[target_slot],
-        send_sem=send_sems.at[send_slot],
-        recv_sem=recv_sems.at[recv_slot],
-        device_id=peer,
-        device_id_type=pl.DeviceIdType.MESH,
-    )
-
-
-class Line:
-    def __init__(self, size, chunks, hop):
-        self.me = lax.axis_index("mp")
-        self.size, self.chunks, self.hop = size, chunks, hop
-        self.reach = size - 1
-
-    def place(self, right):
-        return self.me if right else self.reach - self.me
-
-    def peer(self, right):
-        return {"mp": self.me + 1 if right else self.me - 1}
-
-    def copy(self, source, target, sems, slot, right):
-        return remote(source, target, sems[0], sems[1], slot, slot, slot, slot, self.peer(right))
-
-    def chunk_at(self, tick):
-        positive = jnp.maximum(tick, 0)
-        chunk = positive // self.reach
-        return chunk, (tick >= 0) & (positive == chunk * self.reach) & (chunk < self.chunks)
-
-    def scatter_step(self, tick, part, lanes):
-        for right, held, sems in lanes:
-            place = self.place(right)
-            late = tick - self.hop * place
-            positive = jnp.maximum(late, 0)
-            chunk = positive // self.reach
-            goal = self.reach - (positive - self.reach * chunk)
-            active = (late >= 0) & (chunk < self.chunks) & (goal > place)
-            slot = chunk * self.size + (goal if right else self.reach - goal)
-
-            @pl.when(active & (place == 0))
-            def _():
-                self.copy(part, held, sems, slot, right).start()
-
-            @pl.when(active & (place > 0))
-            def _():
-                self.copy(held, held, sems, slot, right).wait_recv()
-                held[slot] = held[slot] + part[slot]
-                self.copy(held, held, sems, slot, right).start()
-
-    def scatter_sum(self, chunk, part, lanes, total):
-        slot = chunk * self.size + self.me
-        total[...] = part[slot]
-        for right, held, sems in lanes:
-
-            @pl.when(self.place(right) > 0)
-            def _():
-                self.copy(held, held, sems, slot, right).wait_recv()
-                total[...] = total[...] + held[slot]
-
-    def gather_start(self, chunk, whole, lanes):
-        slot = chunk * self.size + self.me
-        for right, sems in lanes:
-
-            @pl.when(self.place(right) < self.reach)
-            def _():
-                self.copy(whole, whole, sems, slot, right).start()
-
-    def gather_step(self, tick, whole, lanes, landed=None):
-        for right, sems in lanes:
-            place = self.place(right)
-            for distance in range(1, self.size):
-                chunk, due = self.chunk_at(tick - self.hop * distance)
-
-                @pl.when(due & (distance <= place))
-                def _():
-                    slot = chunk * self.size + (self.me - distance if right else self.me + distance)
-                    self.copy(whole, whole, sems, slot, right).wait_recv()
-
-                    @pl.when(place < self.reach)
-                    def _():
-                        self.copy(whole, whole, sems, slot, right).start()
-
-                    if landed is not None:
-                        landed(slot)
-
-    def scatter_drain(self, chunk, part, lanes):
-        for right, held, sems in lanes:
-            for goal in range(1, self.size):
-
-                @pl.when(goal > self.place(right))
-                def _():
-                    slot = chunk * self.size + (goal if right else self.reach - goal)
-                    self.copy(part, held, sems, slot, right).wait_send()
-
-    def gather_drain(self, chunk, whole, lanes):
-        for right, sems in lanes:
-            place = self.place(right)
-            for distance in range(self.size):
-
-                @pl.when((distance <= place) & (place < self.reach))
-                def _():
-                    slot = chunk * self.size + (self.me - distance if right else self.me + distance)
-                    self.copy(whole, whole, sems, slot, right).wait_send()
 
 
 def feed_kernel(
@@ -687,20 +779,31 @@
     delay,
     beat,
     mixed_ref,
-    seg_ref,
-    grad_ref,
-    up_ref,
-    down_ref,
+    seg_hbm,
+    grad_hbm,
+    up_hbm,
+    down_hbm,
     begun_ref,
     gain_ref,
     gm_ref,
     gres_ref,
     res_ref,
+    branch_hbm,
+    gdown_hbm,
+    gup_hbm,
+    gout_hbm,
+    gsecond_ref,
+    seg_ref,
+    grad_ref,
+    up_ref,
+    down_ref,
     branch_ref,
     gdown_ref,
     gup_ref,
     gout_ref,
-    gsecond_ref,
+    acted,
+    graded,
+    normed_low,
     heads_in,
     part,
     held_right,
@@ -717,9 +820,17 @@
 ):
     line = Line(size, chunks, hop)
     me = line.me
-    (hr_s, hr_r, hl_s, hl_r, sr_s, sr_r, sl_s, sl_r, x_s, x_r, wd_s, wd_r) = sems
-    gather_lanes = ((True, (hr_s, hr_r)), (False, (hl_s, hl_r)))
-    scatter_lanes = ((True, held_right, (sr_s, sr_r)), (False, held_left, (sl_s, sl_r)))
+    (line_s, hr_r, hl_r, sr_r, sl_r, swap_sem, wd_s, wd_r, load_sem, save_sem, branch_sem) = sems
+    gather_lanes = ((True, (line_s.at[0], hr_r)), (False, (line_s.at[1], hl_r)))
+    scatter_lanes = ((True, held_right, (line_s.at[2], sr_r)), (False, held_left, (line_s.at[3], sl_r)))
+    loads = [
+        pltpu.make_async_copy(source, target, load_sem.at[index])
+        for index, (source, target) in enumerate(
+            ((seg_hbm, seg_ref), (grad_hbm, grad_ref), (up_hbm, up_ref), (down_hbm, down_ref))
+        )
+    ]
+    for load in loads:
+        load.start()
     spread = Spread(size, group, weights_in, (None, None, wd_s, wd_r))
     bits = spread.bits
     piece, columns = weights_in.shape[3:]
@@ -783,24 +894,49 @@
         grad_pre = (slope * mm_t1(grads, down_ref[...])).astype(bf16)
         first = pl.ds(chunk * size, size)
         part[first] = mm_t1(grad_pre, up_ref[...]).reshape(size, rows, width)
-        branch_ref[first] = mm(activated, down_ref[...]).reshape(size, rows, width)
-        gdown_ref[...] += mm_t0(activated, grads)
-        gup_ref[...] += mm_t0(ffn_input, grad_pre)
-
-    def swap(chunk, offset, arriving):
+        acted[...] = activated
+        graded[...] = grad_pre
+        normed_low[...] = ffn_input
+
+    def save_branch(chunk):
+        here = pl.ds(chunk * size, size)
+        return pltpu.make_async_copy(branch_ref.at[here], branch_hbm.at[here], branch_sem.at[chunk])
+
+    def feed_branch(chunk):
+        branch_ref[pl.ds(chunk * size, size)] = mm(acted[...], down_ref[...]).reshape(size, rows, width)
+        save_branch(chunk).start()
+        gdown_ref[...] += mm_t0(acted[...], grad_ref[chunk])
+
+    def feed_grads(chunk):
+        gup_ref[...] += mm_t0(normed_low[...], graded[...])
+
+    saves = [
+        pltpu.make_async_copy(source, target, save_sem.at[index])
+        for index, (source, target) in enumerate(
+            ((gdown_ref, gdown_hbm), (gup_ref, gup_hbm), (gout_ref, gout_hbm))
+        )
+    ]
+
+    def swap(chunk, offset):
         target = lax.rem(me + offset, size)
-        origin = lax.rem(me - offset + size, size)
-        landing = chunk * size + (origin if arriving else me)
-        return remote(
-            swap_out,
-            swap_in,
-            x_s,
-            x_r,
-            chunk * size + target,
-            landing,
-            chunk * size + target,
-            landing,
-            {"mp": target},
+        return pltpu.make_async_remote_copy(
+            src_ref=swap_out.at[chunk * size + target],
+            dst_ref=swap_in.at[chunk * size + me],
+            send_sem=swap_sem.at[0],
+            recv_sem=swap_sem.at[1],
+            device_id={"mp": target},
+            device_id_type=pl.DeviceIdType.MESH,
+        )
+
+    def all_swaps():
+        some = pl.ds(0, chunks * (size - 1))
+        return pltpu.make_async_remote_copy(
+            src_ref=swap_out.at[some],
+            dst_ref=swap_in.at[some],
+            send_sem=swap_sem.at[0],
+            recv_sem=swap_sem.at[1],
+            device_id=spread.others(1),
+            device_id_type=pl.DeviceIdType.MESH,
         )
 
     def settle(chunk):
@@ -822,7 +958,7 @@
         for index in range(size):
             swap_out[chunk * size + index] = grad_mixed[:, index * local : (index + 1) * local]
         for offset in range(1, size):
-            swap(chunk, offset, False).start()
+            swap(chunk, offset).start()
 
     feed_at = hop * line.reach + delay
 
@@ -832,6 +968,8 @@
         @pl.when(tick == feed_at)
         def _():
             weight_finish()
+            for load in loads:
+                load.wait()
 
         chunk, due = line.chunk_at(tick)
 
@@ -847,6 +985,18 @@
             feed_chunk(chunk_f)
 
         line.scatter_step(tick - feed_at, part, scatter_lanes)
+        for late, work in ((1, feed_branch), (2, feed_grads)):
+            chunk_w, due_w = line.chunk_at(tick - feed_at - late)
+
+            @pl.when(due_w)
+            def _():
+                work(chunk_w)
+
+        @pl.when(tick == feed_at + line.reach * (chunks - 1) + 3)
+        def _():
+            for save in saves[:2]:
+                save.start()
+
         chunk_s, due_s = line.chunk_at(tick - feed_at - hop * line.reach)
 
         @pl.when(due_s)
@@ -860,9 +1010,11 @@
         own_mixed[...].reshape(chunks * rows, width), own_grad[...].reshape(chunks * rows, width)
     )
 
+    saves[2].start()
+    all_swaps().wait_recv()
+
     def finish(chunk, _):
-        for offset in range(1, size):
-            swap(chunk, offset, True).wait_recv()
+        save_branch(chunk).wait()
         for index in range(size):
 
             @pl.when(index == me)
@@ -873,13 +1025,14 @@
             def _():
                 gm_ref[chunk * size + index] = swap_in[chunk * size + index].astype(bf16)
 
-        line.gather_drain(chunk, heads_in, gather_lanes)
-        line.scatter_drain(chunk, part, scatter_lanes)
-        for offset in range(1, size):
-            swap(chunk, offset, False).wait_send()
         return 0
 
     lax.fori_loop(0, chunks, finish, 0)
+    line.gather_drain(heads_in, gather_lanes)
+    line.scatter_drain(part, scatter_lanes)
+    all_swaps().wait_send()
+    for save in saves:
+        save.wait()
     for half in range(2):
         for level in range(1, bits):
             spread.within(half, level, False).wait_send()
@@ -892,12 +1045,14 @@
     piece = chunk // size
     hidden = up.shape[1]
     vmem = pl.BlockSpec(memory_space=pltpu.VMEM)
-    slots = pltpu.SemaphoreType.DMA((chunks * size,))
+    anywhere = pl.BlockSpec(memory_space=pl.ANY)
+    dma = pltpu.SemaphoreType.DMA
+    slots = dma((chunks * size,))
     bits = group.bit_length() - 1
     return pl.pallas_call(
         functools.partial(feed_kernel, size, group, chunks, 2, 0, 4),
-        in_specs=[vmem] * 7,
-        out_specs=[vmem] * 8,
+        in_specs=[vmem] + [anywhere] * 4 + [vmem] * 2,
+        out_specs=[vmem] * 3 + [anywhere] * 4 + [vmem],
         out_shape=[
             jax.ShapeDtypeStruct((chunks * size, piece, local), bf16),
             jax.ShapeDtypeStruct((chunks, piece, width), f32),
@@ -909,6 +1064,17 @@
             jax.ShapeDtypeStruct((1, width), f32),
         ],
         scratch_shapes=[
+            pltpu.VMEM((chunks, chunk, width), bf16),
+            pltpu.VMEM((chunks, chunk, width), bf16),
+            pltpu.VMEM(up.shape, bf16),
+            pltpu.VMEM(down.shape, bf16),
+            pltpu.VMEM((chunks * size, piece, width), f32),
+            pltpu.VMEM((hidden, width), f32),
+            pltpu.VMEM((width, hidden), f32),
+            pltpu.VMEM((width, width), f32),
+            pltpu.VMEM((chunk, hidden), bf16),
+            pltpu.VMEM((chunk, hidden), bf16),
+            pltpu.VMEM((chunk, width), bf16),
             pltpu.VMEM((chunks * size, chunk, local), f32),
             pltpu.VMEM((chunks * size, piece, width), f32),
             pltpu.VMEM((chunks * size, piece, width), f32),
@@ -922,8 +1088,9 @@
             pltpu.VMEM((chunks, piece, width), bf16),
             pltpu.VMEM((chunks, piece, width), bf16),
         ]
-        + [slots] * 10
-        + [pltpu.SemaphoreType.DMA((2 * bits,))] * 2,
+        + [dma((4,))]
+        + [slots] * 4
+        + [dma((2,)), dma((2 * bits,)), dma((2 * bits,)), dma((4,)), dma((3,)), dma((chunks,))],
         compiler_params=pltpu.CompilerParams(
             collective_id=0, has_side_effects=True, vmem_limit_bytes=63 << 20
         ),
@@ -1118,13 +1285,14 @@
     hop,
     counts,
     gap,
-    lag,
-    gunit_ref,
-    branch_ref,
-    seg_ref,
-    gres_ref,
-    res_ref,
+    early,
+    gunit_hbm,
+    branch_hbm,
+    seg_hbm,
+    gres_hbm,
+    res_hbm,
     gain_ref,
+    early_ref,
     gout_ref,
     gup_ref,
     gdown_ref,
@@ -1143,6 +1311,11 @@
     gv_sum,
     gpack_sum,
     small_sum,
+    gunit_ref,
+    branch_ref,
+    seg_ref,
+    gres_ref,
+    res_ref,
     whole_seg,
     whole_out,
     seg_right,
@@ -1162,14 +1335,30 @@
 ):
     line = Line(size, chunks, hop)
     me = line.me
-    pairs = [sems[2 * index : 2 * index + 2] for index in range(8)]
-    seg_scatter = ((True, seg_right, pairs[0]), (False, seg_left, pairs[1]))
-    out_scatter = ((True, out_right, pairs[2]), (False, out_left, pairs[3]))
-    seg_gather = ((True, pairs[4]), (False, pairs[5]))
-    out_gather = ((True, pairs[6]), (False, pairs[7]))
-    piece_sems = sems[16:22]
-    cross_s, cross_r, tail_s, tail_r, tail_store = sems[22:27]
-    mix_s, mix_r, small_s, small_r = sems[27:31]
+    line_s, recvs, sems = sems[0], sems[1:9], sems[9:]
+    seg_scatter = ((True, seg_right, (line_s.at[0], recvs[0])), (False, seg_left, (line_s.at[1], recvs[1])))
+    out_scatter = ((True, out_right, (line_s.at[2], recvs[2])), (False, out_left, (line_s.at[3], recvs[3])))
+    seg_gather = ((True, (line_s.at[4], recvs[4])), (False, (line_s.at[5], recvs[5])))
+    out_gather = ((True, (line_s.at[6], recvs[6])), (False, (line_s.at[7], recvs[7])))
+    piece_sems = sems[:6]
+    cross_s, cross_r, tail_s, tail_r, tail_store = sems[6:11]
+    mix_s, mix_r, small_s, small_r = sems[11:15]
+    seg_load, out_load, load_sem = sems[15:18]
+    loads = [
+        pltpu.make_async_copy(source, target, load_sem.at[index])
+        for index, (source, target) in enumerate(((seg_hbm, seg_ref), (gres_hbm, gres_ref), (res_hbm, res_ref)))
+    ]
+
+    def part_load(source, target, load, chunk):
+        here = pl.ds(chunk * size, size)
+        return pltpu.make_async_copy(source.at[here], target.at[here], load.at[chunk])
+
+    for chunk in range(chunks):
+        part_load(gunit_hbm, gunit_ref, seg_load, chunk).start()
+        if chunk >= early:
+            part_load(branch_hbm, branch_ref, out_load, chunk).start()
+    for load in loads:
+        load.start()
     jobs = [
         (gup_ref, gup_sum, counts[1]),
         (gdown_ref, gdown_sum, counts[2]),
@@ -1317,8 +1506,17 @@
 
     def settle_out(chunk):
         slot = chunk * size + me
-        line.scatter_sum(chunk, branch_ref, out_scatter, total)
-        low = (res_ref[chunk] + total[...]).astype(bf16)
+
+        @pl.when(chunk < early)
+        def _():
+            total[...] = early_ref[jnp.minimum(chunk, early - 1)]
+
+        @pl.when(chunk >= early)
+        def _():
+            line.scatter_sum(chunk, branch_ref, out_scatter, total)
+            total[...] = res_ref[chunk] + total[...]
+
+        low = total[...].astype(bf16)
         result_ref[slot] = low
         whole_out[slot] = low.astype(f32)
         line.gather_start(chunk, whole_out, out_gather)
@@ -1330,22 +1528,35 @@
         result_ref[slot] = whole_out[slot].astype(bf16)
 
     settle_at = hop * line.reach
-    seg_lag, out_lag = max(-lag, 0), max(lag, 0)
+    seg_lag, out_lag = 0, -line.reach * early
 
     def step(tick, _):
         flows = (
-            (seg_lag, gunit_ref, seg_scatter, settle_seg, whole_seg, seg_gather, seg_landed),
-            (out_lag, branch_ref, out_scatter, settle_out, whole_out, out_gather, out_landed),
-        )
-        for late, part, scatter, settle, whole, gather, landed in flows:
-            line.scatter_step(tick - late, part, scatter)
+            (seg_lag, gunit_hbm, seg_load, gunit_ref, seg_scatter, settle_seg, whole_seg, seg_gather, seg_landed),
+            (out_lag, branch_hbm, out_load, branch_ref, out_scatter, settle_out, whole_out, out_gather, out_landed),
+        )
+        @pl.when(tick == 0)
+        def _():
+            for load in loads:
+                load.wait()
+
+        for late, source, load, part, scatter, settle, whole, gather, landed in flows:
+            fresh, new = line.chunk_at(tick - late)
+
+            first = early if late < 0 else 0
+
+            @pl.when(new & (fresh >= first))
+            def _():
+                part_load(source, part, load, fresh).wait()
+
+            line.scatter_step(tick - late, part, scatter, first)
             chunk, due = line.chunk_at(tick - late - settle_at)
 
             @pl.when(due)
             def _():
                 settle(chunk)
 
-        for late, part, scatter, settle, whole, gather, landed in flows:
+        for late, source, load, part, scatter, settle, whole, gather, landed in flows:
             line.gather_step(tick - late - settle_at, whole, gather, landed)
         small_step(tick)
 
@@ -1357,21 +1568,17 @@
         lax.fori_loop(beats(tick), beats(tick + 1), piece_step, 0)
         return 0
 
-    line_ticks = line.reach * (chunks - 1) + 2 * settle_at + 1 + abs(lag)
+    line_ticks = line.reach * (chunks - 1) + 2 * settle_at + 1
 
     def beats(tick):
-        return jnp.minimum((tick * pieces.beats + line_ticks - 3) // (line_ticks - 2), pieces.beats)
+        return jnp.minimum((tick * pieces.beats) // (line_ticks - 5), pieces.beats)
 
     lax.fori_loop(0, line_ticks, step, 0)
 
-    def drain(chunk, _):
-        line.scatter_drain(chunk, gunit_ref, seg_scatter)
-        line.scatter_drain(chunk, branch_ref, out_scatter)
-        line.gather_drain(chunk, whole_seg, seg_gather)
-        line.gather_drain(chunk, whole_out, out_gather)
-        return 0
-
-    lax.fori_loop(0, chunks, drain, 0)
+    line.scatter_drain(gunit_ref, seg_scatter)
+    line.scatter_drain(branch_ref, out_scatter, early)
+    line.gather_drain(whole_seg, seg_gather)
+    line.gather_drain(whole_out, out_gather)
     for column in range(across):
         for level in range(bits):
             tail_spread(column, level, False).wait_send()
@@ -1382,12 +1589,14 @@
         small_within(level).wait_send()
 
 
-def close(grad_unit, branch, seg_rows, grad_residual, residual, gain, grads, small, size, group, chunks):
+def close(
+    grad_unit, branch, seg_rows, grad_residual, residual, gain, early, grads, small, size, group, chunks
+):
     rows, width = seg_rows.shape
     piece = rows // (chunks * size)
     vmem = pl.BlockSpec(memory_space=pltpu.VMEM)
     whole = (chunks * size, piece, width)
-    piece_rows, columns, gap = max(256, 8 * group), width // 4, 2
+    piece_rows, columns, gap = max(256, 8 * group), width // 4, 3 if group <= 8 else 2
     bits = group.bit_length() - 1
     slots = 2 * bits * gap + 2
     views = [grad.reshape(-1, piece_rows, grad.shape[1]) for grad in grads]
@@ -1397,11 +1606,17 @@
     sums = [jax.ShapeDtypeStruct(view.shape, f32) for view in views]
     sums[0] = jax.ShapeDtypeStruct((1, piece_rows, width), f32)
     return pl.pallas_call(
-        functools.partial(close_kernel, size, group, chunks, 2, counts, gap, 3),
-        in_specs=[vmem] * 6 + [anywhere] * len(views) + [vmem],
+        functools.partial(close_kernel, size, group, chunks, 2, counts, gap, early.shape[0]),
+        in_specs=[anywhere] * 5 + [vmem] * 2 + [anywhere] * len(views) + [vmem],
         out_specs=[vmem] * 2 + [anywhere] * len(views) + [vmem],
         out_shape=[jax.ShapeDtypeStruct(whole, bf16)] * 2 + sums + [jax.ShapeDtypeStruct(small.shape, f32)],
-        scratch_shapes=[pltpu.VMEM(whole, f32)] * 6
+        scratch_shapes=[pltpu.VMEM(whole, f32)] * 2
+        + [
+            pltpu.VMEM(whole, bf16),
+            pltpu.VMEM(grad_residual.shape, f32),
+            pltpu.VMEM(grad_residual.shape, f32),
+        ]
+        + [pltpu.VMEM(whole, f32)] * 6
         + [
             pltpu.VMEM((piece, width), f32),
             pltpu.VMEM((slots, piece_rows, columns), f32),
@@ -1413,14 +1628,17 @@
             pltpu.VMEM((bits, *small.shape), f32),
             pltpu.VMEM((bits, *small.shape), f32),
         ]
-        + [dma((chunks * size,))] * 16
+        + [dma((8,))]
+        + [dma((chunks * size,))] * 8
         + [dma((slots * bits,))] * 4
         + [dma((slots,))] * 2
         + [dma((width // columns * size,))] * 2
         + [dma((width // columns * bits,))] * 2
         + [dma((width // columns,))]
         + [dma((size,))] * 2
-        + [dma((bits,))] * 2,
+        + [dma((bits,))] * 2
+        + [dma((chunks,))] * 2
+        + [dma((3,))],
         compiler_params=pltpu.CompilerParams(
             collective_id=1, has_side_effects=True, vmem_limit_bytes=63 << 20
         ),
@@ -1433,6 +1651,7 @@
         grad_residual,
         residual,
         gain[None, :],
+        early,
         *views,
         small,
     )
@@ -1496,7 +1715,7 @@
         chunk_count,
     )
     grad_mixed = grad_mixed.reshape(streams, seg_len, local)
-    grad_unit, gq, gk, gv, small = attend_back(
+    grad_unit, gq, gk, gv, small, early = attend_back(
         unit,
         q,
         k,
@@ -1513,6 +1732,10 @@
         grad_second,
         mem_len,
         packed_len,
+        branch,
+        residual,
+        mp_size,
+        early_chunks,
     )
     result, grad_seg, grad_out_w, grad_up, grad_down, gq, gk, gv, grad_pack, small = close(
         grad_unit,
@@ -1521,6 +1744,7 @@
         grad_residual,
         residual,
         first_gain,
+        early,
         (grad_out_full, grad_up, grad_down, gq, gk, gv, grad_pack),
         small,
         mp_size,

time: 460 us -> 440 us (0.957)
  Pallas kernels: 436 us -> 415 us
    pallas_call x1, Pallas kernels: 237 us -> 214 us  [close(): pl.pallas_call(functools.partial(close_kernel, size, group, chunks, 2, co...]
    pallas_call x1, Pallas kernels: 24.2 us -> 36.1 us  [attend_back(): pl.pallas_call(functools.partial(attend_back_kernel, sizes, size, early,...]
    pallas_call x1, Pallas kernels: 144 us -> 134 us  [feed(): pl.pallas_call(functools.partial(feed_kernel, size, group, chunks, 2, 0,...]
where the time goes in v4:
time: 440 us; the launch traced here: 439 us
  Pallas kernels  415 us (94%)
  local copies, waits for them, and re-layouts  22.8 us (5%)
    pallas_call x1, Pallas kernels, close(): pl.pallas_call(functools.partial(close_kernel, size, group, chunks, 2, co...  214 us
    pallas_call x1, Pallas kernels, feed(): pl.pallas_call(functools.partial(feed_kernel, size, group, chunks, 2, 0,...  134 us
    pallas_call x1, Pallas kernels, attend_back(): pl.pallas_call(functools.partial(attend_back_kernel, sizes, size, early,...  36.1 us
    pallas_call x1, Pallas kernels, attend(): pl.pallas_call(functools.partial(attend_kernel, sizes, size, group), grid...  30.5 us
    unnamed x26, local copies, waits for them, and re-layouts  19.9 us

profile of v4, /device:TPU:0, one launch (start us, length us, event | category | flops | bytes accessed | tf_op | source)
XLA Modules:
  0.0 438.6 jit_solution(11318235338671263868)
XLA Ops:
  0.6 30.5 %attend.1 = (bf16[2,1536,1024]{2,1,0:T(8,128)(2,1)}, bf16[2,512,256]{2,1,0:T(8,128)(2,1)}, bf16[2,1536,256]{2,1,0:T(8,128)(2,1)}, bf16[2,1536,256]{2,1,0:T(8,128...) custom-call(s32[2]{0:T(128)} %memory_fill.3, ...), custom_call_target="tpu_custom_call" | custom-call | flops 6442450944 | bytes 17301504 | tf_op jit(solution)/shard_map/attend/pallas_call | solution.py:291
  31.2 134.0 %feed.1 = (bf16[32,32,256]{2,1,0:T(8,128)(2,1)}, f32[8,32,1024]{2,1,0:T(8,128)}, f32[8,32,1024]{2,1,0:T(8,128)}, f32[32,32,1024]{2,1,0:T(8,128)}, f32[1024,1024]...) custom-call(bf16[8,128,256]{2,1,0:T(8,128)(2,1)} %bitcast.46, ...), custom_call_target="tpu_custom_call" | custom-call | tf_op jit(solution)/shard_map/feed/pallas_call | solution.py:1052
  165.2 36.1 %attend_back.1 = (f32[2,512,1024]{2,1,0:T(8,128)}, f32[256,1024]{1,0:T(8,128)}, f32[256,1024]{1,0:T(8,128)}, f32[256,1024]{1,0:T(8,128)}, f32[8,1024]{1,0:T(8,128)}, /*index=5*/f32[2,32,1024]{2,1,0:T(8,128)}) custom-call(s32[2]{0:T(128)} %memory_fill.3, s32[2]{0:T(128)} %packed_fill.3, f32[2,22]{1,0:T(2,128)} %bias_ref.3, ...), custom_call_target="tpu_custom_call" | custom-call | flops 10468982784 | bytes 11010048 | tf_op jit(solution)/shard_map/attend_back/pallas_call | solution.py:689
  201.3 214.5 %close.1 = (bf16[32,32,1024]{2,1,0:T(8,128)(2,1)}, bf16[32,32,1024]{2,1,0:T(8,128)(2,1)}, f32[1,256,1024]{2,1,0:T(8,128)}, f32[4,256,1024]{2,1,0:T(8,128)}, f32[...) custom-call(f32[32,32,1024]{2,1,0:T(8,128)} %bitcast.57, ...), custom_call_target="tpu_custom_call" | custom-call | flops 99999997952 | bytes 1000000000 | tf_op jit(solution)/shard_map/close/pallas_call | solution.py:1608
  415.8 0.0 copy-start.6
  415.8 0.8 slice_reduce_fusion
  416.6 1.4 fusion
  418.0 0.6 reshape_squeeze.3
  418.6 0.0 copy-start.5
  418.6 2.6 copy.30
  421.3 0.0 copy-done.6
  421.3 1.3 copy.31
  422.6 0.0 copy-done.5
  422.6 1.3 copy.32
  423.9 0.0 copy-start.3
  423.9 3.0 copy.33
  426.9 0.0 copy-done.3
  426.9 0.0 copy-start.7
  426.9 0.0 copy-start.2
  426.9 1.3 copy.40
  428.2 0.0 copy-done.7
  428.2 0.0 copy-start.4
  428.2 0.7 copy.41
  428.9 0.5 copy-done.2
  429.4 0.0 copy-start.1
  429.4 1.3 copy.42
  430.8 0.0 copy-done.4
  430.8 1.0 copy.43
  431.7 1.1 copy-done.1
  432.9 0.0 copy-start
  432.9 2.1 copy.44
  435.0 1.6 copy-done
  436.6 2.0 copy.45
Async XLA Ops:
  415.8 5.5 %copy-start.6 = (f32[1,256,1024]{2,1,0:T(8,128)S(1)}, f32[1,256,1024]{2,1,0:T(8,128)}, u32[]{:S(2)}) copy-start(f32[1,256,1024]{2,1,0:T(8,128)} %get-tuple-element.73) | copy-start | bytes 3145732
  418.6 3.9 copy-start.5
  423.9 3.0 copy-start.3
  426.9 1.3 copy-start.7
  426.9 2.5 copy-start.2
  428.2 2.5 copy-start.4
  429.4 3.4 copy-start.1
  432.9 3.7 copy-start

commit v5 on v4

--- a/solution.py
+++ b/solution.py
@@ -542,6 +542,8 @@
     )
     ticks = line.reach * (early - 1) + hop * line.reach + 1
     spans = heads * (seg_len // query_block)
+    starts = [22 * index for index in range(spans + 1)]
+    starts += [starts[-1] + 6, starts[-1] + 17, starts[-1] + 28, starts[-1] + 36]
 
     def line_step(tick, _):
         line.scatter_step(tick, branch_ref, lanes_out)
@@ -555,9 +557,9 @@
         return 0
 
     def line_span(index):
-        unit = stream * spans + index
-        every = spans * pl.num_programs(0)
-        lax.fori_loop((unit * ticks) // every, ((unit + 1) * ticks) // every, line_step, 0)
+        every = starts[-1] * pl.num_programs(0)
+        here, after = stream * starts[-1] + starts[index], stream * starts[-1] + starts[index + 1]
+        lax.fori_loop((here * ticks) // every, (after * ticks) // every, line_step, 0)
 
     @pl.when(stream == 0)
     def _():
@@ -623,9 +625,13 @@
                 ].astype(f32)
         dk_low[:, lanes] = (dk_sum[...] * scale).astype(bf16)
         dv_low[:, lanes] = dv_sum[...].astype(bf16)
+    line_span(spans)
     gq_ref[...] += mm_t0(dq_low[...], unit_ref[0, kept:, :])
+    line_span(spans + 1)
     gk_ref[...] += mm_t0(dk_low[...], unit_ref[0])
+    line_span(spans + 2)
     gv_ref[...] += mm_t0(dv_low[...], unit_ref[0])
+    line_span(spans + 3)
     gunit_ref[0] = (
         mm_t1(dq_low[...], wq_ref[...])
         + mm_t1(dk_low[kept:, :], wk_ref[...])
@@ -639,7 +645,7 @@
         cols = lax.broadcasted_iota(jnp.int32, (block, block), 1)
         width = gain_ref.shape[1]
         lane = lax.broadcasted_iota(jnp.int32, (1, width), 1)
-        relative = jnp.zeros((1, width), f32)
+        relative = [jnp.zeros((1, width), f32) for _ in range(heads)]
         for head in range(heads):
             blocks = []
             for column in range(diagonal_count(seg_len, kept)):
@@ -657,13 +663,13 @@
                             jnp.where(distance >= mark_value, value, 0.0), axis=0, keepdims=True
                         )
                 total = jnp.sum(total, axis=1, keepdims=True)
-                relative = jnp.where(lane == head * len(reach_marks) + position, total, relative)
+                relative[head] = jnp.where(lane == position, total, relative[head])
         first = jnp.zeros((1, width), f32)
         for grad_ref, weight_ref in ((gq_ref, wq_ref), (gk_ref, wk_ref), (gv_ref, wv_ref)):
             turned = weight_ref[...].astype(f32).T
             first = first + jnp.sum(grad_ref[...] * turned, axis=0, keepdims=True)
         small_ref[...] = jnp.concatenate(
-            [first / gain_ref[...], gsecond_ref[...], relative, jnp.zeros((5, width), f32)], axis=0
+            [first / gain_ref[...], gsecond_ref[...], *relative, jnp.zeros((6 - heads, width), f32)], axis=0
         )
 
 
@@ -687,7 +693,7 @@
         return pl.BlockSpec(shape, lambda s: (0,) * len(shape))
 
     return pl.pallas_call(
-        functools.partial(attend_back_kernel, sizes, size, early, 2),
+        functools.partial(attend_back_kernel, sizes, size, early, 3),
         grid=(streams,),
         in_specs=[
             smem,
@@ -1115,6 +1121,7 @@
         self.slots = work.shape[0]
         (self.rs_s, self.rs_r, self.ag_s, self.ag_r, self.load_sem, self.store_sem) = sems
         self.count = crossing[0] + sum(job[2] for job in jobs)
+        self.turned = self.count - sum(job[2] for job in jobs if job[1].shape != job[0].shape)
         self.beats = self.count + 2 * self.bits * gap + 2
 
     def step_of(self, odd, level):
@@ -1193,7 +1200,9 @@
                 index = (piece - low) // across
                 lanes = pl.ds(pl.multiple_of((piece - low - index * across) * columns, columns), columns)
                 inside = self.summed.at[slot] if store else self.work.at[slot]
-                if store:
+                if store and target.shape != source.shape:
+                    copy = pltpu.make_async_copy(inside, target.at[piece - low], self.store_sem.at[slot])
+                elif store:
                     copy = pltpu.make_async_copy(inside, target.at[index, :, lanes], self.store_sem.at[slot])
                 else:
                     copy = pltpu.make_async_copy(source.at[index, :, lanes], inside, self.load_sem.at[slot])
@@ -1219,8 +1228,6 @@
 
                 @pl.when(inside & plain)
                 def _():
-                    for level in range(bits):
-                        self.spread(slot, odd, level, False).wait_send()
                     self.move(piece, slot, True, False)
 
                 @pl.when(inside & jnp.logical_not(plain))
@@ -1232,6 +1239,13 @@
                 @pl.when(inside & plain)
                 def _():
                     self.spread(slot, odd, 0, True).wait_recv()
+                    for level in range(bits):
+                        self.spread(slot, odd, level, False).wait_send()
+
+                    @pl.when(piece >= self.turned)
+                    def _():
+                        self.summed[slot] = self.summed[slot].T
+
                     self.move(piece, slot, True, True)
 
             elif age > bits:
@@ -1605,6 +1619,9 @@
     dma = pltpu.SemaphoreType.DMA
     sums = [jax.ShapeDtypeStruct(view.shape, f32) for view in views]
     sums[0] = jax.ShapeDtypeStruct((1, piece_rows, width), f32)
+    for index in range(3, len(views)):
+        turned_shape = (views[index].shape[2] // columns, columns, piece_rows)
+        sums[index] = jax.ShapeDtypeStruct(turned_shape, f32)
     return pl.pallas_call(
         functools.partial(close_kernel, size, group, chunks, 2, counts, gap, early.shape[0]),
         in_specs=[anywhere] * 5 + [vmem] * 2 + [anywhere] * len(views) + [vmem],
@@ -1752,14 +1769,12 @@
         chunk_count,
     )
     grad_first, grad_second = small[0], small[1]
-    grad_relative = small[2, : relative_bias.size].reshape(relative_bias.shape)
+    grad_relative = small[2 : 2 + relative_bias.shape[0], : relative_bias.shape[1]]
     result = result.reshape(inputs.shape)
     grad_seg = grad_seg.reshape(inputs.shape)
-    grad_query_w = gq.reshape(local, width).T
-    grad_key_w = gk.reshape(local, width).T
-    grad_value_w = gv.reshape(local, width).T
+    grad_query_w, grad_key_w, grad_value_w = (grad.reshape(width, local) for grad in (gq, gk, gv))
     grad_out_w = grad_out_w.reshape(local, width)
-    grad_compress_w = grad_pack.reshape(-1, 2 * width).T
+    grad_compress_w = grad_pack.reshape(2 * width, local)
     grad_up = grad_up.reshape(up_weight.shape)
     grad_down = grad_down.reshape(down_weight.shape)
     return (

time: 440 us -> 435 us (0.989)
    unnamed x26 -> x28, local copies, waits for them, and re-layouts: 19.9 us -> 18.2 us
where the time goes in v5:
time: 435 us; the launch traced here: 434 us
  Pallas kernels  412 us (95%)
  local copies, waits for them, and re-layouts  20.9 us (5%)
    pallas_call x1, Pallas kernels, close(): pl.pallas_call(functools.partial(close_kernel, size, group, chunks, 2, co...  214 us
    pallas_call x1, Pallas kernels, feed(): pl.pallas_call(functools.partial(feed_kernel, size, group, chunks, 2, 0,...  134 us
    pallas_call x1, Pallas kernels, attend_back(): pl.pallas_call(functools.partial(attend_back_kernel, sizes, size, early,...  33.4 us
    pallas_call x1, Pallas kernels, attend(): pl.pallas_call(functools.partial(attend_kernel, sizes, size, group), grid...  30.5 us
    unnamed x28, local copies, waits for them, and re-layouts  18.2 us

profile of v5, /device:TPU:0, one launch (start us, length us, event | category | flops | bytes accessed | tf_op | source)
XLA Modules:
  0.0 434.0 jit_solution(5038170286263781753)
XLA Ops:
  0.6 30.5 %attend.1 = (bf16[2,1536,1024]{2,1,0:T(8,128)(2,1)}, bf16[2,512,256]{2,1,0:T(8,128)(2,1)}, bf16[2,1536,256]{2,1,0:T(8,128)(2,1)}, bf16[2,1536,256]{2,1,0:T(8,128...) custom-call(s32[2]{0:T(128)} %memory_fill.3, ...), custom_call_target="tpu_custom_call" | custom-call | flops 6442450944 | bytes 17301504 | tf_op jit(solution)/shard_map/attend/pallas_call | solution.py:291
  31.2 134.0 %feed.1 = (bf16[32,32,256]{2,1,0:T(8,128)(2,1)}, f32[8,32,1024]{2,1,0:T(8,128)}, f32[8,32,1024]{2,1,0:T(8,128)}, f32[32,32,1024]{2,1,0:T(8,128)}, f32[1024,1024]...) custom-call(bf16[8,128,256]{2,1,0:T(8,128)(2,1)} %bitcast.38, ...), custom_call_target="tpu_custom_call" | custom-call | tf_op jit(solution)/shard_map/feed/pallas_call | solution.py:1058
  165.2 33.4 %attend_back.1 = (f32[2,512,1024]{2,1,0:T(8,128)}, f32[256,1024]{1,0:T(8,128)}, f32[256,1024]{1,0:T(8,128)}, f32[256,1024]{1,0:T(8,128)}, f32[8,1024]{1,0:T(8,128)}, /*index=5*/f32[2,32,1024]{2,1,0:T(8,128)}) custom-call(s32[2]{0:T(128)} %memory_fill.3, s32[2]{0:T(128)} %packed_fill.3, f32[2,22]{1,0:T(2,128)} %bias_ref.3, ...), custom_call_target="tpu_custom_call" | custom-call | flops 10468982784 | bytes 11010048 | tf_op jit(solution)/shard_map/attend_back/pallas_call | solution.py:695
  198.6 214.5 %close.1 = (bf16[32,32,1024]{2,1,0:T(8,128)(2,1)}, bf16[32,32,1024]{2,1,0:T(8,128)(2,1)}, f32[1,256,1024]{2,1,0:T(8,128)}, f32[4,256,1024]{2,1,0:T(8,128)}, f32[...) custom-call(f32[32,32,1024]{2,1,0:T(8,128)} %bitcast.49, ...), custom_call_target="tpu_custom_call" | custom-call | flops 99999997952 | bytes 1000000000 | tf_op jit(solution)/shard_map/close/pallas_call | solution.py:1625
  413.1 1.2 slice.10
  414.4 1.4 fusion
  415.8 0.0 copy-start.8
  415.8 0.0 copy-start.3
  415.8 3.2 copy.40
  419.0 0.0 copy-done.8
  419.0 0.7 copy.41
  419.7 0.0 copy-done.3
  419.7 0.0 copy-start.7
  419.7 0.0 copy-start.6
  419.7 1.3 copy.42
  421.1 0.6 copy-done.7
  421.7 0.0 copy-start.5
  421.7 0.0 copy-start.4
  421.7 1.0 copy.43
  422.7 0.0 copy-done.6
  422.7 0.0 copy-start.1
  422.7 1.0 copy.44
  423.7 0.0 copy-done.5
  423.7 1.0 copy.45
  424.6 0.0 copy-done.4
  424.6 1.0 copy.46
  425.6 0.3 copy-done.1
  425.9 0.0 copy-start
  425.9 2.1 copy.47
  428.0 1.6 copy-done
  429.6 0.0 copy-start.2
  429.6 2.1 copy.48
  431.7 1.0 copy-done.2
  432.7 1.3 copy.49
Async XLA Ops:
  415.8 3.2 copy-start.8
  415.8 3.9 copy-start.3
  419.7 2.0 copy-start.7
  419.7 2.9 copy-start.6
  421.7 2.0 copy-start.5
  421.7 2.9 copy-start.4
  422.7 3.2 copy-start.1
  425.9 3.7 copy-start
  429.6 3.1 copy-start.2

commit v6 on v5

--- a/solution.py
+++ b/solution.py
@@ -72,11 +72,19 @@
     return jnp.where(dead_packed | dead_memory, masked_score, 0.0).astype(f32)
 
 
-def greet(peers):
+def call(peers):
     barrier = pltpu.get_barrier_semaphore()
     for peer in peers:
         pl.semaphore_signal(barrier, inc=1, device_id=peer, device_id_type=pl.DeviceIdType.MESH)
-    pl.semaphore_wait(barrier, len(peers))
+
+
+def hear(peers):
+    pl.semaphore_wait(pltpu.get_barrier_semaphore(), len(peers))
+
+
+def greet(peers):
+    call(peers)
+    hear(peers)
 
 
 class Spread:
@@ -182,18 +190,13 @@
     piece, columns = spread_in.shape[3:]
     width = gain.shape[1]
 
+    first_peers = [spread.others(offset) for offset in range(1, size)] + [
+        spread.partner(half, 0) for half in range(2)
+    ]
+
     @pl.when(stream == 0)
     def _():
-        greet(
-            [spread.others(offset) for offset in range(1, size)]
-            + [spread.partner(half, 0) for half in range(2)]
-        )
-        rows = pl.ds(pl.multiple_of(spread.mine * piece, piece), piece)
-        for half in range(2):
-            lanes = slice(half * columns, (half + 1) * columns)
-            spread_in[half, spread.spots[half], spread.me] = wo_ref[rows, lanes].astype(f32)
-            for offset in range(1, size):
-                spread.across(half, offset, False).start()
+        call(first_peers)
         gpack_ref[...] = jnp.zeros_like(gpack_ref)
 
     slot = lax.broadcasted_iota(jnp.int32, mem_rows.shape[1:], 0)
@@ -211,6 +214,17 @@
         packed_new = packed_new + mm(rows, wc_ref[lanes, :])
         gpack_ref[:, lanes] += mm_t0(gcomp_ref[0], rows)
     packed_new_ref[0] = packed_new.astype(bf16)
+
+    @pl.when(stream == 0)
+    def _():
+        hear(first_peers)
+        rows = pl.ds(pl.multiple_of(spread.mine * piece, piece), piece)
+        for half in range(2):
+            lanes = slice(half * columns, (half + 1) * columns)
+            spread_in[half, spread.spots[half], spread.me] = wo_ref[rows, lanes].astype(f32)
+            for offset in range(1, size):
+                spread.across(half, offset, False).start()
+
     start = 0
     for part_ref, length in ((packed_ref, packed_len), (memory_ref, mem_len), (seg_ref, seg_len)):
         rows = part_ref[0].astype(f32)
@@ -462,7 +476,7 @@
                     self.sent(whole, sems[0], (place + 1) * self.chunks, right).wait_send()
 
 
-def meet(line):
+def call_neighbours(line):
     barrier = pltpu.get_barrier_semaphore()
     for right in (True, False):
 
@@ -472,6 +486,9 @@
                 barrier, inc=1, device_id=line.peer(right), device_id_type=pl.DeviceIdType.MESH
             )
 
+
+def hear_neighbours(line):
+    barrier = pltpu.get_barrier_semaphore()
     inner = (line.me > 0) & (line.me < line.reach)
 
     @pl.when(inner)
@@ -557,17 +574,28 @@
         return 0
 
     def line_span(index):
-        every = starts[-1] * pl.num_programs(0)
-        here, after = stream * starts[-1] + starts[index], stream * starts[-1] + starts[index + 1]
+        if index == 0:
+            return
+        late = starts[1]
+        begin = starts[index] if index > 1 else 0
+        every = starts[-1] * pl.num_programs(0) - late
+        here = jnp.maximum(stream * starts[-1] + begin - late, 0)
+        after = jnp.maximum(stream * starts[-1] + starts[index + 1] - late, 0)
+        if index == 1:
+
+            @pl.when(stream == 0)
+            def _():
+                hear_neighbours(line)
+                for load in loads:
+                    load.wait()
+
         lax.fori_loop((here * ticks) // every, (after * ticks) // every, line_step, 0)
 
     @pl.when(stream == 0)
     def _():
         for load in loads:
             load.start()
-        meet(line)
-        for load in loads:
-            load.wait()
+        call_neighbours(line)
         strip_sum[...] = jnp.zeros_like(strip_sum)
         gq_ref[...] = jnp.zeros_like(gq_ref)
         gk_ref[...] = jnp.zeros_like(gk_ref)

time: 435 us -> 434 us (level)
  no operation moved by 1% of the time
where the time goes in v6:
time: 434 us; the launch traced here: 433 us
  Pallas kernels  411 us (95%)
  local copies, waits for them, and re-layouts  20.9 us (5%)
    pallas_call x1, Pallas kernels, close(): pl.pallas_call(functools.partial(close_kernel, size, group, chunks, 2, co...  214 us
    pallas_call x1, Pallas kernels, feed(): pl.pallas_call(functools.partial(feed_kernel, size, group, chunks, 2, 0,...  132 us
    pallas_call x1, Pallas kernels, attend_back(): pl.pallas_call(functools.partial(attend_back_kernel, sizes, size, early,...  33.9 us
    pallas_call x1, Pallas kernels, attend(): pl.pallas_call(functools.partial(attend_kernel, sizes, size, group), grid...  30.9 us
    unnamed x28, local copies, waits for them, and re-layouts  18.2 us

profile of v6, /device:TPU:0, one launch (start us, length us, event | category | flops | bytes accessed | tf_op | source)
XLA Modules:
  0.0 432.8 jit_solution(2225247039626279280)
XLA Ops:
  0.6 30.9 %attend.1 = (bf16[2,1536,1024]{2,1,0:T(8,128)(2,1)}, bf16[2,512,256]{2,1,0:T(8,128)(2,1)}, bf16[2,1536,256]{2,1,0:T(8,128)(2,1)}, bf16[2,1536,256]{2,1,0:T(8,128...) custom-call(s32[2]{0:T(128)} %memory_fill.3, ...), custom_call_target="tpu_custom_call" | custom-call | flops 6442450944 | bytes 17301504 | tf_op jit(solution)/shard_map/attend/pallas_call | solution.py:305
  31.6 131.9 %feed.1 = (bf16[32,32,256]{2,1,0:T(8,128)(2,1)}, f32[8,32,1024]{2,1,0:T(8,128)}, f32[8,32,1024]{2,1,0:T(8,128)}, f32[32,32,1024]{2,1,0:T(8,128)}, f32[1024,1024]...) custom-call(bf16[8,128,256]{2,1,0:T(8,128)(2,1)} %bitcast.38, ...), custom_call_target="tpu_custom_call" | custom-call | tf_op jit(solution)/shard_map/feed/pallas_call | solution.py:1086
  163.5 33.9 %attend_back.1 = (f32[2,512,1024]{2,1,0:T(8,128)}, f32[256,1024]{1,0:T(8,128)}, f32[256,1024]{1,0:T(8,128)}, f32[256,1024]{1,0:T(8,128)}, f32[8,1024]{1,0:T(8,128)}, /*index=5*/f32[2,32,1024]{2,1,0:T(8,128)}) custom-call(s32[2]{0:T(128)} %memory_fill.3, s32[2]{0:T(128)} %packed_fill.3, f32[2,22]{1,0:T(2,128)} %bias_ref.3, ...), custom_call_target="tpu_custom_call" | custom-call | flops 10468982784 | bytes 11010048 | tf_op jit(solution)/shard_map/attend_back/pallas_call | solution.py:723
  197.4 214.5 %close.1 = (bf16[32,32,1024]{2,1,0:T(8,128)(2,1)}, bf16[32,32,1024]{2,1,0:T(8,128)(2,1)}, f32[1,256,1024]{2,1,0:T(8,128)}, f32[4,256,1024]{2,1,0:T(8,128)}, f32[...) custom-call(f32[32,32,1024]{2,1,0:T(8,128)} %bitcast.49, ...), custom_call_target="tpu_custom_call" | custom-call | flops 99999997952 | bytes 1000000000 | tf_op jit(solution)/shard_map/close/pallas_call | solution.py:1653
  411.9 1.2 slice.10
  413.2 1.4 fusion
  414.6 0.0 copy-start.8
  414.6 0.0 copy-start.3
  414.6 3.2 copy.40
  417.9 0.0 copy-done.8
  417.9 0.7 copy.41
  418.6 0.0 copy-done.3
  418.6 0.0 copy-start.7
  418.6 0.0 copy-start.6
  418.6 1.3 copy.42
  419.9 0.6 copy-done.7
  420.5 0.0 copy-start.5
  420.5 0.0 copy-start.4
  420.5 1.0 copy.43
  421.5 0.0 copy-done.6
  421.5 0.0 copy-start.1
  421.5 1.0 copy.44
  422.5 0.0 copy-done.5
  422.5 1.0 copy.45
  423.4 0.0 copy-done.4
  423.5 1.0 copy.46
  424.4 0.3 copy-done.1
  424.7 0.0 copy-start
  424.7 2.1 copy.47
  426.8 1.6 copy-done
  428.4 0.0 copy-start.2
  428.4 2.1 copy.48
  430.5 1.0 copy-done.2
  431.5 1.3 copy.49
Async XLA Ops:
  414.6 3.2 copy-start.8
  414.6 3.9 copy-start.3
  418.6 2.0 copy-start.7
  418.6 2.9 copy-start.6
  420.5 2.0 copy-start.5
  420.5 2.9 copy-start.4
  421.5 3.2 copy-start.1
  424.7 3.7 copy-start
  428.4 3.1 copy-start.2

commit v7 on v6

--- a/solution.py
+++ b/solution.py
@@ -1352,7 +1352,9 @@
     gk_sum,
     gv_sum,
     gpack_sum,
-    small_sum,
+    first_out,
+    second_out,
+    relative_out,
     gunit_ref,
     branch_ref,
     seg_ref,
@@ -1529,7 +1531,9 @@
                     small_held[level + 1] = value
                     small_within(level + 1).start()
                 else:
-                    small_sum[...] = value
+                    first_out[...] = value[0:1]
+                    second_out[...] = value[1:2]
+                    relative_out[...] = value[2 : 2 + relative_out.shape[0], : relative_out.shape[1]]
 
     def settle_seg(chunk):
         slot = chunk * size + me
@@ -1632,7 +1636,7 @@
 
 
 def close(
-    grad_unit, branch, seg_rows, grad_residual, residual, gain, early, grads, small, size, group, chunks
+    grad_unit, branch, seg_rows, grad_residual, residual, gain, early, grads, small, relative_shape, size, group, chunks
 ):
     rows, width = seg_rows.shape
     piece = rows // (chunks * size)
@@ -1653,8 +1657,9 @@
     return pl.pallas_call(
         functools.partial(close_kernel, size, group, chunks, 2, counts, gap, early.shape[0]),
         in_specs=[anywhere] * 5 + [vmem] * 2 + [anywhere] * len(views) + [vmem],
-        out_specs=[vmem] * 2 + [anywhere] * len(views) + [vmem],
-        out_shape=[jax.ShapeDtypeStruct(whole, bf16)] * 2 + sums + [jax.ShapeDtypeStruct(small.shape, f32)],
+        out_specs=[vmem] * 2 + [anywhere] * len(views) + [vmem] * 3,
+        out_shape=[jax.ShapeDtypeStruct(whole, bf16)] * 2 + sums
+        + [jax.ShapeDtypeStruct(shape, f32) for shape in ((1, width), (1, width), relative_shape)],
         scratch_shapes=[pltpu.VMEM(whole, f32)] * 2
         + [
             pltpu.VMEM(whole, bf16),
@@ -1782,7 +1787,7 @@
         mp_size,
         early_chunks,
     )
-    result, grad_seg, grad_out_w, grad_up, grad_down, gq, gk, gv, grad_pack, small = close(
+    result, grad_seg, grad_out_w, grad_up, grad_down, gq, gk, gv, grad_pack, grad_first, grad_second, grad_relative = close(
         grad_unit,
         branch,
         seg_rows,
@@ -1792,12 +1797,12 @@
         early,
         (grad_out_full, grad_up, grad_down, gq, gk, gv, grad_pack),
         small,
+        relative_bias.shape,
         mp_size,
         dp_size,
         chunk_count,
     )
-    grad_first, grad_second = small[0], small[1]
-    grad_relative = small[2 : 2 + relative_bias.shape[0], : relative_bias.shape[1]]
+    grad_first, grad_second = grad_first[0], grad_second[0]
     result = result.reshape(inputs.shape)
     grad_seg = grad_seg.reshape(inputs.shape)
     grad_query_w, grad_key_w, grad_value_w = (grad.reshape(width, local) for grad in (gq, gk, gv))

time: 434 us -> 433 us (level)
    unnamed x28 -> x37, local copies, waits for them, and re-layouts: 18.2 us -> 19.1 us
where the time goes in v7:
time: 433 us; the launch traced here: 431 us
  Pallas kernels  411 us (95%)
  local copies, waits for them, and re-layouts  19.1 us (4%)
    pallas_call x1, Pallas kernels, close(): pl.pallas_call(functools.partial(close_kernel, size, group, chunks, 2, co...  214 us
    pallas_call x1, Pallas kernels, feed(): pl.pallas_call(functools.partial(feed_kernel, size, group, chunks, 2, 0,...  132 us
    pallas_call x1, Pallas kernels, attend_back(): pl.pallas_call(functools.partial(attend_back_kernel, sizes, size, early,...  34.1 us
    pallas_call x1, Pallas kernels, attend(): pl.pallas_call(functools.partial(attend_kernel, sizes, size, group), grid...  30.9 us
    unnamed x37, local copies, waits for them, and re-layouts  19.1 us

profile of v7, /device:TPU:0, one launch (start us, length us, event | category | flops | bytes accessed | tf_op | source)
XLA Modules:
  0.0 431.3 jit_solution(5198036396169564159)
XLA Ops:
  0.6 30.9 %attend.1 = (bf16[2,1536,1024]{2,1,0:T(8,128)(2,1)}, bf16[2,512,256]{2,1,0:T(8,128)(2,1)}, bf16[2,1536,256]{2,1,0:T(8,128)(2,1)}, bf16[2,1536,256]{2,1,0:T(8,128...) custom-call(s32[2]{0:T(128)} %memory_fill.3, ...), custom_call_target="tpu_custom_call" | custom-call | flops 6442450944 | bytes 17301504 | tf_op jit(solution)/shard_map/attend/pallas_call | solution.py:305
  31.6 131.9 %feed.1 = (bf16[32,32,256]{2,1,0:T(8,128)(2,1)}, f32[8,32,1024]{2,1,0:T(8,128)}, f32[8,32,1024]{2,1,0:T(8,128)}, f32[32,32,1024]{2,1,0:T(8,128)}, f32[1024,1024]...) custom-call(bf16[8,128,256]{2,1,0:T(8,128)(2,1)} %bitcast.38, ...), custom_call_target="tpu_custom_call" | custom-call | tf_op jit(solution)/shard_map/feed/pallas_call | solution.py:1086
  163.5 34.1 %attend_back.1 = (f32[2,512,1024]{2,1,0:T(8,128)}, f32[256,1024]{1,0:T(8,128)}, f32[256,1024]{1,0:T(8,128)}, f32[256,1024]{1,0:T(8,128)}, f32[8,1024]{1,0:T(8,128)}, /*index=5*/f32[2,32,1024]{2,1,0:T(8,128)}) custom-call(s32[2]{0:T(128)} %memory_fill.3, s32[2]{0:T(128)} %packed_fill.3, f32[2,22]{1,0:T(2,128)} %bias_ref.3, ...), custom_call_target="tpu_custom_call" | custom-call | flops 10468982784 | bytes 11010048 | tf_op jit(solution)/shard_map/attend_back/pallas_call | solution.py:723
  197.6 214.5 %close.1 = (bf16[32,32,1024]{2,1,0:T(8,128)(2,1)}, bf16[32,32,1024]{2,1,0:T(8,128)(2,1)}, f32[1,256,1024]{2,1,0:T(8,128)}, f32[4,256,1024]{2,1,0:T(8,128)}, f32[...) custom-call(f32[32,32,1024]{2,1,0:T(8,128)} %bitcast.49, ...), custom_call_target="tpu_custom_call" | custom-call | flops 99999997952 | bytes 1000000000 | tf_op jit(solution)/shard_map/close/pallas_call | solution.py:1657
  412.1 0.0 copy-start.8
  412.1 0.0 copy-start.3
  412.2 3.2 copy.43
  415.4 0.0 copy-done.8
  415.4 0.7 copy.44
  416.1 0.0 copy-done.3
  416.1 0.0 copy-start.10
  416.1 0.0 copy-start.7
  416.1 1.3 copy.45
  417.4 0.0 copy-done.10
  417.4 0.0 copy-start.6
  417.4 0.6 copy.46
  418.0 0.0 copy-done.7
  418.1 0.0 copy-start.5
  418.1 1.0 copy.47
  419.0 0.0 copy-done.6
  419.0 0.0 copy-start.11
  419.0 0.0 copy-start.4
  419.0 0.0 copy-start.9
  419.0 1.0 copy.48
  420.0 0.0 copy-done.5
  420.0 0.0 copy-start.1
  420.0 1.0 copy.49
  421.0 0.0 copy-done.11
  421.0 0.6 copy.50
  421.6 0.0 copy-done.4
  421.6 1.0 copy.51
  422.5 0.0 copy-done.9
  422.5 0.6 copy.52
  423.1 0.0 copy-done.1
  423.1 0.0 copy-start
  423.1 2.1 copy.53
  425.3 1.6 copy-done
  426.8 0.0 copy-start.2
  426.8 2.1 copy.54
  429.0 1.0 copy-done.2
  429.9 1.3 copy.55
Async XLA Ops:
  412.1 3.3 copy-start.8
  412.1 3.9 copy-start.3
  416.1 1.3 copy-start.10
  416.1 2.0 copy-start.7
  417.4 1.6 copy-start.6
  418.1 2.0 copy-start.5
  419.0 2.0 copy-start.11
  419.0 2.5 copy-start.4
  419.0 3.5 copy-start.9
  420.0 3.1 copy-start.1
  423.1 3.7 copy-start
  426.8 3.1 copy-start.2
